TPU v7x, 1024 devices: a whole 4x4x32 slice. The times are simulated.
1024 devices in a mesh: ctx: 256 (over z, x, core), head: 4 (over y).
Axes of the slice: x: 4, y: 4, z: 32, core: 2. Of those that a mesh axis runs over, the one named last changes fastest.
Arguments:
- query: bfloat16 [32768, 4096], P('ctx', 'head')
- key: bfloat16 [32768, 512], P(('ctx', 'head'))
- value: bfloat16 [32768, 512], P(('ctx', 'head')), may hold values from -6 to 6
- dout: bfloat16 [32768, 4096], P('ctx', 'head'), may hold values from -6 to 6
- doc_ids: int32 [32768], replicated, may hold values from 0 to 31, never falling along the last dimension, each value on 1 to 2048 neighbouring positions
- pair_flags: int32 [256, 8], P('ctx'), may hold values from 0 to 1, as said below
Outputs:
- dquery: bfloat16 [32768, 4096], P('ctx', 'head')
- dkey: bfloat16 [32768, 512], P(('ctx', 'head'))
- dvalue: bfloat16 [32768, 512], P(('ctx', 'head'))
Inputs may be any that keep to these rules, and one draw needn't show every extreme that they name: `pair_flags`: column 0 is always 1; entries [b, d] with b - d < 0 are 0; for b < 8 every entry with b - d >= 0 is 1. `doc_ids`: ids never fall along the tokens.
All inputs are finite; a program needn't handle non-finite values.
Results may differ from a plain program's by a relative error of at most 0.0063.
Values may be sent and summed in bfloat16 or wider, within the bound.
No kernel may reach another device: no remote copies, remote signals or barrier semaphores. Data moves between devices by JAX's collectives and lax.ppermute only.
A program may use at most 32 MiB of HBM per device.

v0:
```python
import math

import jax
import jax.numpy as jnp
from jax import lax
from jax.sharding import PartitionSpec as P

HD = 128
QPK = 8


def passed_along(array, axis, by):
    length = lax.axis_size(axis)
    pairs = [(i, i + by) for i in range(length) if 0 <= i + by < length]
    return lax.ppermute(array, axis, pairs)


def shifted(array, axis, by):
    length = lax.axis_size(axis)
    return lax.ppermute(array, axis, [(i, (i + by) % length) for i in range(length)])


def allowed_mask(query_start, key_start, query_docs, key_docs, active):
    query_pos = query_start + jnp.arange(query_docs.shape[0], dtype=jnp.int32)[:, None]
    key_pos = key_start + jnp.arange(key_docs.shape[0], dtype=jnp.int32)[None, :]
    return active & (key_pos <= query_pos) & (query_docs[:, None] == key_docs[None, :])


def head_scores(query_rows, key_block, allowed, q_heads):
    inv_root = 1.0 / math.sqrt(key_block.shape[1])
    scores = jnp.dot(query_rows, key_block.T, preferred_element_type=jnp.float32) * inv_root
    scores = scores.reshape(q_heads, -1, key_block.shape[0])
    return jnp.where(allowed[None], scores, -1e30)


def forward_step(state, query_rows, key_block, value_block, allowed, q_heads):
    top_score, total, output = state
    scores = head_scores(query_rows, key_block, allowed, q_heads)
    new_top = jnp.maximum(top_score, jnp.max(scores, axis=-1, keepdims=True))
    rescale = jnp.exp(top_score - new_top)
    probs = jnp.exp(scores - new_top)
    total = total * rescale + jnp.sum(probs, axis=-1, keepdims=True)
    weighted = jnp.dot(
        probs.astype(jnp.bfloat16).reshape(-1, key_block.shape[0]),
        value_block,
        preferred_element_type=jnp.float32,
    )
    output = output * rescale.reshape(-1, 1) + weighted
    return (new_top, total, output)


def finish(state, dout_rows, q_heads):
    top_score, total, output = state
    log_total = top_score + jnp.log(total)
    result = output / total.reshape(-1, 1)
    row_dot = jnp.sum(dout_rows.astype(jnp.float32) * result, axis=-1).reshape(q_heads, -1, 1)
    return (log_total, row_dot)


def backward_step(
    query_rows, dout_rows, key_block, value_block, allowed, log_total, row_dot, q_heads
):
    inv_root = 1.0 / math.sqrt(key_block.shape[1])
    width = key_block.shape[0]
    scores = head_scores(query_rows, key_block, allowed, q_heads)
    probs = jnp.exp(scores - log_total)
    grad_probs = jnp.dot(dout_rows, value_block.T, preferred_element_type=jnp.float32).reshape(
        q_heads, -1, width
    )
    grad_scores = probs * (grad_probs - row_dot)
    probs_low = probs.astype(jnp.bfloat16).reshape(-1, width)
    grad_low = grad_scores.astype(jnp.bfloat16).reshape(-1, width)
    value_grad = jnp.dot(probs_low.T, dout_rows, preferred_element_type=jnp.float32)
    key_grad = jnp.dot(grad_low.T, query_rows, preferred_element_type=jnp.float32) * inv_root
    query_grad = jnp.dot(grad_low, key_block, preferred_element_type=jnp.float32) * inv_root
    return (query_grad, key_grad, value_grad)


def to_rows(array, groups, block_rows):
    return (
        array.reshape(block_rows, groups * QPK, HD)
        .transpose(1, 0, 2)
        .reshape(groups, QPK * block_rows, HD)
    )


def shards(query, key, value, dout, doc_ids, pair_flags):
    keys_all, values_all = (
        lax.all_to_all(key, "head", split_axis=1, concat_axis=0, tiled=True),
        lax.all_to_all(value, "head", split_axis=1, concat_axis=0, tiled=True),
    )
    block_rows = keys_all.shape[0]
    groups = keys_all.shape[1] // HD
    window = pair_flags.shape[1]
    block_count = doc_ids.shape[0] // block_rows
    q_heads = QPK
    own_block = lax.axis_index("ctx")
    query_start = own_block * block_rows
    query_docs = lax.dynamic_slice_in_dim(doc_ids, query_start, block_rows)
    query_rows = to_rows(query, groups, block_rows)
    dout_rows = to_rows(dout, groups, block_rows)
    received = [(keys_all, values_all)]
    packet = (keys_all, values_all)
    for offset in range(1, window):
        packet = passed_along((packet[0], packet[1]), "ctx", 1)
        received.append(packet)
    allowed_list = []
    actives = []
    for offset in range(window):
        source = (own_block - offset) % block_count
        key_start = source * block_rows
        key_docs = lax.dynamic_slice_in_dim(doc_ids, key_start, block_rows)
        active = (pair_flags[0, offset] > 0) & (own_block - offset >= 0)
        allowed_list.append(allowed_mask(query_start, key_start, query_docs, key_docs, active))
        actives.append(active)
    states = tuple(
        (
            (
                jnp.full((q_heads, block_rows, 1), -1e30, jnp.float32),
                jnp.zeros((q_heads, block_rows, 1), jnp.float32),
                jnp.zeros((q_heads * block_rows, HD), jnp.float32),
            )
            for group in range(groups)
        )
    )
    for offset in range(window):
        keys_here, values_here = received[offset]

        def advance(
            states_in, keys_here=keys_here, values_here=values_here, allowed=allowed_list[offset]
        ):
            return tuple(
                (
                    forward_step(
                        states_in[group],
                        query_rows[group],
                        keys_here,
                        values_here,
                        allowed,
                        q_heads,
                    )
                    for group in range(groups)
                )
            )

        states = advance(states)
    finals = [finish(states[0], dout_rows[0], q_heads)]

    def gradients(offset):
        keys_here, values_here = received[offset]

        def contribute(
            unused, keys_here=keys_here, values_here=values_here, allowed=allowed_list[offset]
        ):
            query_part, key_part, value_part = backward_step(
                query_rows[0],
                dout_rows[0],
                keys_here,
                values_here,
                allowed,
                finals[0][0],
                finals[0][1],
                q_heads,
            )
            query_parts = [query_part]
            return (jnp.stack(query_parts), key_part, value_part)

        return contribute(0)

    query_acc = jnp.zeros((groups, q_heads * block_rows, HD), jnp.float32)
    key_grads = jnp.zeros((block_rows, groups * HD), jnp.float32)
    value_grads = jnp.zeros((block_rows, groups * HD), jnp.float32)
    for offset in range(window):
        if offset > 0:
            key_grads, value_grads = shifted((key_grads, value_grads), "ctx", 1)
        query_part, key_part, value_part = gradients(offset)
        query_acc = query_acc + query_part
        key_grads = key_grads + key_part
        value_grads = value_grads + value_part
    key_grads, value_grads = (
        shifted(key_grads.astype(jnp.bfloat16), "ctx", -(window - 1)).astype(key_grads.dtype),
        shifted(value_grads.astype(jnp.bfloat16), "ctx", -(window - 1)).astype(value_grads.dtype),
    )
    dquery = (
        query_acc.reshape(groups, q_heads, block_rows, HD)
        .transpose(2, 0, 1, 3)
        .reshape(block_rows, groups * q_heads * HD)
        .astype(jnp.bfloat16)
    )
    dkey, dvalue = (
        lax.all_to_all(
            key_grads.astype(jnp.bfloat16), "head", split_axis=0, concat_axis=1, tiled=True
        ),
        lax.all_to_all(
            value_grads.astype(jnp.bfloat16), "head", split_axis=0, concat_axis=1, tiled=True
        ),
    )
    return (dquery, dkey, dvalue)


def solution(mesh):
    in_specs = (
        P("ctx", "head"),
        P(("ctx", "head"), None),
        P(("ctx", "head"), None),
        P("ctx", "head"),
        P(),
        P("ctx", None),
    )
    out_specs = (P("ctx", "head"), P(("ctx", "head"), None), P(("ctx", "head"), None))
    return jax.shard_map(shards, mesh=mesh, in_specs=in_specs, out_specs=out_specs, check_vma=False)
```

profile of v0, /device:TPU:768, one launch (start us, length us, event | category | flops | bytes accessed | tf_op | source)
XLA Modules:
  0.0 172.6 jit_solution(17932704821786228923)
XLA Ops:
  2.1 4.5 %all-to-all-start = ((bf16[32,4,128]{2,0,1:T(8,128)(2,1)}), bf16[32,4,128]{2,0,1:T(8,128)(2,1)S(1)}, u32[]{:S(2)}, u32[]{:S(2)}) async-start(bf16[32,4,128]{2,0,1:T(8,128)(2,1)} %copy_bitcast_fusion.6), calls=%async_computation | async-start | bytes 65536 | tf_op jit(solution)/shard_map/all_to_all | solution.py:89
  9.6 2.4 %all-to-all-done = bf16[32,4,128]{2,0,1:T(8,128)(2,1)S(1)} async-done(((bf16[32,4,128]{2,0,1:T(8,128)(2,1)}), bf16[32,4,128]{2,0,1:T(8,128)(2,1)S(1)}, u32[]{:S(2)}, u32[]{:S(2)}) %all-to-all-start) | async-done | bytes 32800 | tf_op jit(solution)/shard_map/all_to_all | solution.py:89
  12.0 3.3 %all-to-all-start.1 = ((bf16[32,4,128]{2,0,1:T(8,128)(2,1)}), bf16[32,4,128]{2,0,1:T(8,128)(2,1)S(1)}, u32[]{:S(2)}, u32[]{:S(2)}) async-start(bf16[32,4,128]{2,0,1:T(8,128)(2,1)} %copy_bitcast_fusion.5), calls=%async_computation.1 | async-start | bytes 65536 | tf_op jit(solution)/shard_map/all_to_all | solution.py:90
  15.3 1.9 %collective-permute-start = (bf16[128,128]{1,0:T(8,128)(2,1)S(1)}, bf16[128,128]{1,0:T(8,128)(2,1)S(1)}, u32[]{:S(2)}, u32[]{:S(2)}) collective-permute-start(bf16[128,128]{1,0:T(8,128)(2,1)S(1)} %bitcast.618), channel_id=1, source_target_pairs={{0,4},{4,8},{8,12},{12,16},{16,20},{20,24},{24,28},{28,32},{32,36}... | collective-permute-start | bytes 98312 | tf_op jit(solution)/shard_map/ppermute | solution.py:15
  18.2 2.4 %all-to-all-done.1 = bf16[32,4,128]{2,0,1:T(8,128)(2,1)S(1)} async-done(((bf16[32,4,128]{2,0,1:T(8,128)(2,1)}), bf16[32,4,128]{2,0,1:T(8,128)(2,1)S(1)}, u32[]{:S(2)}, u32[]{:S(2)}) %all-to-all-start.1) | async-done | bytes 32800 | tf_op jit(solution)/shard_map/all_to_all | solution.py:90
  20.7 1.9 %collective-permute-start.7 = (bf16[128,128]{1,0:T(8,128)(2,1)S(1)}, bf16[128,128]{1,0:T(8,128)(2,1)S(1)}, u32[]{:S(2)}, u32[]{:S(2)}) collective-permute-start(bf16[128,128]{1,0:T(8,128)(2,1)S(1)} %bitcast.622), channel_id=1, source_target_pairs={{0,4},{4,8},{8,12},{12,16},{16,20},{20,24},{24,28},{28,32},{32,36}... | collective-permute-start | bytes 98312 | tf_op jit(solution)/shard_map/ppermute | solution.py:15
  23.8 2.3 %collective-permute-start.1 = (bf16[128,128]{1,0:T(8,128)(2,1)S(1)}, bf16[128,128]{1,0:T(8,128)(2,1)S(1)}, u32[]{:S(2)}, u32[]{:S(2)}) collective-permute-start(bf16[128,128]{1,0:T(8,128)(2,1)S(1)} %collective-permute-done), channel_id=1, source_target_pairs={{0,4},{4,8},{8,12},{12,16},{16,20},{20,24},{24,28},{28,32},{32,36}... | collective-permute-start | bytes 98312 | tf_op jit(solution)/shard_map/ppermute | solution.py:15
  26.1 3.1 %collective-permute-done.7 = bf16[128,128]{1,0:T(8,128)(2,1)S(1)} collective-permute-done((bf16[128,128]{1,0:T(8,128)(2,1)S(1)}, bf16[128,128]{1,0:T(8,128)(2,1)S(1)}, u32[]{:S(2)}, u32[]{:S(2)}) %collective-permute-start.7) | collective-permute-done | bytes 32800 | tf_op jit(solution)/shard_map/ppermute | solution.py:15
  29.2 1.9 %collective-permute-start.8 = (bf16[128,128]{1,0:T(8,128)(2,1)S(1)}, bf16[128,128]{1,0:T(8,128)(2,1)S(1)}, u32[]{:S(2)}, u32[]{:S(2)}) collective-permute-start(bf16[128,128]{1,0:T(8,128)(2,1)S(1)} %collective-permute-done.7), channel_id=1, source_target_pairs={{0,4},{4,8},{8,12},{12,16},{16,20},{20,24},{24,28},{28,32},{32,36}... | collective-permute-start | bytes 98312 | tf_op jit(solution)/shard_map/ppermute | solution.py:15
  32.4 1.9 %collective-permute-start.2 = (bf16[128,128]{1,0:T(8,128)(2,1)S(1)}, bf16[128,128]{1,0:T(8,128)(2,1)S(1)}, u32[]{:S(2)}, u32[]{:S(2)}) collective-permute-start(bf16[128,128]{1,0:T(8,128)(2,1)S(1)} %collective-permute-done.1), channel_id=1, source_target_pairs={{0,4},{4,8},{8,12},{12,16},{16,20},{20,24},{24,28},{28,32},{32,36}... | collective-permute-start | bytes 98312 | tf_op jit(solution)/shard_map/ppermute | solution.py:15
  34.3 3.5 %collective-permute-done.8 = bf16[128,128]{1,0:T(8,128)(2,1)S(1)} collective-permute-done((bf16[128,128]{1,0:T(8,128)(2,1)S(1)}, bf16[128,128]{1,0:T(8,128)(2,1)S(1)}, u32[]{:S(2)}, u32[]{:S(2)}) %collective-permute-start.8) | collective-permute-done | bytes 32800 | tf_op jit(solution)/shard_map/ppermute | solution.py:15
  37.8 1.9 %collective-permute-start.9 = (bf16[128,128]{1,0:T(8,128)(2,1)S(1)}, bf16[128,128]{1,0:T(8,128)(2,1)S(1)}, u32[]{:S(2)}, u32[]{:S(2)}) collective-permute-start(bf16[128,128]{1,0:T(8,128)(2,1)S(1)} %collective-permute-done.8), channel_id=1, source_target_pairs={{0,4},{4,8},{8,12},{12,16},{16,20},{20,24},{24,28},{28,32},{32,36}... | collective-permute-start | bytes 98312 | tf_op jit(solution)/shard_map/ppermute | solution.py:15
  40.9 1.9 %collective-permute-start.3 = (bf16[128,128]{1,0:T(8,128)(2,1)S(1)}, bf16[128,128]{1,0:T(8,128)(2,1)S(1)}, u32[]{:S(2)}, u32[]{:S(2)}) collective-permute-start(bf16[128,128]{1,0:T(8,128)(2,1)S(1)} %collective-permute-done.2), channel_id=1, source_target_pairs={{0,4},{4,8},{8,12},{12,16},{16,20},{20,24},{24,28},{28,32},{32,36}... | collective-permute-start | bytes 98312 | tf_op jit(solution)/shard_map/ppermute | solution.py:15
  46.3 1.9 %collective-permute-start.10 = (bf16[128,128]{1,0:T(8,128)(2,1)S(1)}, bf16[128,128]{1,0:T(8,128)(2,1)S(1)}, u32[]{:S(2)}, u32[]{:S(2)}) collective-permute-start(bf16[128,128]{1,0:T(8,128)(2,1)S(1)} %collective-permute-done.9), channel_id=1, source_target_pairs={{0,4},{4,8},{8,12},{12,16},{16,20},{20,24},{24,28},{28,32},{32,36}... | collective-permute-start | bytes 98312 | tf_op jit(solution)/shard_map/ppermute | solution.py:15
  49.4 1.9 %collective-permute-start.4 = (bf16[128,128]{1,0:T(8,128)(2,1)S(1)}, bf16[128,128]{1,0:T(8,128)(2,1)S(1)}, u32[]{:S(2)}, u32[]{:S(2)}) collective-permute-start(bf16[128,128]{1,0:T(8,128)(2,1)S(1)} %collective-permute-done.3), channel_id=1, source_target_pairs={{0,4},{4,8},{8,12},{12,16},{16,20},{20,24},{24,28},{28,32},{32,36}... | collective-permute-start | bytes 98312 | tf_op jit(solution)/shard_map/ppermute | solution.py:15
  51.5 3.3 %collective-permute-done.10 = bf16[128,128]{1,0:T(8,128)(2,1)S(1)} collective-permute-done((bf16[128,128]{1,0:T(8,128)(2,1)S(1)}, bf16[128,128]{1,0:T(8,128)(2,1)S(1)}, u32[]{:S(2)}, u32[]{:S(2)}) %collective-permute-start.10) | collective-permute-done | bytes 32800 | tf_op jit(solution)/shard_map/ppermute | solution.py:15
  54.8 1.9 %collective-permute-start.11 = (bf16[128,128]{1,0:T(8,128)(2,1)S(1)}, bf16[128,128]{1,0:T(8,128)(2,1)S(1)}, u32[]{:S(2)}, u32[]{:S(2)}) collective-permute-start(bf16[128,128]{1,0:T(8,128)(2,1)S(1)} %collective-permute-done.10), channel_id=1, source_target_pairs={{0,4},{4,8},{8,12},{12,16},{16,20},{20,24},{24,28},{28,32},{32,36}... | collective-permute-start | bytes 98312 | tf_op jit(solution)/shard_map/ppermute | solution.py:15
  58.0 1.9 %collective-permute-start.5 = (bf16[128,128]{1,0:T(8,128)(2,1)S(1)}, bf16[128,128]{1,0:T(8,128)(2,1)S(1)}, u32[]{:S(2)}, u32[]{:S(2)}) collective-permute-start(bf16[128,128]{1,0:T(8,128)(2,1)S(1)} %collective-permute-done.4), channel_id=1, source_target_pairs={{0,4},{4,8},{8,12},{12,16},{16,20},{20,24},{24,28},{28,32},{32,36}... | collective-permute-start | bytes 98312 | tf_op jit(solution)/shard_map/ppermute | solution.py:15
  63.4 1.9 %collective-permute-start.12 = (bf16[128,128]{1,0:T(8,128)(2,1)S(1)}, bf16[128,128]{1,0:T(8,128)(2,1)S(1)}, u32[]{:S(2)}, u32[]{:S(2)}) collective-permute-start(bf16[128,128]{1,0:T(8,128)(2,1)S(1)} %collective-permute-done.11), channel_id=1, source_target_pairs={{0,4},{4,8},{8,12},{12,16},{16,20},{20,24},{24,28},{28,32},{32,36}... | collective-permute-start | bytes 98312 | tf_op jit(solution)/shard_map/ppermute | solution.py:15
  66.5 1.9 %collective-permute-start.6 = (bf16[128,128]{1,0:T(8,128)(2,1)S(1)}, bf16[128,128]{1,0:T(8,128)(2,1)S(1)}, u32[]{:S(2)}, u32[]{:S(2)}) collective-permute-start(bf16[128,128]{1,0:T(8,128)(2,1)S(1)} %collective-permute-done.5), channel_id=1, source_target_pairs={{0,4},{4,8},{8,12},{12,16},{16,20},{20,24},{24,28},{28,32},{32,36}... | collective-permute-start | bytes 98312 | tf_op jit(solution)/shard_map/ppermute | solution.py:15
  71.9 1.9 %collective-permute-start.13 = (bf16[128,128]{1,0:T(8,128)(2,1)S(1)}, bf16[128,128]{1,0:T(8,128)(2,1)S(1)}, u32[]{:S(2)}, u32[]{:S(2)}) collective-permute-start(bf16[128,128]{1,0:T(8,128)(2,1)S(1)} %collective-permute-done.12), channel_id=1, source_target_pairs={{0,4},{4,8},{8,12},{12,16},{16,20},{20,24},{24,28},{28,32},{32,36}... | collective-permute-start | bytes 98312 | tf_op jit(solution)/shard_map/ppermute | solution.py:15
  78.9 1.9 %collective-permute-start.22 = (f32[128,128]{1,0:T(8,128)S(1)}, f32[128,128]{1,0:T(8,128)S(1)}, u32[]{:S(2)}, u32[]{:S(2)}) collective-permute-start(f32[128,128]{1,0:T(8,128)S(1)} %convolution_bitcast_fusion.7), channel_id=1, source_target_pairs={{0,4},{4,8},{8,12},{12,16},{16,20},{20,24},{24,28},{28,32},{32,36}... | collective-permute-start | bytes 196616 | tf_op jit(solution)/shard_map/ppermute | solution.py:20
  84.3 2.1 %collective-permute-start.14 = (f32[128,128]{1,0:T(8,128)S(1)}, f32[128,128]{1,0:T(8,128)S(1)}, u32[]{:S(2)}, u32[]{:S(2)}) collective-permute-start(f32[128,128]{1,0:T(8,128)S(1)} %fusion.35), channel_id=1, source_target_pairs={{0,4},{4,8},{8,12},{12,16},{16,20},{20,24},{24,28},{28,32},{32,36}... | collective-permute-start | bytes 196616 | tf_op jit(solution)/shard_map/ppermute | solution.py:20
  93.0 1.9 %collective-permute-start.23 = (f32[128,128]{1,0:T(8,128)S(1)}, f32[128,128]{1,0:T(8,128)S(1)}, u32[]{:S(2)}, u32[]{:S(2)}) collective-permute-start(f32[128,128]{1,0:T(8,128)S(1)} %fusion.37), channel_id=1, source_target_pairs={{0,4},{4,8},{8,12},{12,16},{16,20},{20,24},{24,28},{28,32},{32,36}... | collective-permute-start | bytes 196616 | tf_op jit(solution)/shard_map/ppermute | solution.py:20
  95.2 1.9 %collective-permute-start.15 = (f32[128,128]{1,0:T(8,128)S(1)}, f32[128,128]{1,0:T(8,128)S(1)}, u32[]{:S(2)}, u32[]{:S(2)}) collective-permute-start(f32[128,128]{1,0:T(8,128)S(1)} %fusion.36), channel_id=1, source_target_pairs={{0,4},{4,8},{8,12},{12,16},{16,20},{20,24},{24,28},{28,32},{32,36}... | collective-permute-start | bytes 196616 | tf_op jit(solution)/shard_map/ppermute | solution.py:20
  97.1 4.8 %collective-permute-done.23 = f32[128,128]{1,0:T(8,128)S(1)} collective-permute-done((f32[128,128]{1,0:T(8,128)S(1)}, f32[128,128]{1,0:T(8,128)S(1)}, u32[]{:S(2)}, u32[]{:S(2)}) %collective-permute-start.23) | collective-permute-done | bytes 65568 | tf_op jit(solution)/shard_map/ppermute | solution.py:20
  101.9 1.9 %collective-permute-start.24 = (f32[128,128]{1,0:T(8,128)S(1)}, f32[128,128]{1,0:T(8,128)S(1)}, u32[]{:S(2)}, u32[]{:S(2)}) collective-permute-start(f32[128,128]{1,0:T(8,128)S(1)} %add.469), channel_id=1, source_target_pairs={{0,4},{4,8},{8,12},{12,16},{16,20},{20,24},{24,28},{28,32},{32,36}... | collective-permute-start | bytes 196616 | tf_op jit(solution)/shard_map/ppermute | solution.py:20
  104.3 1.9 %collective-permute-start.16 = (f32[128,128]{1,0:T(8,128)S(1)}, f32[128,128]{1,0:T(8,128)S(1)}, u32[]{:S(2)}, u32[]{:S(2)}) collective-permute-start(f32[128,128]{1,0:T(8,128)S(1)} %add.462), channel_id=1, source_target_pairs={{0,4},{4,8},{8,12},{12,16},{16,20},{20,24},{24,28},{28,32},{32,36}... | collective-permute-start | bytes 196616 | tf_op jit(solution)/shard_map/ppermute | solution.py:20
  106.2 4.6 %collective-permute-done.24 = f32[128,128]{1,0:T(8,128)S(1)} collective-permute-done((f32[128,128]{1,0:T(8,128)S(1)}, f32[128,128]{1,0:T(8,128)S(1)}, u32[]{:S(2)}, u32[]{:S(2)}) %collective-permute-start.24) | collective-permute-done | bytes 65568 | tf_op jit(solution)/shard_map/ppermute | solution.py:20
  110.8 1.9 %collective-permute-start.25 = (f32[128,128]{1,0:T(8,128)S(1)}, f32[128,128]{1,0:T(8,128)S(1)}, u32[]{:S(2)}, u32[]{:S(2)}) collective-permute-start(f32[128,128]{1,0:T(8,128)S(1)} %add.470), channel_id=1, source_target_pairs={{0,4},{4,8},{8,12},{12,16},{16,20},{20,24},{24,28},{28,32},{32,36}... | collective-permute-start | bytes 196616 | tf_op jit(solution)/shard_map/ppermute | solution.py:20
  113.2 1.9 %collective-permute-start.17 = (f32[128,128]{1,0:T(8,128)S(1)}, f32[128,128]{1,0:T(8,128)S(1)}, u32[]{:S(2)}, u32[]{:S(2)}) collective-permute-start(f32[128,128]{1,0:T(8,128)S(1)} %add.463), channel_id=1, source_target_pairs={{0,4},{4,8},{8,12},{12,16},{16,20},{20,24},{24,28},{28,32},{32,36}... | collective-permute-start | bytes 196616 | tf_op jit(solution)/shard_map/ppermute | solution.py:20
  115.2 4.6 %collective-permute-done.25 = f32[128,128]{1,0:T(8,128)S(1)} collective-permute-done((f32[128,128]{1,0:T(8,128)S(1)}, f32[128,128]{1,0:T(8,128)S(1)}, u32[]{:S(2)}, u32[]{:S(2)}) %collective-permute-start.25) | collective-permute-done | bytes 65568 | tf_op jit(solution)/shard_map/ppermute | solution.py:20
  119.8 1.9 %collective-permute-start.26 = (f32[128,128]{1,0:T(8,128)S(1)}, f32[128,128]{1,0:T(8,128)S(1)}, u32[]{:S(2)}, u32[]{:S(2)}) collective-permute-start(f32[128,128]{1,0:T(8,128)S(1)} %add.471), channel_id=1, source_target_pairs={{0,4},{4,8},{8,12},{12,16},{16,20},{20,24},{24,28},{28,32},{32,36}... | collective-permute-start | bytes 196616 | tf_op jit(solution)/shard_map/ppermute | solution.py:20
  122.1 1.9 %collective-permute-start.18 = (f32[128,128]{1,0:T(8,128)S(1)}, f32[128,128]{1,0:T(8,128)S(1)}, u32[]{:S(2)}, u32[]{:S(2)}) collective-permute-start(f32[128,128]{1,0:T(8,128)S(1)} %add.464), channel_id=1, source_target_pairs={{0,4},{4,8},{8,12},{12,16},{16,20},{20,24},{24,28},{28,32},{32,36}... | collective-permute-start | bytes 196616 | tf_op jit(solution)/shard_map/ppermute | solution.py:20
  124.1 4.6 %collective-permute-done.26 = f32[128,128]{1,0:T(8,128)S(1)} collective-permute-done((f32[128,128]{1,0:T(8,128)S(1)}, f32[128,128]{1,0:T(8,128)S(1)}, u32[]{:S(2)}, u32[]{:S(2)}) %collective-permute-start.26) | collective-permute-done | bytes 65568 | tf_op jit(solution)/shard_map/ppermute | solution.py:20
  128.7 1.9 %collective-permute-start.27 = (f32[128,128]{1,0:T(8,128)S(1)}, f32[128,128]{1,0:T(8,128)S(1)}, u32[]{:S(2)}, u32[]{:S(2)}) collective-permute-start(f32[128,128]{1,0:T(8,128)S(1)} %add.472), channel_id=1, source_target_pairs={{0,4},{4,8},{8,12},{12,16},{16,20},{20,24},{24,28},{28,32},{32,36}... | collective-permute-start | bytes 196616 | tf_op jit(solution)/shard_map/ppermute | solution.py:20
  131.1 1.9 %collective-permute-start.19 = (f32[128,128]{1,0:T(8,128)S(1)}, f32[128,128]{1,0:T(8,128)S(1)}, u32[]{:S(2)}, u32[]{:S(2)}) collective-permute-start(f32[128,128]{1,0:T(8,128)S(1)} %add.465), channel_id=1, source_target_pairs={{0,4},{4,8},{8,12},{12,16},{16,20},{20,24},{24,28},{28,32},{32,36}... | collective-permute-start | bytes 196616 | tf_op jit(solution)/shard_map/ppermute | solution.py:20
  133.0 4.6 %collective-permute-done.27 = f32[128,128]{1,0:T(8,128)S(1)} collective-permute-done((f32[128,128]{1,0:T(8,128)S(1)}, f32[128,128]{1,0:T(8,128)S(1)}, u32[]{:S(2)}, u32[]{:S(2)}) %collective-permute-start.27) | collective-permute-done | bytes 65568 | tf_op jit(solution)/shard_map/ppermute | solution.py:20
  137.6 1.9 %collective-permute-start.28 = (f32[128,128]{1,0:T(8,128)S(1)}, f32[128,128]{1,0:T(8,128)S(1)}, u32[]{:S(2)}, u32[]{:S(2)}) collective-permute-start(f32[128,128]{1,0:T(8,128)S(1)} %add.473), channel_id=1, source_target_pairs={{0,4},{4,8},{8,12},{12,16},{16,20},{20,24},{24,28},{28,32},{32,36}... | collective-permute-start | bytes 196616 | tf_op jit(solution)/shard_map/ppermute | solution.py:20
  140.0 1.9 %collective-permute-start.20 = (f32[128,128]{1,0:T(8,128)S(1)}, f32[128,128]{1,0:T(8,128)S(1)}, u32[]{:S(2)}, u32[]{:S(2)}) collective-permute-start(f32[128,128]{1,0:T(8,128)S(1)} %add.466), channel_id=1, source_target_pairs={{0,4},{4,8},{8,12},{12,16},{16,20},{20,24},{24,28},{28,32},{32,36}... | collective-permute-start | bytes 196616 | tf_op jit(solution)/shard_map/ppermute | solution.py:20
  141.9 4.6 %collective-permute-done.28 = f32[128,128]{1,0:T(8,128)S(1)} collective-permute-done((f32[128,128]{1,0:T(8,128)S(1)}, f32[128,128]{1,0:T(8,128)S(1)}, u32[]{:S(2)}, u32[]{:S(2)}) %collective-permute-start.28) | collective-permute-done | bytes 65568 | tf_op jit(solution)/shard_map/ppermute | solution.py:20
  146.5 1.9 %collective-permute-start.29 = (bf16[128,128]{1,0:T(8,128)(2,1)S(1)}, bf16[128,128]{1,0:T(8,128)(2,1)}, u32[]{:S(2)}, u32[]{:S(2)}) collective-permute-start(bf16[128,128]{1,0:T(8,128)(2,1)S(1)} %add_convert_fusion), channel_id=1, source_target_pairs={{0,996},{4,1000},{8,1004},{12,1008},{16,1012},{20,1016},{24,1020},... | collective-permute-start | bytes 98312 | tf_op jit(solution)/shard_map/ppermute | solution.py:20
  148.9 1.9 %collective-permute-start.21 = (bf16[128,128]{1,0:T(8,128)(2,1)S(1)}, bf16[128,128]{1,0:T(8,128)(2,1)}, u32[]{:S(2)}, u32[]{:S(2)}) collective-permute-start(bf16[128,128]{1,0:T(8,128)(2,1)S(1)} %add_convert_fusion.1), channel_id=1, source_target_pairs={{0,996},{4,1000},{8,1004},{12,1008},{16,1012},{20,1016},{24,1020},... | collective-permute-start | bytes 98312 | tf_op jit(solution)/shard_map/ppermute | solution.py:20
  150.8 2.2 %collective-permute-done.29 = bf16[128,128]{1,0:T(8,128)(2,1)} collective-permute-done((bf16[128,128]{1,0:T(8,128)(2,1)S(1)}, bf16[128,128]{1,0:T(8,128)(2,1)}, u32[]{:S(2)}, u32[]{:S(2)}) %collective-permute-start.29) | collective-permute-done | bytes 32800 | tf_op jit(solution)/shard_map/ppermute | solution.py:20
  153.1 4.8 %all-to-all-start.3 = ((bf16[4,32,128]{2,1,0:T(8,128)(2,1)}), bf16[4,32,128]{2,1,0:T(8,128)(2,1)S(1)}, u32[]{:S(2)}, u32[]{:S(2)}) async-start(bf16[4,32,128]{2,1,0:T(8,128)(2,1)} %bitcast.88), calls=%async_computation.3 | async-start | bytes 65536 | tf_op jit(solution)/shard_map/all_to_all | solution.py:194
  159.0 4.3 %all-to-all-done.3 = bf16[4,32,128]{2,1,0:T(8,128)(2,1)S(1)} async-done(((bf16[4,32,128]{2,1,0:T(8,128)(2,1)}), bf16[4,32,128]{2,1,0:T(8,128)(2,1)S(1)}, u32[]{:S(2)}, u32[]{:S(2)}) %all-to-all-start.3) | async-done | bytes 32800 | tf_op jit(solution)/shard_map/all_to_all | solution.py:194
  163.3 3.3 %all-to-all-start.2 = ((bf16[4,32,128]{2,1,0:T(8,128)(2,1)}), bf16[4,32,128]{2,1,0:T(8,128)(2,1)S(1)}, u32[]{:S(2)}, u32[]{:S(2)}) async-start(bf16[4,32,128]{2,1,0:T(8,128)(2,1)} %bitcast.78), calls=%async_computation.2 | async-start | bytes 65536 | tf_op jit(solution)/shard_map/all_to_all | solution.py:191
  167.2 4.8 %all-to-all-done.2 = bf16[4,32,128]{2,1,0:T(8,128)(2,1)S(1)} async-done(((bf16[4,32,128]{2,1,0:T(8,128)(2,1)}), bf16[4,32,128]{2,1,0:T(8,128)(2,1)S(1)}, u32[]{:S(2)}, u32[]{:S(2)}) %all-to-all-start.2) | async-done | bytes 32800 | tf_op jit(solution)/shard_map/all_to_all | solution.py:191
  (117 shorter events, 38.5 us)
Async XLA Ops:
  0.6 7.5 %copy-start = (bf16[128,1024]{1,0:T(8,128)(2,1)S(1)}, bf16[128,1024]{1,0:T(8,128)(2,1)}, u32[]{:S(2)}) copy-start(bf16[128,1024]{1,0:T(8,128)(2,1)} %param.9) | copy-start | bytes 786436
  2.1 9.9 %all-to-all-start = ((bf16[32,4,128]{2,0,1:T(8,128)(2,1)}), bf16[32,4,128]{2,0,1:T(8,128)(2,1)S(1)}, u32[]{:S(2)}, u32[]{:S(2)}) async-start(bf16[32,4,128]{2,0,1:T(8,128)(2,1)} %copy_bitcast_fusion.6), calls=%async_computation | async-start | bytes 65536 | tf_op jit(solution)/shard_map/all_to_all | solution.py:89
  6.5 1.0 copy-start.2
  8.2 0.7 copy-start.3
  12.0 8.7 %all-to-all-start.1 = ((bf16[32,4,128]{2,0,1:T(8,128)(2,1)}), bf16[32,4,128]{2,0,1:T(8,128)(2,1)S(1)}, u32[]{:S(2)}, u32[]{:S(2)}) async-start(bf16[32,4,128]{2,0,1:T(8,128)(2,1)} %copy_bitcast_fusion.5), calls=%async_computation.1 | async-start | bytes 65536 | tf_op jit(solution)/shard_map/all_to_all | solution.py:90
  15.3 8.6 %collective-permute-start = (bf16[128,128]{1,0:T(8,128)(2,1)S(1)}, bf16[128,128]{1,0:T(8,128)(2,1)S(1)}, u32[]{:S(2)}, u32[]{:S(2)}) collective-permute-start(bf16[128,128]{1,0:T(8,128)(2,1)S(1)} %bitcast.618), channel_id=1, source_target_pairs={{0,4},{4,8},{8,12},{12,16},{16,20},{20,24},{24,28},{28,32},{32,36}... | collective-permute-start | bytes 98312 | tf_op jit(solution)/shard_map/ppermute | solution.py:15
  20.7 8.5 %collective-permute-start.7 = (bf16[128,128]{1,0:T(8,128)(2,1)S(1)}, bf16[128,128]{1,0:T(8,128)(2,1)S(1)}, u32[]{:S(2)}, u32[]{:S(2)}) collective-permute-start(bf16[128,128]{1,0:T(8,128)(2,1)S(1)} %bitcast.622), channel_id=1, source_target_pairs={{0,4},{4,8},{8,12},{12,16},{16,20},{20,24},{24,28},{28,32},{32,36}... | collective-permute-start | bytes 98312 | tf_op jit(solution)/shard_map/ppermute | solution.py:15
  23.8 8.5 %collective-permute-start.1 = (bf16[128,128]{1,0:T(8,128)(2,1)S(1)}, bf16[128,128]{1,0:T(8,128)(2,1)S(1)}, u32[]{:S(2)}, u32[]{:S(2)}) collective-permute-start(bf16[128,128]{1,0:T(8,128)(2,1)S(1)} %collective-permute-done), channel_id=1, source_target_pairs={{0,4},{4,8},{8,12},{12,16},{16,20},{20,24},{24,28},{28,32},{32,36}... | collective-permute-start | bytes 98312 | tf_op jit(solution)/shard_map/ppermute | solution.py:15
  29.2 8.5 %collective-permute-start.8 = (bf16[128,128]{1,0:T(8,128)(2,1)S(1)}, bf16[128,128]{1,0:T(8,128)(2,1)S(1)}, u32[]{:S(2)}, u32[]{:S(2)}) collective-permute-start(bf16[128,128]{1,0:T(8,128)(2,1)S(1)} %collective-permute-done.7), channel_id=1, source_target_pairs={{0,4},{4,8},{8,12},{12,16},{16,20},{20,24},{24,28},{28,32},{32,36}... | collective-permute-start | bytes 98312 | tf_op jit(solution)/shard_map/ppermute | solution.py:15
  32.4 8.5 %collective-permute-start.2 = (bf16[128,128]{1,0:T(8,128)(2,1)S(1)}, bf16[128,128]{1,0:T(8,128)(2,1)S(1)}, u32[]{:S(2)}, u32[]{:S(2)}) collective-permute-start(bf16[128,128]{1,0:T(8,128)(2,1)S(1)} %collective-permute-done.1), channel_id=1, source_target_pairs={{0,4},{4,8},{8,12},{12,16},{16,20},{20,24},{24,28},{28,32},{32,36}... | collective-permute-start | bytes 98312 | tf_op jit(solution)/shard_map/ppermute | solution.py:15
  37.8 8.5 %collective-permute-start.9 = (bf16[128,128]{1,0:T(8,128)(2,1)S(1)}, bf16[128,128]{1,0:T(8,128)(2,1)S(1)}, u32[]{:S(2)}, u32[]{:S(2)}) collective-permute-start(bf16[128,128]{1,0:T(8,128)(2,1)S(1)} %collective-permute-done.8), channel_id=1, source_target_pairs={{0,4},{4,8},{8,12},{12,16},{16,20},{20,24},{24,28},{28,32},{32,36}... | collective-permute-start | bytes 98312 | tf_op jit(solution)/shard_map/ppermute | solution.py:15
  40.9 8.5 %collective-permute-start.3 = (bf16[128,128]{1,0:T(8,128)(2,1)S(1)}, bf16[128,128]{1,0:T(8,128)(2,1)S(1)}, u32[]{:S(2)}, u32[]{:S(2)}) collective-permute-start(bf16[128,128]{1,0:T(8,128)(2,1)S(1)} %collective-permute-done.2), channel_id=1, source_target_pairs={{0,4},{4,8},{8,12},{12,16},{16,20},{20,24},{24,28},{28,32},{32,36}... | collective-permute-start | bytes 98312 | tf_op jit(solution)/shard_map/ppermute | solution.py:15
  46.3 8.5 %collective-permute-start.10 = (bf16[128,128]{1,0:T(8,128)(2,1)S(1)}, bf16[128,128]{1,0:T(8,128)(2,1)S(1)}, u32[]{:S(2)}, u32[]{:S(2)}) collective-permute-start(bf16[128,128]{1,0:T(8,128)(2,1)S(1)} %collective-permute-done.9), channel_id=1, source_target_pairs={{0,4},{4,8},{8,12},{12,16},{16,20},{20,24},{24,28},{28,32},{32,36}... | collective-permute-start | bytes 98312 | tf_op jit(solution)/shard_map/ppermute | solution.py:15
  49.4 8.5 %collective-permute-start.4 = (bf16[128,128]{1,0:T(8,128)(2,1)S(1)}, bf16[128,128]{1,0:T(8,128)(2,1)S(1)}, u32[]{:S(2)}, u32[]{:S(2)}) collective-permute-start(bf16[128,128]{1,0:T(8,128)(2,1)S(1)} %collective-permute-done.3), channel_id=1, source_target_pairs={{0,4},{4,8},{8,12},{12,16},{16,20},{20,24},{24,28},{28,32},{32,36}... | collective-permute-start | bytes 98312 | tf_op jit(solution)/shard_map/ppermute | solution.py:15
  54.8 8.5 %collective-permute-start.11 = (bf16[128,128]{1,0:T(8,128)(2,1)S(1)}, bf16[128,128]{1,0:T(8,128)(2,1)S(1)}, u32[]{:S(2)}, u32[]{:S(2)}) collective-permute-start(bf16[128,128]{1,0:T(8,128)(2,1)S(1)} %collective-permute-done.10), channel_id=1, source_target_pairs={{0,4},{4,8},{8,12},{12,16},{16,20},{20,24},{24,28},{28,32},{32,36}... | collective-permute-start | bytes 98312 | tf_op jit(solution)/shard_map/ppermute | solution.py:15
  58.0 8.5 %collective-permute-start.5 = (bf16[128,128]{1,0:T(8,128)(2,1)S(1)}, bf16[128,128]{1,0:T(8,128)(2,1)S(1)}, u32[]{:S(2)}, u32[]{:S(2)}) collective-permute-start(bf16[128,128]{1,0:T(8,128)(2,1)S(1)} %collective-permute-done.4), channel_id=1, source_target_pairs={{0,4},{4,8},{8,12},{12,16},{16,20},{20,24},{24,28},{28,32},{32,36}... | collective-permute-start | bytes 98312 | tf_op jit(solution)/shard_map/ppermute | solution.py:15
  63.4 8.5 %collective-permute-start.12 = (bf16[128,128]{1,0:T(8,128)(2,1)S(1)}, bf16[128,128]{1,0:T(8,128)(2,1)S(1)}, u32[]{:S(2)}, u32[]{:S(2)}) collective-permute-start(bf16[128,128]{1,0:T(8,128)(2,1)S(1)} %collective-permute-done.11), channel_id=1, source_target_pairs={{0,4},{4,8},{8,12},{12,16},{16,20},{20,24},{24,28},{28,32},{32,36}... | collective-permute-start | bytes 98312 | tf_op jit(solution)/shard_map/ppermute | solution.py:15
  66.5 8.5 %collective-permute-start.6 = (bf16[128,128]{1,0:T(8,128)(2,1)S(1)}, bf16[128,128]{1,0:T(8,128)(2,1)S(1)}, u32[]{:S(2)}, u32[]{:S(2)}) collective-permute-start(bf16[128,128]{1,0:T(8,128)(2,1)S(1)} %collective-permute-done.5), channel_id=1, source_target_pairs={{0,4},{4,8},{8,12},{12,16},{16,20},{20,24},{24,28},{28,32},{32,36}... | collective-permute-start | bytes 98312 | tf_op jit(solution)/shard_map/ppermute | solution.py:15
  71.9 10.8 %collective-permute-start.13 = (bf16[128,128]{1,0:T(8,128)(2,1)S(1)}, bf16[128,128]{1,0:T(8,128)(2,1)S(1)}, u32[]{:S(2)}, u32[]{:S(2)}) collective-permute-start(bf16[128,128]{1,0:T(8,128)(2,1)S(1)} %collective-permute-done.12), channel_id=1, source_target_pairs={{0,4},{4,8},{8,12},{12,16},{16,20},{20,24},{24,28},{28,32},{32,36}... | collective-permute-start | bytes 98312 | tf_op jit(solution)/shard_map/ppermute | solution.py:15
  78.9 13.7 %collective-permute-start.22 = (f32[128,128]{1,0:T(8,128)S(1)}, f32[128,128]{1,0:T(8,128)S(1)}, u32[]{:S(2)}, u32[]{:S(2)}) collective-permute-start(f32[128,128]{1,0:T(8,128)S(1)} %convolution_bitcast_fusion.7), channel_id=1, source_target_pairs={{0,4},{4,8},{8,12},{12,16},{16,20},{20,24},{24,28},{28,32},{32,36}... | collective-permute-start | bytes 196616 | tf_op jit(solution)/shard_map/ppermute | solution.py:20
  83.1 1.0 copy-start.1
  84.3 10.7 %collective-permute-start.14 = (f32[128,128]{1,0:T(8,128)S(1)}, f32[128,128]{1,0:T(8,128)S(1)}, u32[]{:S(2)}, u32[]{:S(2)}) collective-permute-start(f32[128,128]{1,0:T(8,128)S(1)} %fusion.35), channel_id=1, source_target_pairs={{0,4},{4,8},{8,12},{12,16},{16,20},{20,24},{24,28},{28,32},{32,36}... | collective-permute-start | bytes 196616 | tf_op jit(solution)/shard_map/ppermute | solution.py:20
  93.0 8.9 %collective-permute-start.23 = (f32[128,128]{1,0:T(8,128)S(1)}, f32[128,128]{1,0:T(8,128)S(1)}, u32[]{:S(2)}, u32[]{:S(2)}) collective-permute-start(f32[128,128]{1,0:T(8,128)S(1)} %fusion.37), channel_id=1, source_target_pairs={{0,4},{4,8},{8,12},{12,16},{16,20},{20,24},{24,28},{28,32},{32,36}... | collective-permute-start | bytes 196616 | tf_op jit(solution)/shard_map/ppermute | solution.py:20
  95.2 9.1 %collective-permute-start.15 = (f32[128,128]{1,0:T(8,128)S(1)}, f32[128,128]{1,0:T(8,128)S(1)}, u32[]{:S(2)}, u32[]{:S(2)}) collective-permute-start(f32[128,128]{1,0:T(8,128)S(1)} %fusion.36), channel_id=1, source_target_pairs={{0,4},{4,8},{8,12},{12,16},{16,20},{20,24},{24,28},{28,32},{32,36}... | collective-permute-start | bytes 196616 | tf_op jit(solution)/shard_map/ppermute | solution.py:20
  101.9 8.9 %collective-permute-start.24 = (f32[128,128]{1,0:T(8,128)S(1)}, f32[128,128]{1,0:T(8,128)S(1)}, u32[]{:S(2)}, u32[]{:S(2)}) collective-permute-start(f32[128,128]{1,0:T(8,128)S(1)} %add.469), channel_id=1, source_target_pairs={{0,4},{4,8},{8,12},{12,16},{16,20},{20,24},{24,28},{28,32},{32,36}... | collective-permute-start | bytes 196616 | tf_op jit(solution)/shard_map/ppermute | solution.py:20
  104.3 8.9 %collective-permute-start.16 = (f32[128,128]{1,0:T(8,128)S(1)}, f32[128,128]{1,0:T(8,128)S(1)}, u32[]{:S(2)}, u32[]{:S(2)}) collective-permute-start(f32[128,128]{1,0:T(8,128)S(1)} %add.462), channel_id=1, source_target_pairs={{0,4},{4,8},{8,12},{12,16},{16,20},{20,24},{24,28},{28,32},{32,36}... | collective-permute-start | bytes 196616 | tf_op jit(solution)/shard_map/ppermute | solution.py:20
  110.8 8.9 %collective-permute-start.25 = (f32[128,128]{1,0:T(8,128)S(1)}, f32[128,128]{1,0:T(8,128)S(1)}, u32[]{:S(2)}, u32[]{:S(2)}) collective-permute-start(f32[128,128]{1,0:T(8,128)S(1)} %add.470), channel_id=1, source_target_pairs={{0,4},{4,8},{8,12},{12,16},{16,20},{20,24},{24,28},{28,32},{32,36}... | collective-permute-start | bytes 196616 | tf_op jit(solution)/shard_map/ppermute | solution.py:20
  113.2 8.9 %collective-permute-start.17 = (f32[128,128]{1,0:T(8,128)S(1)}, f32[128,128]{1,0:T(8,128)S(1)}, u32[]{:S(2)}, u32[]{:S(2)}) collective-permute-start(f32[128,128]{1,0:T(8,128)S(1)} %add.463), channel_id=1, source_target_pairs={{0,4},{4,8},{8,12},{12,16},{16,20},{20,24},{24,28},{28,32},{32,36}... | collective-permute-start | bytes 196616 | tf_op jit(solution)/shard_map/ppermute | solution.py:20
  119.8 8.9 %collective-permute-start.26 = (f32[128,128]{1,0:T(8,128)S(1)}, f32[128,128]{1,0:T(8,128)S(1)}, u32[]{:S(2)}, u32[]{:S(2)}) collective-permute-start(f32[128,128]{1,0:T(8,128)S(1)} %add.471), channel_id=1, source_target_pairs={{0,4},{4,8},{8,12},{12,16},{16,20},{20,24},{24,28},{28,32},{32,36}... | collective-permute-start | bytes 196616 | tf_op jit(solution)/shard_map/ppermute | solution.py:20
  122.1 8.9 %collective-permute-start.18 = (f32[128,128]{1,0:T(8,128)S(1)}, f32[128,128]{1,0:T(8,128)S(1)}, u32[]{:S(2)}, u32[]{:S(2)}) collective-permute-start(f32[128,128]{1,0:T(8,128)S(1)} %add.464), channel_id=1, source_target_pairs={{0,4},{4,8},{8,12},{12,16},{16,20},{20,24},{24,28},{28,32},{32,36}... | collective-permute-start | bytes 196616 | tf_op jit(solution)/shard_map/ppermute | solution.py:20
  128.7 8.9 %collective-permute-start.27 = (f32[128,128]{1,0:T(8,128)S(1)}, f32[128,128]{1,0:T(8,128)S(1)}, u32[]{:S(2)}, u32[]{:S(2)}) collective-permute-start(f32[128,128]{1,0:T(8,128)S(1)} %add.472), channel_id=1, source_target_pairs={{0,4},{4,8},{8,12},{12,16},{16,20},{20,24},{24,28},{28,32},{32,36}... | collective-permute-start | bytes 196616 | tf_op jit(solution)/shard_map/ppermute | solution.py:20
  131.1 8.9 %collective-permute-start.19 = (f32[128,128]{1,0:T(8,128)S(1)}, f32[128,128]{1,0:T(8,128)S(1)}, u32[]{:S(2)}, u32[]{:S(2)}) collective-permute-start(f32[128,128]{1,0:T(8,128)S(1)} %add.465), channel_id=1, source_target_pairs={{0,4},{4,8},{8,12},{12,16},{16,20},{20,24},{24,28},{28,32},{32,36}... | collective-permute-start | bytes 196616 | tf_op jit(solution)/shard_map/ppermute | solution.py:20
  137.6 8.9 %collective-permute-start.28 = (f32[128,128]{1,0:T(8,128)S(1)}, f32[128,128]{1,0:T(8,128)S(1)}, u32[]{:S(2)}, u32[]{:S(2)}) collective-permute-start(f32[128,128]{1,0:T(8,128)S(1)} %add.473), channel_id=1, source_target_pairs={{0,4},{4,8},{8,12},{12,16},{16,20},{20,24},{24,28},{28,32},{32,36}... | collective-permute-start | bytes 196616 | tf_op jit(solution)/shard_map/ppermute | solution.py:20
  140.0 8.9 %collective-permute-start.20 = (f32[128,128]{1,0:T(8,128)S(1)}, f32[128,128]{1,0:T(8,128)S(1)}, u32[]{:S(2)}, u32[]{:S(2)}) collective-permute-start(f32[128,128]{1,0:T(8,128)S(1)} %add.466), channel_id=1, source_target_pairs={{0,4},{4,8},{8,12},{12,16},{16,20},{20,24},{24,28},{28,32},{32,36}... | collective-permute-start | bytes 196616 | tf_op jit(solution)/shard_map/ppermute | solution.py:20
  146.5 6.6 %collective-permute-start.29 = (bf16[128,128]{1,0:T(8,128)(2,1)S(1)}, bf16[128,128]{1,0:T(8,128)(2,1)}, u32[]{:S(2)}, u32[]{:S(2)}) collective-permute-start(bf16[128,128]{1,0:T(8,128)(2,1)S(1)} %add_convert_fusion), channel_id=1, source_target_pairs={{0,996},{4,1000},{8,1004},{12,1008},{16,1012},{20,1016},{24,1020},... | collective-permute-start | bytes 98312 | tf_op jit(solution)/shard_map/ppermute | solution.py:20
  148.9 10.1 %collective-permute-start.21 = (bf16[128,128]{1,0:T(8,128)(2,1)S(1)}, bf16[128,128]{1,0:T(8,128)(2,1)}, u32[]{:S(2)}, u32[]{:S(2)}) collective-permute-start(bf16[128,128]{1,0:T(8,128)(2,1)S(1)} %add_convert_fusion.1), channel_id=1, source_target_pairs={{0,996},{4,1000},{8,1004},{12,1008},{16,1012},{20,1016},{24,1020},... | collective-permute-start | bytes 98312 | tf_op jit(solution)/shard_map/ppermute | solution.py:20
  153.1 10.2 %all-to-all-start.3 = ((bf16[4,32,128]{2,1,0:T(8,128)(2,1)}), bf16[4,32,128]{2,1,0:T(8,128)(2,1)S(1)}, u32[]{:S(2)}, u32[]{:S(2)}) async-start(bf16[4,32,128]{2,1,0:T(8,128)(2,1)} %bitcast.88), calls=%async_computation.3 | async-start | bytes 65536 | tf_op jit(solution)/shard_map/all_to_all | solution.py:194
  163.3 8.7 %all-to-all-start.2 = ((bf16[4,32,128]{2,1,0:T(8,128)(2,1)}), bf16[4,32,128]{2,1,0:T(8,128)(2,1)S(1)}, u32[]{:S(2)}, u32[]{:S(2)}) async-start(bf16[4,32,128]{2,1,0:T(8,128)(2,1)} %bitcast.78), calls=%async_computation.2 | async-start | bytes 65536 | tf_op jit(solution)/shard_map/all_to_all | solution.py:191
where the time goes:
time: 174 us; the launch traced here: 173 us
  starting transfers between devices  73.8 us (42%)
  waiting for transfers between devices  65.2 us (37%)
  matrix products  15.3 us (9%)
  local copies, waits for them, and re-layouts  7.31 us (4%)
  between operations  6.52 us (4%)
  other arithmetic  4.49 us (3%)
    ppermute x16, starting transfers between devices, shifted(): lax.ppermute(array, axis, [(i, (i + by) % length) for i in range(length)])  30.9 us
    ppermute x16, waiting for transfers between devices, shifted(): lax.ppermute(array, axis, [(i, (i + by) % length) for i in range(length)])  30.5 us
    ppermute x14, starting transfers between devices, passed_along(): return lax.ppermute(array, axis, pairs)  27.1 us
    ppermute x14, waiting for transfers between devices, passed_along(): return lax.ppermute(array, axis, pairs)  20.7 us
    all_to_all x1, waiting for transfers between devices, shards(): lax.all_to_all(key_grads.astype(jnp.bfloat16), 'head', split_axis=0, conc...  4.8 us
    all_to_all x1, starting transfers between devices, shards(): lax.all_to_all(value_grads.astype(jnp.bfloat16), 'head', split_axis=0, co...  4.79 us
    all_to_all x1, starting transfers between devices, shards(): lax.all_to_all(key, 'head', split_axis=1, concat_axis=0, tiled=True)  4.46 us
    all_to_all x1, waiting for transfers between devices, shards(): lax.all_to_all(value_grads.astype(jnp.bfloat16), 'head', split_axis=0, co...  4.29 us
  transfers between devices with their start and end apart: 34, of which 25 were waited for; matrix products, arithmetic and copies ran while one was open for 14% of the time, Pallas kernels for 0%

commit v1 on v0

v1 whole, which is shorter than its diff:
```python
import math

import jax
import jax.numpy as jnp
from jax import lax
from jax.experimental import pallas as pl
from jax.experimental.pallas import tpu as pltpu
from jax.sharding import Mesh, PartitionSpec as P

HD = 128
QPK = 8
ROW = 8
VMEM = pl.BlockSpec(memory_space=pltpu.VMEM)
SMEM = pl.BlockSpec(memory_space=pltpu.SMEM)
CONTRACT_LAST = (((1,), (1,)), ((), ()))


def spread_kernel(place_ref, key_ref, value_ref, prev_ref, out_ref):
    j = place_ref[1]
    groups = key_ref.shape[1] // HD
    for g in range(groups):
        cols = slice(g * HD, (g + 1) * HD)
        own_k, own_v = key_ref[:, cols], value_ref[:, cols]
        prev_k = prev_ref[:, cols]
        prev_v = prev_ref[:, (groups + g) * HD : (groups + g + 1) * HD]
        for jp in range(ROW):
            own = j <= jp
            out_ref[jp * groups + g, :, :HD] = jnp.where(own, own_k, prev_k)
            out_ref[jp * groups + g, :, HD:] = jnp.where(own, own_v, prev_v)


def attention_kernel(
    place_ref, flags_ref, docs_ref, q_ref, do_ref, kv_ref, dq_ref, dkv_ref, cap, s_buf, dp_buf
):
    z, jp = place_ref[0], place_ref[1]
    block = q_ref.shape[0]
    root = 1.0 / math.sqrt(HD)
    to_exp2 = root * math.log2(math.e)
    own_docs = docs_ref[pl.ds(pl.multiple_of(z * ROW, ROW), ROW), :]
    prev_docs = docs_ref[pl.ds(pl.multiple_of(jnp.maximum(z - 1, 0) * ROW, ROW), ROW), :]
    row_at = lax.broadcasted_iota(jnp.int32, own_docs.shape, 0)
    query_docs = jnp.sum(jnp.where(row_at == jp, own_docs, 0), axis=0, keepdims=True)
    query_docs = query_docs.astype(jnp.float32)
    key_at = lax.broadcasted_iota(jnp.int32, (block, block), 0)
    query_at = lax.broadcasted_iota(jnp.int32, (block, block), 1)
    for j in range(ROW):
        own = j <= jp
        offset = jnp.where(own, jp - j, jp - j + ROW)
        active = (flags_ref[0, offset] > 0) & (z * ROW + jp - offset >= 0)
        docs = jnp.where(own, own_docs[j : j + 1], prev_docs[j : j + 1])
        docs = jnp.where(active, docs, -1).astype(jnp.float32)
        docs = jnp.broadcast_to(docs, (block, block)).T
        allowed = (docs == query_docs) & (key_at <= query_at + offset * block)
        cap[j * block : (j + 1) * block, :] = jnp.where(allowed, 3e38, -1e30)

    keys, values = kv_ref[:, :HD], kv_ref[:, HD:]
    keys_t = keys.T
    dk = dv = None
    for pair in range(QPK // 2):
        first, second = (slice((2 * pair + i) * HD, (2 * pair + i + 1) * HD) for i in (0, 1))
        q2 = jnp.concatenate([q_ref[:, first], q_ref[:, second]], axis=0)
        do2 = jnp.concatenate([do_ref[:, first], do_ref[:, second]], axis=0)
        s_now, dp_now = s_buf.at[pair % 2], dp_buf.at[pair % 2]
        tops = []
        for j in range(ROW):
            rows = slice(j * block, (j + 1) * block)
            s = lax.dot_general(
                kv_ref[rows, :HD], q2, CONTRACT_LAST, preferred_element_type=jnp.float32
            )
            c = cap[rows, :]
            s = jnp.minimum(s, jnp.concatenate([c, c], axis=1))
            s_now[rows, :] = s
            tops.append(jnp.max(s.reshape(-1, 8, 2 * block), axis=0))
            dp_now[rows, :] = lax.dot_general(
                kv_ref[rows, HD:], do2, CONTRACT_LAST, preferred_element_type=jnp.float32
            )
        top = tops[0]
        for t in tops[1:]:
            top = jnp.maximum(top, t)
        top = jnp.max(top, axis=0, keepdims=True)
        total = jnp.zeros((8, 2 * block), jnp.float32)
        dot = jnp.zeros((8, 2 * block), jnp.float32)
        for j in range(ROW):
            rows = slice(j * block, (j + 1) * block)
            e = jnp.exp2((s_now[rows, :] - top) * to_exp2)
            s_now[rows, :] = e
            total += jnp.sum(e.reshape(-1, 8, 2 * block), axis=0)
            dot += jnp.sum((e * dp_now[rows, :]).reshape(-1, 8, 2 * block), axis=0)
        inverse = 1.0 / jnp.sum(total, axis=0, keepdims=True)
        row_dot = jnp.sum(dot, axis=0, keepdims=True) * inverse
        probs, grads = [], []
        for j in range(ROW):
            rows = slice(j * block, (j + 1) * block)
            p = s_now[rows, :] * inverse
            probs.append(p.astype(jnp.bfloat16))
            grads.append((p * (dp_now[rows, :] - row_dot)).astype(jnp.bfloat16))
        probs = jnp.concatenate(probs, axis=0)
        grads = jnp.concatenate(grads, axis=0)
        dv_part = jnp.dot(probs, do2, preferred_element_type=jnp.float32)
        dk_part = jnp.dot(grads, q2, preferred_element_type=jnp.float32)
        dv = dv_part if dv is None else dv + dv_part
        dk = dk_part if dk is None else dk + dk_part
        dq_t = jnp.dot(keys_t, grads, preferred_element_type=jnp.float32) * root
        dq_ref[:, first] = dq_t[:, :block].T.astype(jnp.bfloat16)
        dq_ref[:, second] = dq_t[:, block:].T.astype(jnp.bfloat16)
    dkv_ref[:, :HD] = (dk * root).astype(jnp.bfloat16)
    dkv_ref[:, HD:] = dv.astype(jnp.bfloat16)


def sums_kernel(place_ref, parts_ref, own_ref, prev_ref):
    jp = place_ref[1]
    groups = parts_ref.shape[0] // ROW
    for g in range(groups):
        own = jnp.zeros(own_ref.shape[1:], jnp.float32)
        prev = jnp.zeros(own_ref.shape[1:], jnp.float32)
        for j in range(ROW):
            part = parts_ref[j * groups + g].astype(jnp.float32)
            own += jnp.where(j >= jp, part, 0.0)
            prev += jnp.where(j < jp, part, 0.0)
        own_ref[g] = own
        prev_ref[g] = prev.astype(jnp.bfloat16)


def join_kernel(own_ref, next_ref, dkey_ref, dvalue_ref):
    for g in range(own_ref.shape[0]):
        cols = slice(g * HD, (g + 1) * HD)
        both = own_ref[g] + next_ref[g].astype(jnp.float32)
        dkey_ref[:, cols] = both[:, :HD].astype(jnp.bfloat16)
        dvalue_ref[:, cols] = both[:, HD:].astype(jnp.bfloat16)


def shards(query, key, value, dout, doc_ids, pair_flags):
    shape = jax.ShapeDtypeStruct
    tokens, width = key.shape
    groups = width // HD
    block = query.shape[0]
    slots = ROW * groups
    rows = lax.axis_size("z")
    place = jnp.stack([lax.axis_index("z"), lax.axis_index("j")]).astype(jnp.int32)
    prev = lax.ppermute(
        jnp.concatenate([key, value], axis=1), "z", [(i, i + 1) for i in range(rows - 1)]
    )
    sent = pl.pallas_call(
        spread_kernel,
        out_shape=shape((slots, tokens, 2 * HD), jnp.bfloat16),
        in_specs=[SMEM, VMEM, VMEM, VMEM],
        out_specs=VMEM,
        name="spread",
    )(place, key, value, prev)
    taken = lax.all_to_all(sent, ("j", "head"), 0, 0, tiled=True)
    dquery, parts = pl.pallas_call(
        attention_kernel,
        out_shape=(
            shape(query.shape, jnp.bfloat16),
            shape((ROW * block, 2 * HD), jnp.bfloat16),
        ),
        in_specs=[SMEM, SMEM, VMEM, VMEM, VMEM, VMEM],
        out_specs=(VMEM, VMEM),
        scratch_shapes=[
            pltpu.VMEM((ROW * block, block), jnp.float32),
            pltpu.VMEM((2, ROW * block, 2 * block), jnp.float32),
            pltpu.VMEM((2, ROW * block, 2 * block), jnp.float32),
        ],
        name="attention",
    )(
        place,
        pair_flags,
        doc_ids.reshape(-1, block),
        query,
        dout,
        taken.reshape(ROW * block, 2 * HD),
    )
    back = lax.all_to_all(
        parts.reshape(slots, tokens, 2 * HD), ("j", "head"), 0, 0, tiled=True
    )
    own, to_prev = pl.pallas_call(
        sums_kernel,
        out_shape=(
            shape((groups, tokens, 2 * HD), jnp.float32),
            shape((groups, tokens, 2 * HD), jnp.bfloat16),
        ),
        in_specs=[SMEM, VMEM],
        out_specs=(VMEM, VMEM),
        name="sums",
    )(place, back)
    from_next = lax.ppermute(to_prev, "z", [(i, i - 1) for i in range(1, rows)])
    dkey, dvalue = pl.pallas_call(
        join_kernel,
        out_shape=(shape(key.shape, jnp.bfloat16), shape(value.shape, jnp.bfloat16)),
        in_specs=[VMEM, VMEM],
        out_specs=(VMEM, VMEM),
        name="join",
    )(own, from_next)
    return (dquery, dkey, dvalue)


def solution(mesh):
    ctx, head = mesh.shape["ctx"], mesh.shape["head"]
    fine = Mesh(mesh.devices.reshape(ctx // ROW, ROW, head), ("z", "j", "head"))
    by_token = P(("z", "j", "head"), None)
    in_specs = (
        P(("z", "j"), "head"),
        by_token,
        by_token,
        P(("z", "j"), "head"),
        P(),
        P(("z", "j"), None),
    )
    out_specs = (P(("z", "j"), "head"), by_token, by_token)
    return jax.shard_map(shards, mesh=fine, in_specs=in_specs, out_specs=out_specs, check_vma=False)
```

time: 174 us -> 70.5 us (0.41)
  the two profiles are of different devices: /device:TPU:768 before, /device:TPU:1 now
where the time goes in v1:
time: 70.5 us; the launch traced here: 69.6 us
  blocking collectives  43.4 us (62%)
  Pallas kernels  12 us (17%)
  starting transfers between devices  5.63 us (8%)
  waiting for transfers between devices  5.28 us (7%)
  other arithmetic  1.39 us (2%)
  local copies, waits for them, and re-layouts  1.26 us (2%)
    all_to_all x1, blocking collectives, shards(): taken = lax.all_to_all(sent, ('j', 'head'), 0, 0, tiled=True)  27 us
    all_to_all x1, blocking collectives, shards(): lax.all_to_all(parts.reshape(slots, tokens, 2 * HD), ('j', 'head'), 0, 0,...  16.4 us
    pallas_call x1, Pallas kernels, shards(): pl.pallas_call(attention_kernel, out_shape=(shape(query.shape, jnp.bfloat...  6.77 us
    ppermute x1, waiting for transfers between devices, shards(): from_next = lax.ppermute(to_prev, 'z', [(i, i - 1) for i in range(1, rows)])  4.55 us
    ppermute x1, starting transfers between devices, shards(): lax.ppermute(jnp.concatenate([key, value], axis=1), 'z', [(i, i + 1) for...  4.35 us
    pallas_call x1, Pallas kernels, shards(): pl.pallas_call(sums_kernel, out_shape=(shape((groups, tokens, 2 * HD), jn...  1.9 us
    pallas_call x1, Pallas kernels, shards(): pl.pallas_call(spread_kernel, out_shape=shape((slots, tokens, 2 * HD), jn...  1.76 us
    pallas_call x1, Pallas kernels, shards(): pl.pallas_call(join_kernel, out_shape=(shape(key.shape, jnp.bfloat16), sh...  1.55 us
  transfers between devices with their start and end apart: 2, of which 2 were waited for; matrix products, arithmetic and copies ran while one was open for 1% of the time, Pallas kernels for 0%

profile of v1, /device:TPU:1, one launch (start us, length us, event | category | flops | bytes accessed | tf_op | source)
XLA Modules:
  0.0 69.6 jit_solution(17837045140720491795)
XLA Ops:
  0.6 0.8 %pad_maximum_fusion = bf16[32,1024]{1,0:T(8,128)(2,1)S(1)} fusion(bf16[32,512]{1,0:T(8,128)(2,1)} %value_ref.1, bf16[32,512]{1,0:T(8,128)(2,1)} %key_ref.1), kind=kLoop, calls=%fused_computation | loop fusion | flops 131072 | bytes 131072 | tf_op jit(solution)/shard_map/concatenate | solution.py:141
  1.4 4.4 %collective-permute-start = (bf16[32,1024]{1,0:T(8,128)(2,1)S(1)}, bf16[32,1024]{1,0:T(8,128)(2,1)S(1)}, u32[]{:S(2)}, u32[]{:S(2)}) collective-permute-start(bf16[32,1024]{1,0:T(8,128)(2,1)S(1)} %pad_maximum_fusion), channel_id=1, source_target_pairs={{0,32},{32,64},{64,96},{96,128},{128,160},{160,192},{192,224},{224... | collective-permute-start | bytes 196616 | tf_op jit(solution)/shard_map/ppermute | solution.py:140
  5.8 0.6 pad_add_fusion.place_ref
  6.4 0.7 %collective-permute-done.prev_ref = bf16[32,1024]{1,0:T(8,128)(2,1)S(1)} collective-permute-done((bf16[32,1024]{1,0:T(8,128)(2,1)S(1)}, bf16[32,1024]{1,0:T(8,128)(2,1)S(1)}, u32[]{:S(2)}, u32[]{:S(2)}) %collective-permute-start) | collective-permute-done | bytes 65568 | tf_op jit(solution)/shard_map/ppermute | solution.py:140
  7.1 0.0 copy-start
  7.1 0.6 copy-done
  7.7 1.8 %spread.1 = bf16[32,32,256]{2,1,0:T(8,128)(2,1)} custom-call(s32[2]{0:T(128)} %pad_add_fusion.place_ref, bf16[32,512]{1,0:T(8,128)(2,1)} %key_ref.1, bf16[32,512]{1,0:T(8,128)(2,1)} %value_ref.1, bf16[32,1024]{1,0:T(8,128)(2,1)} %copy-done), custom_call_target="tpu_custom_call" | custom-call | tf_op jit(solution)/shard_map/spread/pallas_call | solution.py:143
  9.5 27.0 %all_to_all.10 = bf16[32,32,256]{2,1,0:T(8,128)(2,1)} all-to-all(bf16[32,32,256]{2,1,0:T(8,128)(2,1)} %spread.1), channel_id=1, replica_groups=mesh['z'=32,'j'=8,'head'=4] {'j','head'}, dimensions={0} | all-to-all | bytes 1048576 | tf_op jit(solution)/shard_map/all_to_all | solution.py:150
  36.5 6.8 %attention.1 = (bf16[128,1024]{1,0:T(8,128)(2,1)}, bf16[1024,256]{1,0:T(8,128)(2,1)}) custom-call(s32[2]{0:T(128)} %pad_add_fusion.place_ref, s32[1,8]{1,0:T(1,128)} %flags_ref.1, s32[256,128]{1,0:T(8,128)} %bitcast.7, bf16[128,1024]{1,0:T(8,128)(2,1)} %q_ref.1, bf16[128,1024]{1,0:T(8,128)(2,1)} %do_ref.1, bf16[1024,256]{1,0:T(8,128)(2,1)} %bitcast.5), custom_call_target="tpu_custom_call" | custom-call | tf_op jit(solution)/shard_map/attention/pallas_call | solution.py:151
  43.3 16.4 %all_to_all.11.parts_ref = bf16[32,32,256]{2,1,0:T(8,128)(2,1)} all-to-all(bf16[32,32,256]{2,1,0:T(8,128)(2,1)} %bitcast.6), channel_id=1, replica_groups=mesh['z'=32,'j'=8,'head'=4] {'j','head'}, dimensions={0} | all-to-all | bytes 1048576 | tf_op jit(solution)/shard_map/all_to_all | solution.py:173
  59.7 1.9 %sums.1 = (f32[4,32,256]{2,1,0:T(8,128)}, bf16[4,32,256]{2,1,0:T(8,128)(2,1)}) custom-call(s32[2]{0:T(128)} %pad_add_fusion.place_ref, bf16[32,32,256]{2,1,0:T(8,128)(2,1)} %all_to_all.11.parts_ref), custom_call_target="tpu_custom_call" | custom-call | tf_op jit(solution)/shard_map/sums/pallas_call | solution.py:176
  61.6 1.3 %collective-permute-start.1 = (bf16[4,32,256]{2,1,0:T(8,128)(2,1)}, bf16[4,32,256]{2,1,0:T(8,128)(2,1)S(1)}, u32[]{:S(2)}, u32[]{:S(2)}) collective-permute-start(bf16[4,32,256]{2,1,0:T(8,128)(2,1)} %get-tuple-element.12), channel_id=1, source_target_pairs={{32,0},{64,32},{96,64},{128,96},{160,128},{192,160},{224,192},{256... | collective-permute-start | bytes 196616 | tf_op jit(solution)/shard_map/ppermute | solution.py:186
  62.8 4.5 %collective-permute-done.1.next_ref = bf16[4,32,256]{2,1,0:T(8,128)(2,1)S(1)} collective-permute-done((bf16[4,32,256]{2,1,0:T(8,128)(2,1)}, bf16[4,32,256]{2,1,0:T(8,128)(2,1)S(1)}, u32[]{:S(2)}, u32[]{:S(2)}) %collective-permute-start.1) | collective-permute-done | bytes 65568 | tf_op jit(solution)/shard_map/ppermute | solution.py:186
  67.4 0.0 copy-start.1
  67.4 0.6 copy-done.1
  68.0 1.5 %join.1 = (bf16[32,512]{1,0:T(8,128)(2,1)}, bf16[32,512]{1,0:T(8,128)(2,1)}) custom-call(f32[4,32,256]{2,1,0:T(8,128)} %get-tuple-element.11.own_ref, bf16[4,32,256]{2,1,0:T(8,128)(2,1)} %copy-done.1), custom_call_target="tpu_custom_call" | custom-call | tf_op jit(solution)/shard_map/join/pallas_call | solution.py:187
Async XLA Ops:
  1.4 5.7 %collective-permute-start = (bf16[32,1024]{1,0:T(8,128)(2,1)S(1)}, bf16[32,1024]{1,0:T(8,128)(2,1)S(1)}, u32[]{:S(2)}, u32[]{:S(2)}) collective-permute-start(bf16[32,1024]{1,0:T(8,128)(2,1)S(1)} %pad_maximum_fusion), channel_id=1, source_target_pairs={{0,32},{32,64},{64,96},{96,128},{128,160},{160,192},{192,224},{224... | collective-permute-start | bytes 196616 | tf_op jit(solution)/shard_map/ppermute | solution.py:140
  7.1 0.6 copy-start
  61.6 5.8 %collective-permute-start.1 = (bf16[4,32,256]{2,1,0:T(8,128)(2,1)}, bf16[4,32,256]{2,1,0:T(8,128)(2,1)S(1)}, u32[]{:S(2)}, u32[]{:S(2)}) collective-permute-start(bf16[4,32,256]{2,1,0:T(8,128)(2,1)} %get-tuple-element.12), channel_id=1, source_target_pairs={{32,0},{64,32},{96,64},{128,96},{160,128},{192,160},{224,192},{256... | collective-permute-start | bytes 196616 | tf_op jit(solution)/shard_map/ppermute | solution.py:186
  67.4 0.6 copy-start.1

commit v2 on v1

--- a/solution.py
+++ b/solution.py
@@ -18,24 +18,20 @@
 def spread_kernel(place_ref, key_ref, value_ref, prev_ref, out_ref):
     j = place_ref[1]
     groups = key_ref.shape[1] // HD
-    for g in range(groups):
-        cols = slice(g * HD, (g + 1) * HD)
-        own_k, own_v = key_ref[:, cols], value_ref[:, cols]
-        prev_k = prev_ref[:, cols]
-        prev_v = prev_ref[:, (groups + g) * HD : (groups + g + 1) * HD]
-        for jp in range(ROW):
-            own = j <= jp
-            out_ref[jp * groups + g, :, :HD] = jnp.where(own, own_k, prev_k)
-            out_ref[jp * groups + g, :, HD:] = jnp.where(own, own_v, prev_v)
-
-
-def attention_kernel(
-    place_ref, flags_ref, docs_ref, q_ref, do_ref, kv_ref, dq_ref, dkv_ref, cap, s_buf, dp_buf
-):
+    for part, mine_ref in enumerate((key_ref, value_ref)):
+        for g in range(groups):
+            at = part * groups + g
+            mine = mine_ref[:, g * HD : (g + 1) * HD]
+            prev = prev_ref[:, at * HD : (at + 1) * HD]
+            for jp in range(ROW):
+                out_ref[jp * groups + g, :, part * HD : (part + 1) * HD] = jnp.where(
+                    j <= jp, mine, prev
+                )
+
+
+def mask_kernel(place_ref, flags_ref, docs_ref, cap_ref):
     z, jp = place_ref[0], place_ref[1]
-    block = q_ref.shape[0]
-    root = 1.0 / math.sqrt(HD)
-    to_exp2 = root * math.log2(math.e)
+    block = docs_ref.shape[1]
     own_docs = docs_ref[pl.ds(pl.multiple_of(z * ROW, ROW), ROW), :]
     prev_docs = docs_ref[pl.ds(pl.multiple_of(jnp.maximum(z - 1, 0) * ROW, ROW), ROW), :]
     row_at = lax.broadcasted_iota(jnp.int32, own_docs.shape, 0)
@@ -51,10 +47,13 @@
         docs = jnp.where(active, docs, -1).astype(jnp.float32)
         docs = jnp.broadcast_to(docs, (block, block)).T
         allowed = (docs == query_docs) & (key_at <= query_at + offset * block)
-        cap[j * block : (j + 1) * block, :] = jnp.where(allowed, 3e38, -1e30)
-
-    keys, values = kv_ref[:, :HD], kv_ref[:, HD:]
-    keys_t = keys.T
+        cap_ref[j * block : (j + 1) * block, :] = jnp.where(allowed, 3e38, -1e30)
+
+
+def attention_kernel(cap_ref, q_ref, do_ref, kv_ref, dkv_ref, grads_ref, s_buf, dp_buf):
+    block = q_ref.shape[0]
+    root = 1.0 / math.sqrt(HD)
+    to_exp2 = root * math.log2(math.e)
     dk = dv = None
     for pair in range(QPK // 2):
         first, second = (slice((2 * pair + i) * HD, (2 * pair + i + 1) * HD) for i in (0, 1))
@@ -67,7 +66,7 @@
             s = lax.dot_general(
                 kv_ref[rows, :HD], q2, CONTRACT_LAST, preferred_element_type=jnp.float32
             )
-            c = cap[rows, :]
+            c = cap_ref[rows, :]
             s = jnp.minimum(s, jnp.concatenate([c, c], axis=1))
             s_now[rows, :] = s
             tops.append(jnp.max(s.reshape(-1, 8, 2 * block), axis=0))
@@ -89,6 +88,7 @@
         inverse = 1.0 / jnp.sum(total, axis=0, keepdims=True)
         row_dot = jnp.sum(dot, axis=0, keepdims=True) * inverse
         probs, grads = [], []
+        both = slice(2 * pair * HD, (2 * pair + 2) * HD)
         for j in range(ROW):
             rows = slice(j * block, (j + 1) * block)
             p = s_now[rows, :] * inverse
@@ -100,11 +100,19 @@
         dk_part = jnp.dot(grads, q2, preferred_element_type=jnp.float32)
         dv = dv_part if dv is None else dv + dv_part
         dk = dk_part if dk is None else dk + dk_part
-        dq_t = jnp.dot(keys_t, grads, preferred_element_type=jnp.float32) * root
-        dq_ref[:, first] = dq_t[:, :block].T.astype(jnp.bfloat16)
-        dq_ref[:, second] = dq_t[:, block:].T.astype(jnp.bfloat16)
+        grads_ref[:, both] = grads
     dkv_ref[:, :HD] = (dk * root).astype(jnp.bfloat16)
     dkv_ref[:, HD:] = dv.astype(jnp.bfloat16)
+
+
+def dquery_kernel(kv_ref, grads_ref, dq_ref):
+    block = dq_ref.shape[0]
+    keys_t = kv_ref[:, :HD].T
+    dq_t = jnp.dot(keys_t, grads_ref[...], preferred_element_type=jnp.float32)
+    dq_t = dq_t * (1.0 / math.sqrt(HD))
+    for h in range(QPK):
+        cols = slice(h * HD, (h + 1) * HD)
+        dq_ref[:, cols] = dq_t[:, h * block : (h + 1) * block].T.astype(jnp.bfloat16)
 
 
 def sums_kernel(place_ref, parts_ref, own_ref, prev_ref):
@@ -129,68 +137,84 @@
         dvalue_ref[:, cols] = both[:, HD:].astype(jnp.bfloat16)
 
 
+def held(array):
+    return pltpu.with_memory_space_constraint(array, pltpu.VMEM)
+
+
 def shards(query, key, value, dout, doc_ids, pair_flags):
-    shape = jax.ShapeDtypeStruct
+    bf16, f32 = jnp.bfloat16, jnp.float32
     tokens, width = key.shape
     groups = width // HD
     block = query.shape[0]
     slots = ROW * groups
     rows = lax.axis_size("z")
     place = jnp.stack([lax.axis_index("z"), lax.axis_index("j")]).astype(jnp.int32)
-    prev = lax.ppermute(
-        jnp.concatenate([key, value], axis=1), "z", [(i, i + 1) for i in range(rows - 1)]
-    )
+    mine = jnp.concatenate([key, value], axis=1)
+    prev = lax.ppermute(mine, "z", [(i, i + 1) for i in range(rows - 1)])
     sent = pl.pallas_call(
         spread_kernel,
-        out_shape=shape((slots, tokens, 2 * HD), jnp.bfloat16),
+        out_shape=pltpu.VMEM((slots, tokens, 2 * HD), bf16),
         in_specs=[SMEM, VMEM, VMEM, VMEM],
         out_specs=VMEM,
+        compiler_params=pltpu.CompilerParams(vmem_limit_bytes=4 << 20),
         name="spread",
-    )(place, key, value, prev)
+    )(place, held(key), held(value), held(prev))
     taken = lax.all_to_all(sent, ("j", "head"), 0, 0, tiled=True)
-    dquery, parts = pl.pallas_call(
+    taken = taken.reshape(ROW * block, 2 * HD)
+    cap = pl.pallas_call(
+        mask_kernel,
+        out_shape=pltpu.VMEM((ROW * block, block), f32),
+        in_specs=[SMEM, SMEM, VMEM],
+        out_specs=VMEM,
+        compiler_params=pltpu.CompilerParams(vmem_limit_bytes=4 << 20),
+        name="mask",
+    )(place, pair_flags, doc_ids.reshape(-1, block))
+    parts, grads = pl.pallas_call(
         attention_kernel,
         out_shape=(
-            shape(query.shape, jnp.bfloat16),
-            shape((ROW * block, 2 * HD), jnp.bfloat16),
+            pltpu.VMEM((ROW * block, 2 * HD), bf16),
+            pltpu.VMEM((ROW * block, QPK * block), bf16),
         ),
-        in_specs=[SMEM, SMEM, VMEM, VMEM, VMEM, VMEM],
+        in_specs=[VMEM, VMEM, VMEM, VMEM],
         out_specs=(VMEM, VMEM),
-        scratch_shapes=[
-            pltpu.VMEM((ROW * block, block), jnp.float32),
-            pltpu.VMEM((2, ROW * block, 2 * block), jnp.float32),
-            pltpu.VMEM((2, ROW * block, 2 * block), jnp.float32),
-        ],
+        scratch_shapes=[pltpu.VMEM((2, ROW * block, 2 * block), f32)] * 2,
+        compiler_params=pltpu.CompilerParams(vmem_limit_bytes=32 << 20),
         name="attention",
-    )(
-        place,
-        pair_flags,
-        doc_ids.reshape(-1, block),
-        query,
-        dout,
-        taken.reshape(ROW * block, 2 * HD),
-    )
+    )(held(cap), held(query), held(dout), held(taken))
     back = lax.all_to_all(
         parts.reshape(slots, tokens, 2 * HD), ("j", "head"), 0, 0, tiled=True
     )
+    dquery = pl.pallas_call(
+        dquery_kernel,
+        out_shape=jax.ShapeDtypeStruct(query.shape, bf16),
+        in_specs=[VMEM, VMEM],
+        out_specs=VMEM,
+        compiler_params=pltpu.CompilerParams(vmem_limit_bytes=8 << 20),
+        name="dquery",
+    )(held(taken), held(grads))
     own, to_prev = pl.pallas_call(
         sums_kernel,
         out_shape=(
-            shape((groups, tokens, 2 * HD), jnp.float32),
-            shape((groups, tokens, 2 * HD), jnp.bfloat16),
+            pltpu.VMEM((groups, tokens, 2 * HD), f32),
+            pltpu.VMEM((groups, tokens, 2 * HD), bf16),
         ),
         in_specs=[SMEM, VMEM],
         out_specs=(VMEM, VMEM),
+        compiler_params=pltpu.CompilerParams(vmem_limit_bytes=4 << 20),
         name="sums",
-    )(place, back)
+    )(place, held(back))
     from_next = lax.ppermute(to_prev, "z", [(i, i - 1) for i in range(1, rows)])
     dkey, dvalue = pl.pallas_call(
         join_kernel,
-        out_shape=(shape(key.shape, jnp.bfloat16), shape(value.shape, jnp.bfloat16)),
+        out_shape=(
+            jax.ShapeDtypeStruct(key.shape, bf16),
+            jax.ShapeDtypeStruct(value.shape, bf16),
+        ),
         in_specs=[VMEM, VMEM],
         out_specs=(VMEM, VMEM),
+        compiler_params=pltpu.CompilerParams(vmem_limit_bytes=4 << 20),
         name="join",
-    )(own, from_next)
+    )(held(own), held(from_next))
     return (dquery, dkey, dvalue)
 
 

time: 70.5 us -> 63.9 us (0.906)
  blocking collectives: 43.4 us -> 15.3 us
  starting transfers between devices: 5.63 us -> 20.8 us
  waiting for transfers between devices: 5.28 us -> 13.2 us
  Pallas kernels: 12 us -> 9.07 us
  local copies, waits for them, and re-layouts: 1.26 us -> 3.08 us
    all_to_all x1 -> x0, blocking collectives: 27 us -> none  [shards(): taken = lax.all_to_all(sent, ('j', 'head'), 0, 0, tiled=True)]
    all_to_all x0 -> x1, starting transfers between devices: none -> 15.2 us  [shards(): taken = lax.all_to_all(sent, ('j', 'head'), 0, 0, tiled=True)]
    all_to_all x0 -> x1, waiting for transfers between devices: none -> 8.86 us  [shards(): taken = lax.all_to_all(sent, ('j', 'head'), 0, 0, tiled=True)]
    pallas_call x4 -> x6, Pallas kernels: 12 us -> 9.07 us  [the longest x1 4.26 us: shards(): pl.pallas_call(attention_kernel, out_shape=(pltpu.VMEM((ROW * block, 2 *...]
    unnamed x4 -> x12, local copies, waits for them, and re-layouts: 1.26 us -> 3.08 us
    ppermute x1, waiting for transfers between devices: 4.55 us -> 3.09 us  [shards(): from_next = lax.ppermute(to_prev, 'z', [(i, i - 1) for i in range(1, rows)])]
    all_to_all x1, blocking collectives: 16.4 us -> 15.3 us  [shards(): lax.all_to_all(parts.reshape(slots, tokens, 2 * HD), ('j', 'head'), 0, 0,...]
  transfers between devices with their start and end apart: 2 -> 3, of which waited for: 2 -> 3; matrix products, arithmetic and copies ran while one was open for 1% -> 0% of each run, Pallas kernels for 0% -> 3%
where the time goes in v2:
time: 63.9 us; the launch traced here: 63.1 us
  starting transfers between devices  20.8 us (33%)
  blocking collectives  15.3 us (24%)
  waiting for transfers between devices  13.2 us (21%)
  Pallas kernels  9.07 us (14%)
  local copies, waits for them, and re-layouts  3.08 us (5%)
  other arithmetic  0.91 us (1%)
  between operations  0.71 us (1%)
    all_to_all x1, blocking collectives, shards(): lax.all_to_all(parts.reshape(slots, tokens, 2 * HD), ('j', 'head'), 0, 0,...  15.3 us
    all_to_all x1, starting transfers between devices, shards(): taken = lax.all_to_all(sent, ('j', 'head'), 0, 0, tiled=True)  15.2 us
    all_to_all x1, waiting for transfers between devices, shards(): taken = lax.all_to_all(sent, ('j', 'head'), 0, 0, tiled=True)  8.86 us
    ppermute x1, starting transfers between devices, shards(): prev = lax.ppermute(mine, 'z', [(i, i + 1) for i in range(rows - 1)])  4.35 us
    pallas_call x1, Pallas kernels, shards(): pl.pallas_call(attention_kernel, out_shape=(pltpu.VMEM((ROW * block, 2 *...  4.26 us
    ppermute x1, waiting for transfers between devices, shards(): from_next = lax.ppermute(to_prev, 'z', [(i, i - 1) for i in range(1, rows)])  3.09 us
    unnamed x12, local copies, waits for them, and re-layouts  3.08 us
    pallas_call x1, Pallas kernels, shards(): pl.pallas_call(spread_kernel, out_shape=pltpu.VMEM((slots, tokens, 2 * HD...  1.42 us
  transfers between devices with their start and end apart: 3, of which 3 were waited for; matrix products, arithmetic and copies ran while one was open for 0% of the time, Pallas kernels for 3%

profile of v2, /device:TPU:1, one launch (start us, length us, event | category | flops | bytes accessed | tf_op | source)
XLA Modules:
  0.0 63.1 jit_solution(3324939516172792945)
XLA Ops:
  0.6 0.0 copy-start.1
  0.6 0.0 copy-start
  0.6 0.8 %pad_maximum_fusion = bf16[32,1024]{1,0:T(8,128)(2,1)S(1)} fusion(bf16[32,512]{1,0:T(8,128)(2,1)} %value_ref.1, bf16[32,512]{1,0:T(8,128)(2,1)} %key_ref.1), kind=kLoop, calls=%fused_computation | loop fusion | flops 131072 | bytes 131072 | tf_op jit(solution)/shard_map/concatenate | solution.py:152
  1.5 4.4 %collective-permute-start = (bf16[32,1024]{1,0:T(8,128)(2,1)S(1)}, bf16[32,1024]{1,0:T(8,128)(2,1)S(1)}, u32[]{:S(2)}, u32[]{:S(2)}) collective-permute-start(bf16[32,1024]{1,0:T(8,128)(2,1)S(1)} %pad_maximum_fusion), channel_id=1, source_target_pairs={{0,32},{32,64},{64,96},{96,128},{128,160},{160,192},{192,224},{224... | collective-permute-start | bytes 196616 | tf_op jit(solution)/shard_map/ppermute | solution.py:153
  5.9 0.1 pad_add_fusion.place_ref
  5.9 1.2 %collective-permute-done.prev_ref = bf16[32,1024]{1,0:T(8,128)(2,1)S(1)} collective-permute-done((bf16[32,1024]{1,0:T(8,128)(2,1)S(1)}, bf16[32,1024]{1,0:T(8,128)(2,1)S(1)}, u32[]{:S(2)}, u32[]{:S(2)}) %collective-permute-start) | collective-permute-done | bytes 65568 | tf_op jit(solution)/shard_map/ppermute | solution.py:153
  7.2 0.0 copy-start.3
  7.2 0.8 %copy-done.3 = bf16[32,512]{1,0:T(8,128)(2,1)S(1)} copy-done((bf16[32,512]{1,0:T(8,128)(2,1)S(1)}, bf16[32,512]{1,0:T(8,128)(2,1)}, u32[]{:S(2)}) %copy-start.3) | copy-done | bytes 32792
  7.9 0.0 copy-start.4
  7.9 0.8 %copy-done.4 = bf16[32,512]{1,0:T(8,128)(2,1)S(1)} copy-done((bf16[32,512]{1,0:T(8,128)(2,1)S(1)}, bf16[32,512]{1,0:T(8,128)(2,1)}, u32[]{:S(2)}) %copy-start.4) | copy-done | bytes 32792
  8.7 1.4 %spread.1 = bf16[32,32,256]{2,1,0:T(8,128)(2,1)} custom-call(s32[2]{0:T(128)S(1)} %pad_add_fusion.place_ref, bf16[32,512]{1,0:T(8,128)(2,1)S(1)} %copy-done.3, bf16[32,512]{1,0:T(8,128)(2,1)S(1)} %copy-done.4, bf16[32,1024]{1,0:T(8,128)(2,1)S(1)} %collective-permute-done.prev_ref), custom_call_target="tpu_custom_call" | custom-call | tf_op jit(solution)/shard_map/spread/pallas_call | solution.py:154
  10.1 15.2 %all-to-all-start = ((bf16[32,32,256]{2,1,0:T(8,128)(2,1)}), bf16[32,32,256]{2,1,0:T(8,128)(2,1)S(1)}, u32[]{:S(2)}, u32[]{:S(2)}) async-start(bf16[32,32,256]{2,1,0:T(8,128)(2,1)} %spread.1), calls=%async_computation | async-start | bytes 1048576 | tf_op jit(solution)/shard_map/all_to_all | solution.py:162
  25.3 0.0 copy-start.2
  25.3 0.9 %copy-done.2 = s32[32768]{0:T(1024)S(1)} copy-done((s32[32768]{0:T(1024)S(1)}, s32[32768]{0:T(1024)}, u32[]{:S(2)}) %copy-start.2) | copy-done | bytes 131096
  26.2 0.0 copy-start.5
  26.2 0.7 %copy-done.5 = s32[1,8]{1,0:T(1,128)S(1)} copy-done((s32[1,8]{1,0:T(1,128)S(1)}, s32[1,8]{1,0:T(1,128)}, u32[]{:S(2)}) %copy-start.5) | copy-done | bytes 56
  26.8 0.8 %mask.1.cap_ref = f32[1024,128]{1,0:T(8,128)S(1)} custom-call(s32[2]{0:T(128)S(1)} %pad_add_fusion.place_ref, s32[1,8]{1,0:T(1,128)S(1)} %copy-done.5, s32[256,128]{1,0:T(8,128)S(1)} %bitcast.8), custom_call_target="tpu_custom_call" | custom-call | tf_op jit(solution)/shard_map/mask/pallas_call | solution.py:164
  27.6 8.9 %all-to-all-done = bf16[32,32,256]{2,1,0:T(8,128)(2,1)S(1)} async-done(((bf16[32,32,256]{2,1,0:T(8,128)(2,1)}), bf16[32,32,256]{2,1,0:T(8,128)(2,1)S(1)}, u32[]{:S(2)}, u32[]{:S(2)}) %all-to-all-start) | async-done | bytes 524320 | tf_op jit(solution)/shard_map/all_to_all | solution.py:162
  36.5 0.0 copy-done.1
  36.5 0.0 copy-done
  36.5 4.3 %attention.1 = (bf16[1024,256]{1,0:T(8,128)(2,1)S(1)}, bf16[1024,1024]{1,0:T(8,128)(2,1)S(1)}) custom-call(f32[1024,128]{1,0:T(8,128)S(1)} %mask.1.cap_ref, bf16[128,1024]{1,0:T(8,128)(2,1)S(1)} %copy-done, bf16[128,1024]{1,0:T(8,128)(2,1)S(1)} %copy-done.1, bf16[1024,256]{1,0:T(8,128)(2,1)S(1)} %bitcast.5), custom_call_target="tpu_custom_call" | custom-call | tf_op jit(solution)/shard_map/attention/pallas_call | solution.py:172
  40.7 15.3 %all_to_all.10.parts_ref = bf16[32,32,256]{2,1,0:T(8,128)(2,1)S(1)} all-to-all(bf16[32,32,256]{2,1,0:T(8,128)(2,1)S(1)} %bitcast.7), channel_id=1, replica_groups=mesh['z'=32,'j'=8,'head'=4] {'j','head'}, dimensions={0} | all-to-all | bytes 1048576 | tf_op jit(solution)/shard_map/all_to_all | solution.py:184
  56.1 0.7 %sums.1 = (f32[4,32,256]{2,1,0:T(8,128)S(1)}, bf16[4,32,256]{2,1,0:T(8,128)(2,1)S(1)}) custom-call(s32[2]{0:T(128)S(1)} %pad_add_fusion.place_ref, bf16[32,32,256]{2,1,0:T(8,128)(2,1)S(1)} %all_to_all.10.parts_ref), custom_call_target="tpu_custom_call" | custom-call | tf_op jit(solution)/shard_map/sums/pallas_call | solution.py:195
  56.8 1.3 %collective-permute-start.1 = (bf16[4,32,256]{2,1,0:T(8,128)(2,1)S(1)}, bf16[4,32,256]{2,1,0:T(8,128)(2,1)S(1)}, u32[]{:S(2)}, u32[]{:S(2)}) collective-permute-start(bf16[4,32,256]{2,1,0:T(8,128)(2,1)S(1)} %get-tuple-element.12), channel_id=1, source_target_pairs={{32,0},{64,32},{96,64},{128,96},{160,128},{192,160},{224,192},{256... | collective-permute-start | bytes 196616 | tf_op jit(solution)/shard_map/ppermute | solution.py:206
  58.1 1.2 %dquery.1 = bf16[128,1024]{1,0:T(8,128)(2,1)} custom-call(bf16[1024,256]{1,0:T(8,128)(2,1)S(1)} %bitcast.6, bf16[1024,1024]{1,0:T(8,128)(2,1)S(1)} %get-tuple-element.9.grads_ref), custom_call_target="tpu_custom_call" | custom-call | tf_op jit(solution)/shard_map/dquery/pallas_call | solution.py:187
  59.4 3.1 %collective-permute-done.1.next_ref = bf16[4,32,256]{2,1,0:T(8,128)(2,1)S(1)} collective-permute-done((bf16[4,32,256]{2,1,0:T(8,128)(2,1)S(1)}, bf16[4,32,256]{2,1,0:T(8,128)(2,1)S(1)}, u32[]{:S(2)}, u32[]{:S(2)}) %collective-permute-start.1) | collective-permute-done | bytes 65568 | tf_op jit(solution)/shard_map/ppermute | solution.py:206
  62.5 0.6 %join.1 = (bf16[32,512]{1,0:T(8,128)(2,1)}, bf16[32,512]{1,0:T(8,128)(2,1)}) custom-call(f32[4,32,256]{2,1,0:T(8,128)S(1)} %get-tuple-element.11.own_ref, bf16[4,32,256]{2,1,0:T(8,128)(2,1)S(1)} %collective-permute-done.1.next_ref), custom_call_target="tpu_custom_call" | custom-call | tf_op jit(solution)/shard_map/join/pallas_call | solution.py:207
Async XLA Ops:
  0.6 35.8 %copy-start.1 = (bf16[128,1024]{1,0:T(8,128)(2,1)S(1)}, bf16[128,1024]{1,0:T(8,128)(2,1)}, u32[]{:S(2)}) copy-start(bf16[128,1024]{1,0:T(8,128)(2,1)} %do_ref.1) | copy-start | bytes 786436
  0.6 35.8 %copy-start = (bf16[128,1024]{1,0:T(8,128)(2,1)S(1)}, bf16[128,1024]{1,0:T(8,128)(2,1)}, u32[]{:S(2)}) copy-start(bf16[128,1024]{1,0:T(8,128)(2,1)} %q_ref.1) | copy-start | bytes 786436
  1.5 5.7 %collective-permute-start = (bf16[32,1024]{1,0:T(8,128)(2,1)S(1)}, bf16[32,1024]{1,0:T(8,128)(2,1)S(1)}, u32[]{:S(2)}, u32[]{:S(2)}) collective-permute-start(bf16[32,1024]{1,0:T(8,128)(2,1)S(1)} %pad_maximum_fusion), channel_id=1, source_target_pairs={{0,32},{32,64},{64,96},{96,128},{128,160},{160,192},{192,224},{224... | collective-permute-start | bytes 196616 | tf_op jit(solution)/shard_map/ppermute | solution.py:153
  7.2 0.8 %copy-start.3 = (bf16[32,512]{1,0:T(8,128)(2,1)S(1)}, bf16[32,512]{1,0:T(8,128)(2,1)}, u32[]{:S(2)}) copy-start(bf16[32,512]{1,0:T(8,128)(2,1)} %key_ref.1) | copy-start | bytes 98308
  7.9 0.8 %copy-start.4 = (bf16[32,512]{1,0:T(8,128)(2,1)S(1)}, bf16[32,512]{1,0:T(8,128)(2,1)}, u32[]{:S(2)}) copy-start(bf16[32,512]{1,0:T(8,128)(2,1)} %value_ref.1) | copy-start | bytes 98308
  10.1 26.4 %all-to-all-start = ((bf16[32,32,256]{2,1,0:T(8,128)(2,1)}), bf16[32,32,256]{2,1,0:T(8,128)(2,1)S(1)}, u32[]{:S(2)}, u32[]{:S(2)}) async-start(bf16[32,32,256]{2,1,0:T(8,128)(2,1)} %spread.1), calls=%async_computation | async-start | bytes 1048576 | tf_op jit(solution)/shard_map/all_to_all | solution.py:162
  25.3 0.9 %copy-start.2 = (s32[32768]{0:T(1024)S(1)}, s32[32768]{0:T(1024)}, u32[]{:S(2)}) copy-start(s32[32768]{0:T(1024)} %param.10) | copy-start | bytes 393220
  26.2 0.7 %copy-start.5 = (s32[1,8]{1,0:T(1,128)S(1)}, s32[1,8]{1,0:T(1,128)}, u32[]{:S(2)}) copy-start(s32[1,8]{1,0:T(1,128)} %flags_ref.1) | copy-start | bytes 100
  56.8 5.6 %collective-permute-start.1 = (bf16[4,32,256]{2,1,0:T(8,128)(2,1)S(1)}, bf16[4,32,256]{2,1,0:T(8,128)(2,1)S(1)}, u32[]{:S(2)}, u32[]{:S(2)}) collective-permute-start(bf16[4,32,256]{2,1,0:T(8,128)(2,1)S(1)} %get-tuple-element.12), channel_id=1, source_target_pairs={{32,0},{64,32},{96,64},{128,96},{160,128},{192,160},{224,192},{256... | collective-permute-start | bytes 196616 | tf_op jit(solution)/shard_map/ppermute | solution.py:206

commit v3 on v2

--- a/solution.py
+++ b/solution.py
@@ -11,46 +11,70 @@
 QPK = 8
 ROW = 8
 VMEM = pl.BlockSpec(memory_space=pltpu.VMEM)
+HBM = pl.BlockSpec(memory_space=pltpu.HBM)
 SMEM = pl.BlockSpec(memory_space=pltpu.SMEM)
 CONTRACT_LAST = (((1,), (1,)), ((), ()))
 
 
-def spread_kernel(place_ref, key_ref, value_ref, prev_ref, out_ref):
+def pack_kernel(
+    place_ref, key_ref, value_ref, docs_ref, flags_ref, mine_ref, rows_ref, flags_out_ref, sems
+):
+    z = place_ref[0]
+    width = key_ref.shape[1]
+    copies = [
+        pltpu.make_async_copy(key_ref, mine_ref.at[:, :width], sems.at[0]),
+        pltpu.make_async_copy(value_ref, mine_ref.at[:, width:], sems.at[1]),
+        pltpu.make_async_copy(flags_ref, flags_out_ref, sems.at[2]),
+    ]
+    for at, row in enumerate((z, jnp.maximum(z - 1, 0))):
+        source = docs_ref.at[pl.ds(pl.multiple_of(row * ROW, ROW), ROW), :]
+        copies.append(pltpu.make_async_copy(source, rows_ref.at[at], sems.at[3 + at]))
+    for copy in copies:
+        copy.start()
+    for copy in copies:
+        copy.wait()
+
+
+def spread_kernel(place_ref, mine_ref, prev_ref, out_ref):
     j = place_ref[1]
-    groups = key_ref.shape[1] // HD
-    for part, mine_ref in enumerate((key_ref, value_ref)):
+    groups = mine_ref.shape[1] // (2 * HD)
+    for part in range(2):
         for g in range(groups):
-            at = part * groups + g
-            mine = mine_ref[:, g * HD : (g + 1) * HD]
-            prev = prev_ref[:, at * HD : (at + 1) * HD]
+            cols = slice((part * groups + g) * HD, (part * groups + g + 1) * HD)
+            mine, prev = mine_ref[:, cols], prev_ref[:, cols]
             for jp in range(ROW):
                 out_ref[jp * groups + g, :, part * HD : (part + 1) * HD] = jnp.where(
                     j <= jp, mine, prev
                 )
 
 
-def mask_kernel(place_ref, flags_ref, docs_ref, cap_ref):
-    z, jp = place_ref[0], place_ref[1]
-    block = docs_ref.shape[1]
-    own_docs = docs_ref[pl.ds(pl.multiple_of(z * ROW, ROW), ROW), :]
-    prev_docs = docs_ref[pl.ds(pl.multiple_of(jnp.maximum(z - 1, 0) * ROW, ROW), ROW), :]
-    row_at = lax.broadcasted_iota(jnp.int32, own_docs.shape, 0)
-    query_docs = jnp.sum(jnp.where(row_at == jp, own_docs, 0), axis=0, keepdims=True)
-    query_docs = query_docs.astype(jnp.float32)
+def fill_cap(z, jp, rows_ref, flags_ref, cap):
+    block = cap.shape[1]
+    slot = lax.broadcasted_iota(jnp.int32, (ROW, block), 0)
+    lane = lax.broadcasted_iota(jnp.int32, (ROW, block), 1)
+    own_docs = rows_ref[0].astype(jnp.float32)
+    query_docs = jnp.sum(jnp.where(slot == jp, own_docs, 0.0), axis=0, keepdims=True)
+    docs = jnp.where(slot <= jp, own_docs, rows_ref[1].astype(jnp.float32))
+    offset = jnp.where(slot <= jp, jp - slot, jp - slot + ROW)
+    flags = jnp.concatenate([flags_ref[...]] * (block // ROW), axis=1)
+    flag = jnp.where(lane == offset, jnp.broadcast_to(flags, (ROW, block)), 0)
+    flag = jnp.max(flag, axis=1, keepdims=True)
+    active = (flag > 0) & (z * ROW + jp - offset >= 0)
+    docs = jnp.where(active, docs, -1.0)
+    columns = jnp.concatenate([docs] * (block // ROW), axis=0).T
     key_at = lax.broadcasted_iota(jnp.int32, (block, block), 0)
     query_at = lax.broadcasted_iota(jnp.int32, (block, block), 1)
+    ahead = key_at - query_at
     for j in range(ROW):
-        own = j <= jp
-        offset = jnp.where(own, jp - j, jp - j + ROW)
-        active = (flags_ref[0, offset] > 0) & (z * ROW + jp - offset >= 0)
-        docs = jnp.where(own, own_docs[j : j + 1], prev_docs[j : j + 1])
-        docs = jnp.where(active, docs, -1).astype(jnp.float32)
-        docs = jnp.broadcast_to(docs, (block, block)).T
-        allowed = (docs == query_docs) & (key_at <= query_at + offset * block)
-        cap_ref[j * block : (j + 1) * block, :] = jnp.where(allowed, 3e38, -1e30)
-
-
-def attention_kernel(cap_ref, q_ref, do_ref, kv_ref, dkv_ref, grads_ref, s_buf, dp_buf):
+        reach = jnp.where(j == jp, 0, block)
+        allowed = (columns[:, j : j + 1] == query_docs) & (ahead <= reach)
+        cap[j * block : (j + 1) * block, :] = jnp.where(allowed, 3e38, -1e30)
+
+
+def attention_kernel(
+    place_ref, rows_ref, flags_ref, q_ref, do_ref, kv_ref, dkv_ref, grads_ref, cap_ref, s_buf, dp_buf
+):
+    fill_cap(place_ref[0], place_ref[1], rows_ref, flags_ref, cap_ref)
     block = q_ref.shape[0]
     root = 1.0 / math.sqrt(HD)
     to_exp2 = root * math.log2(math.e)
@@ -115,18 +139,34 @@
         dq_ref[:, cols] = dq_t[:, h * block : (h + 1) * block].T.astype(jnp.bfloat16)
 
 
-def sums_kernel(place_ref, parts_ref, own_ref, prev_ref):
+def part_sum(parts_ref, g, keep):
+    groups = parts_ref.shape[0] // ROW
+    total = None
+    for j in range(ROW):
+        part = parts_ref[j * groups + g].astype(jnp.float32)
+        part = jnp.where(keep(j), part, 0.0)
+        total = part if total is None else total + part
+    return total
+
+
+def prev_sum_kernel(place_ref, parts_ref, prev_ref):
+    groups = prev_ref.shape[0]
+    count = jnp.where(place_ref[0] > 0, place_ref[1], 0)
+
+    def add(j, sums):
+        return tuple(
+            total + parts_ref[j * groups + g].astype(jnp.float32) for g, total in enumerate(sums)
+        )
+
+    zero = jnp.zeros(prev_ref.shape[1:], jnp.float32)
+    for g, total in enumerate(lax.fori_loop(0, count, add, (zero,) * groups)):
+        prev_ref[g] = total.astype(jnp.bfloat16)
+
+
+def own_sum_kernel(place_ref, parts_ref, own_ref):
     jp = place_ref[1]
-    groups = parts_ref.shape[0] // ROW
-    for g in range(groups):
-        own = jnp.zeros(own_ref.shape[1:], jnp.float32)
-        prev = jnp.zeros(own_ref.shape[1:], jnp.float32)
-        for j in range(ROW):
-            part = parts_ref[j * groups + g].astype(jnp.float32)
-            own += jnp.where(j >= jp, part, 0.0)
-            prev += jnp.where(j < jp, part, 0.0)
-        own_ref[g] = own
-        prev_ref[g] = prev.astype(jnp.bfloat16)
+    for g in range(own_ref.shape[0]):
+        own_ref[g] = part_sum(parts_ref, g, lambda j: j >= jp)
 
 
 def join_kernel(own_ref, next_ref, dkey_ref, dvalue_ref):
@@ -139,6 +179,10 @@
 
 def held(array):
     return pltpu.with_memory_space_constraint(array, pltpu.VMEM)
+
+
+def off_chip(array):
+    return pltpu.with_memory_space_constraint(array, pltpu.HBM)
 
 
 def shards(query, key, value, dout, doc_ids, pair_flags):
@@ -149,38 +193,53 @@
     slots = ROW * groups
     rows = lax.axis_size("z")
     place = jnp.stack([lax.axis_index("z"), lax.axis_index("j")]).astype(jnp.int32)
-    mine = jnp.concatenate([key, value], axis=1)
-    prev = lax.ppermute(mine, "z", [(i, i + 1) for i in range(rows - 1)])
+    mine, doc_rows, flags = pl.pallas_call(
+        pack_kernel,
+        out_shape=(
+            pltpu.VMEM((tokens, 2 * width), bf16),
+            pltpu.VMEM((2, ROW, block), jnp.int32),
+            pltpu.VMEM(pair_flags.shape, jnp.int32),
+        ),
+        in_specs=[SMEM, HBM, HBM, HBM, HBM],
+        out_specs=(VMEM, VMEM, VMEM),
+        scratch_shapes=[pltpu.SemaphoreType.DMA((5,))],
+        compiler_params=pltpu.CompilerParams(vmem_limit_bytes=4 << 20),
+        name="pack",
+    )(
+        place,
+        off_chip(key),
+        off_chip(value),
+        off_chip(doc_ids.reshape(-1, block)),
+        off_chip(pair_flags),
+    )
+    passed = [(z * ROW + j, (z + 1) * ROW + j) for z in range(rows - 1) for j in range(1, ROW)]
+    prev = lax.ppermute(mine, ("z", "j"), passed)
     sent = pl.pallas_call(
         spread_kernel,
         out_shape=pltpu.VMEM((slots, tokens, 2 * HD), bf16),
-        in_specs=[SMEM, VMEM, VMEM, VMEM],
+        in_specs=[SMEM, VMEM, VMEM],
         out_specs=VMEM,
         compiler_params=pltpu.CompilerParams(vmem_limit_bytes=4 << 20),
         name="spread",
-    )(place, held(key), held(value), held(prev))
+    )(place, held(mine), held(prev))
     taken = lax.all_to_all(sent, ("j", "head"), 0, 0, tiled=True)
     taken = taken.reshape(ROW * block, 2 * HD)
-    cap = pl.pallas_call(
-        mask_kernel,
-        out_shape=pltpu.VMEM((ROW * block, block), f32),
-        in_specs=[SMEM, SMEM, VMEM],
-        out_specs=VMEM,
-        compiler_params=pltpu.CompilerParams(vmem_limit_bytes=4 << 20),
-        name="mask",
-    )(place, pair_flags, doc_ids.reshape(-1, block))
     parts, grads = pl.pallas_call(
         attention_kernel,
         out_shape=(
             pltpu.VMEM((ROW * block, 2 * HD), bf16),
             pltpu.VMEM((ROW * block, QPK * block), bf16),
         ),
-        in_specs=[VMEM, VMEM, VMEM, VMEM],
+        in_specs=[SMEM, VMEM, VMEM, VMEM, VMEM, VMEM],
         out_specs=(VMEM, VMEM),
-        scratch_shapes=[pltpu.VMEM((2, ROW * block, 2 * block), f32)] * 2,
+        scratch_shapes=[
+            pltpu.VMEM((ROW * block, block), f32),
+            pltpu.VMEM((2, ROW * block, 2 * block), f32),
+            pltpu.VMEM((2, ROW * block, 2 * block), f32),
+        ],
         compiler_params=pltpu.CompilerParams(vmem_limit_bytes=32 << 20),
         name="attention",
-    )(held(cap), held(query), held(dout), held(taken))
+    )(place, held(doc_rows), held(flags), held(query), held(dout), held(taken))
     back = lax.all_to_all(
         parts.reshape(slots, tokens, 2 * HD), ("j", "head"), 0, 0, tiled=True
     )
@@ -192,18 +251,23 @@
         compiler_params=pltpu.CompilerParams(vmem_limit_bytes=8 << 20),
         name="dquery",
     )(held(taken), held(grads))
-    own, to_prev = pl.pallas_call(
-        sums_kernel,
-        out_shape=(
-            pltpu.VMEM((groups, tokens, 2 * HD), f32),
-            pltpu.VMEM((groups, tokens, 2 * HD), bf16),
-        ),
+    to_prev = pl.pallas_call(
+        prev_sum_kernel,
+        out_shape=pltpu.VMEM((groups, tokens, 2 * HD), bf16),
         in_specs=[SMEM, VMEM],
-        out_specs=(VMEM, VMEM),
-        compiler_params=pltpu.CompilerParams(vmem_limit_bytes=4 << 20),
-        name="sums",
+        out_specs=VMEM,
+        compiler_params=pltpu.CompilerParams(vmem_limit_bytes=4 << 20),
+        name="prev_sum",
     )(place, held(back))
-    from_next = lax.ppermute(to_prev, "z", [(i, i - 1) for i in range(1, rows)])
+    from_next = lax.ppermute(to_prev, ("z", "j"), [(b, a) for a, b in passed])
+    own = pl.pallas_call(
+        own_sum_kernel,
+        out_shape=pltpu.VMEM((groups, tokens, 2 * HD), f32),
+        in_specs=[SMEM, VMEM],
+        out_specs=VMEM,
+        compiler_params=pltpu.CompilerParams(vmem_limit_bytes=4 << 20),
+        name="own_sum",
+    )(place, held(back))
     dkey, dvalue = pl.pallas_call(
         join_kernel,
         out_shape=(

time: 63.9 us -> 57.9 us (0.906)
  blocking collectives: 15.3 us -> 38.3 us
  starting transfers between devices: 20.8 us -> 5.65 us
  waiting for transfers between devices: 13.2 us -> 3.12 us
  local copies, waits for them, and re-layouts: 3.08 us -> 0.01 us
  other arithmetic: 0.91 us -> 0.08 us
  Pallas kernels: 9.07 us -> 9.77 us
    all_to_all x0 -> x1, blocking collectives: none -> 23 us  [shards(): taken = lax.all_to_all(sent, ('j', 'head'), 0, 0, tiled=True)]
    all_to_all x1 -> x0, starting transfers between devices: 15.2 us -> none  [shards(): taken = lax.all_to_all(sent, ('j', 'head'), 0, 0, tiled=True)]
    all_to_all x1 -> x0, waiting for transfers between devices: 8.86 us -> none  [shards(): taken = lax.all_to_all(sent, ('j', 'head'), 0, 0, tiled=True)]
    unnamed x12 -> x4, local copies, waits for them, and re-layouts: 3.08 us -> 0.01 us
    ppermute x2, waiting for transfers between devices: 4.32 us -> 3.12 us  [the longest x1 1.81 us: shards(): from_next = lax.ppermute(to_prev, ('z', 'j'), [(b, a) for a, b in passed])]
    pallas_call x2 -> x3, Pallas kernels: 1.5 us -> 2.56 us  [the longest x1 1.36 us: shards(): pl.pallas_call(pack_kernel, out_shape=(pltpu.VMEM((tokens, 2 * width), bf...]
    concatenate x1 -> x0, other arithmetic: 0.84 us -> none  [shards(): mine = jnp.concatenate([key, value], axis=1)]
    pallas_call x1, Pallas kernels: 1.42 us -> 0.61 us  [shards(): pl.pallas_call(spread_kernel, out_shape=pltpu.VMEM((slots, tokens, 2 * HD...]
  transfers between devices with their start and end apart: 3 -> 2, of which waited for: 3 -> 2; matrix products, arithmetic and copies ran while one was open for 0% -> 0% of each run, Pallas kernels for 3% -> 3%
where the time goes in v3:
time: 57.9 us; the launch traced here: 57.7 us
  blocking collectives  38.3 us (66%)
  Pallas kernels  9.77 us (17%)
  starting transfers between devices  5.65 us (10%)
  waiting for transfers between devices  3.12 us (5%)
  between operations  0.71 us (1%)
    all_to_all x1, blocking collectives, shards(): taken = lax.all_to_all(sent, ('j', 'head'), 0, 0, tiled=True)  23 us
    all_to_all x1, blocking collectives, shards(): lax.all_to_all(parts.reshape(slots, tokens, 2 * HD), ('j', 'head'), 0, 0,...  15.4 us
    pallas_call x1, Pallas kernels, shards(): pl.pallas_call(attention_kernel, out_shape=(pltpu.VMEM((ROW * block, 2 *...  4.71 us
    ppermute x1, starting transfers between devices, shards(): prev = lax.ppermute(mine, ('z', 'j'), passed)  4.36 us
    ppermute x1, waiting for transfers between devices, shards(): from_next = lax.ppermute(to_prev, ('z', 'j'), [(b, a) for a, b in passed])  1.81 us
    pallas_call x1, Pallas kernels, shards(): pl.pallas_call(pack_kernel, out_shape=(pltpu.VMEM((tokens, 2 * width), bf...  1.36 us
    ppermute x1, waiting for transfers between devices, shards(): prev = lax.ppermute(mine, ('z', 'j'), passed)  1.31 us
    ppermute x1, starting transfers between devices, shards(): from_next = lax.ppermute(to_prev, ('z', 'j'), [(b, a) for a, b in passed])  1.29 us
  transfers between devices with their start and end apart: 2, of which 2 were waited for; matrix products, arithmetic and copies ran while one was open for 0% of the time, Pallas kernels for 3%

profile of v3, /device:TPU:1, one launch (start us, length us, event | category | flops | bytes accessed | tf_op | source)
XLA Modules:
  0.0 57.7 jit_solution(2350385208114961730)
XLA Ops:
  0.6 0.0 copy-start.1
  0.6 0.0 copy-start
  0.7 0.1 pad_add_fusion.place_ref
  0.7 1.4 %pack.1 = (bf16[32,1024]{1,0:T(8,128)(2,1)S(1)}, s32[2,8,128]{2,1,0:T(8,128)S(1)}, s32[1,8]{1,0:T(1,128)S(1)}) custom-call(s32[2]{0:T(128)S(1)} %pad_add_fusion.place_ref, bf16[32,512]{1,0:T(8,128)(2,1)} %key_ref.1, bf16[32,512]{1,0:T(8,128)(2,1)} %value_ref.1, s32[256,128]{1,0:T(8,128)} %bitcast.8, s32[1,8]{1,0:T(1,128)} %flags_ref.1), custom_call_target="tpu_custom_call" | custom-call | tf_op jit(solution)/shard_map/pack/pallas_call | solution.py:196
  2.1 4.4 %collective-permute-start = (bf16[32,1024]{1,0:T(8,128)(2,1)S(1)}, bf16[32,1024]{1,0:T(8,128)(2,1)S(1)}, u32[]{:S(2)}, u32[]{:S(2)}) collective-permute-start(bf16[32,1024]{1,0:T(8,128)(2,1)S(1)} %get-tuple-element.10.mine_ref), channel_id=1, source_target_pairs={{4,36},{8,40},{12,44},{16,48},{20,52},{24,56},{28,60},{36,68},{40,... | collective-permute-start | bytes 196616 | tf_op jit(solution)/shard_map/ppermute | solution.py:216
  6.5 1.3 %collective-permute-done.prev_ref = bf16[32,1024]{1,0:T(8,128)(2,1)S(1)} collective-permute-done((bf16[32,1024]{1,0:T(8,128)(2,1)S(1)}, bf16[32,1024]{1,0:T(8,128)(2,1)S(1)}, u32[]{:S(2)}, u32[]{:S(2)}) %collective-permute-start) | collective-permute-done | bytes 65568 | tf_op jit(solution)/shard_map/ppermute | solution.py:216
  7.8 0.6 %spread.1 = bf16[32,32,256]{2,1,0:T(8,128)(2,1)S(1)} custom-call(s32[2]{0:T(128)S(1)} %pad_add_fusion.place_ref, bf16[32,1024]{1,0:T(8,128)(2,1)S(1)} %get-tuple-element.10.mine_ref, bf16[32,1024]{1,0:T(8,128)(2,1)S(1)} %collective-permute-done.prev_ref), custom_call_target="tpu_custom_call" | custom-call | tf_op jit(solution)/shard_map/spread/pallas_call | solution.py:217
  8.4 23.0 %all_to_all.10 = bf16[32,32,256]{2,1,0:T(8,128)(2,1)S(1)} all-to-all(bf16[32,32,256]{2,1,0:T(8,128)(2,1)S(1)} %spread.1), channel_id=1, replica_groups=mesh['z'=32,'j'=8,'head'=4] {'j','head'}, dimensions={0} | all-to-all | bytes 1048576 | tf_op jit(solution)/shard_map/all_to_all | solution.py:225
  31.4 0.0 copy-done.1
  31.4 0.0 copy-done
  31.4 4.7 %attention.1 = (bf16[1024,256]{1,0:T(8,128)(2,1)S(1)}, bf16[1024,1024]{1,0:T(8,128)(2,1)S(1)}) custom-call(s32[2]{0:T(128)S(1)} %pad_add_fusion.place_ref, s32[2,8,128]{2,1,0:T(8,128)S(1)} %get-tuple-element.11.rows_ref, s32[1,8]{1,0:T(1,128)S(1)} %get-tuple-element.12.flags_ref, bf16[128,1024]{1,0:T(8,128)(2,1)S(1)} %copy-done, ...), custom_call_target="tpu_custom_call" | custom-call | tf_op jit(solution)/shard_map/attention/pallas_call | solution.py:227
  36.1 15.4 %all_to_all.11.parts_ref = bf16[32,32,256]{2,1,0:T(8,128)(2,1)S(1)} all-to-all(bf16[32,32,256]{2,1,0:T(8,128)(2,1)S(1)} %bitcast.7), channel_id=1, replica_groups=mesh['z'=32,'j'=8,'head'=4] {'j','head'}, dimensions={0} | all-to-all | bytes 1048576 | tf_op jit(solution)/shard_map/all_to_all | solution.py:243
  51.4 0.6 prev_sum.1
  52.0 1.3 %collective-permute-start.1 = (bf16[4,32,256]{2,1,0:T(8,128)(2,1)S(1)}, bf16[4,32,256]{2,1,0:T(8,128)(2,1)S(1)}, u32[]{:S(2)}, u32[]{:S(2)}) collective-permute-start(bf16[4,32,256]{2,1,0:T(8,128)(2,1)S(1)} %prev_sum.1), channel_id=1, source_target_pairs={{36,4},{40,8},{44,12},{48,16},{52,20},{56,24},{60,28},{68,36},{72,... | collective-permute-start | bytes 196616 | tf_op jit(solution)/shard_map/ppermute | solution.py:262
  53.3 1.2 %dquery.1 = bf16[128,1024]{1,0:T(8,128)(2,1)} custom-call(bf16[1024,256]{1,0:T(8,128)(2,1)S(1)} %bitcast.6, bf16[1024,1024]{1,0:T(8,128)(2,1)S(1)} %get-tuple-element.13.grads_ref), custom_call_target="tpu_custom_call" | custom-call | tf_op jit(solution)/shard_map/dquery/pallas_call | solution.py:246
  54.6 0.6 %own_sum.1.own_ref = f32[4,32,256]{2,1,0:T(8,128)S(1)} custom-call(s32[2]{0:T(128)S(1)} %pad_add_fusion.place_ref, bf16[32,32,256]{2,1,0:T(8,128)(2,1)S(1)} %all_to_all.11.parts_ref), custom_call_target="tpu_custom_call" | custom-call | tf_op jit(solution)/shard_map/own_sum/pallas_call | solution.py:263
  55.2 1.8 %collective-permute-done.1.next_ref = bf16[4,32,256]{2,1,0:T(8,128)(2,1)S(1)} collective-permute-done((bf16[4,32,256]{2,1,0:T(8,128)(2,1)S(1)}, bf16[4,32,256]{2,1,0:T(8,128)(2,1)S(1)}, u32[]{:S(2)}, u32[]{:S(2)}) %collective-permute-start.1) | collective-permute-done | bytes 65568 | tf_op jit(solution)/shard_map/ppermute | solution.py:262
  57.0 0.6 %join.1 = (bf16[32,512]{1,0:T(8,128)(2,1)}, bf16[32,512]{1,0:T(8,128)(2,1)}) custom-call(f32[4,32,256]{2,1,0:T(8,128)S(1)} %own_sum.1.own_ref, bf16[4,32,256]{2,1,0:T(8,128)(2,1)S(1)} %collective-permute-done.1.next_ref), custom_call_target="tpu_custom_call" | custom-call | tf_op jit(solution)/shard_map/join/pallas_call | solution.py:271
Async XLA Ops:
  0.6 30.7 %copy-start.1 = (bf16[128,1024]{1,0:T(8,128)(2,1)S(1)}, bf16[128,1024]{1,0:T(8,128)(2,1)}, u32[]{:S(2)}) copy-start(bf16[128,1024]{1,0:T(8,128)(2,1)} %do_ref.1) | copy-start | bytes 786436
  0.6 30.7 %copy-start = (bf16[128,1024]{1,0:T(8,128)(2,1)S(1)}, bf16[128,1024]{1,0:T(8,128)(2,1)}, u32[]{:S(2)}) copy-start(bf16[128,1024]{1,0:T(8,128)(2,1)} %q_ref.1) | copy-start | bytes 786436
  2.1 5.7 %collective-permute-start = (bf16[32,1024]{1,0:T(8,128)(2,1)S(1)}, bf16[32,1024]{1,0:T(8,128)(2,1)S(1)}, u32[]{:S(2)}, u32[]{:S(2)}) collective-permute-start(bf16[32,1024]{1,0:T(8,128)(2,1)S(1)} %get-tuple-element.10.mine_ref), channel_id=1, source_target_pairs={{4,36},{8,40},{12,44},{16,48},{20,52},{24,56},{28,60},{36,68},{40,... | collective-permute-start | bytes 196616 | tf_op jit(solution)/shard_map/ppermute | solution.py:216
  52.0 5.0 %collective-permute-start.1 = (bf16[4,32,256]{2,1,0:T(8,128)(2,1)S(1)}, bf16[4,32,256]{2,1,0:T(8,128)(2,1)S(1)}, u32[]{:S(2)}, u32[]{:S(2)}) collective-permute-start(bf16[4,32,256]{2,1,0:T(8,128)(2,1)S(1)} %prev_sum.1), channel_id=1, source_target_pairs={{36,4},{40,8},{44,12},{48,16},{52,20},{56,24},{60,28},{68,36},{72,... | collective-permute-start | bytes 196616 | tf_op jit(solution)/shard_map/ppermute | solution.py:262

commit v4 on v3

v4 whole, which is shorter than its diff:
```python
import math

import jax
import jax.numpy as jnp
from jax import lax
from jax.experimental import pallas as pl
from jax.experimental.pallas import tpu as pltpu
from jax.sharding import Mesh, PartitionSpec as P

HD = 128
QPK = 8
ROW = 8
VMEM = pl.BlockSpec(memory_space=pltpu.VMEM)
HBM = pl.BlockSpec(memory_space=pltpu.HBM)
CHUNK = 512
CONTRACT_LAST = (((1,), (1,)), ((), ()))


def pack_kernel(key_ref, value_ref, mine_ref, sems):
    width = key_ref.shape[1]
    copies = [
        pltpu.make_async_copy(key_ref, mine_ref.at[:, :width], sems.at[0]),
        pltpu.make_async_copy(value_ref, mine_ref.at[:, width:], sems.at[1]),
    ]
    for copy in copies:
        copy.start()
    for copy in copies:
        copy.wait()


def spread_kernel(mine_ref, prev_ref, docs_ref, flags_ref, out_ref, rows_ref, flags_out_ref, sems):
    z, j = lax.axis_index("z"), lax.axis_index("j")
    copies = [pltpu.make_async_copy(flags_ref, flags_out_ref, sems.at[2])]
    for at, row in enumerate((z, jnp.maximum(z - 1, 0))):
        source = docs_ref.at[pl.ds(pl.multiple_of(row * ROW, ROW), ROW), :]
        copies.append(pltpu.make_async_copy(source, rows_ref.at[at], sems.at[at]))
    for copy in copies:
        copy.start()
    groups = mine_ref.shape[1] // (2 * HD)
    for part in range(2):
        for g in range(groups):
            cols = slice((part * groups + g) * HD, (part * groups + g + 1) * HD)
            mine, prev = mine_ref[:, cols], prev_ref[:, cols]
            for jp in range(ROW):
                out_ref[jp * groups + g, :, part * HD : (part + 1) * HD] = jnp.where(
                    j <= jp, mine, prev
                )
    for copy in copies:
        copy.wait()


def fill_cap(z, jp, rows_ref, flags_ref, cap):
    block = cap.shape[1]
    slot = lax.broadcasted_iota(jnp.int32, (ROW, block), 0)
    lane = lax.broadcasted_iota(jnp.int32, (ROW, block), 1)
    own_docs = rows_ref[0].astype(jnp.float32)
    query_docs = jnp.sum(jnp.where(slot == jp, own_docs, 0.0), axis=0, keepdims=True)
    docs = jnp.where(slot <= jp, own_docs, rows_ref[1].astype(jnp.float32))
    offset = jnp.where(slot <= jp, jp - slot, jp - slot + ROW)
    flags = jnp.concatenate([flags_ref[...]] * (block // ROW), axis=1)
    flag = jnp.where(lane == offset, jnp.broadcast_to(flags, (ROW, block)), 0)
    flag = jnp.max(flag, axis=1, keepdims=True)
    active = (flag > 0) & (z * ROW + jp - offset >= 0)
    docs = jnp.where(active, docs, -1.0)
    columns = jnp.concatenate([docs] * (block // ROW), axis=0).T
    key_at = lax.broadcasted_iota(jnp.int32, (block, block), 0)
    query_at = lax.broadcasted_iota(jnp.int32, (block, block), 1)
    ahead = key_at - query_at
    for j in range(ROW):
        reach = jnp.where(j == jp, 0, block)
        allowed = (columns[:, j : j + 1] == query_docs) & (ahead <= reach)
        cap[j * block : (j + 1) * block, :] = jnp.where(allowed, 3e38, -1e30)


def attention_kernel(
    rows_ref, flags_ref, q_ref, do_ref, kv_ref, dkv_ref, grads_ref,
    cap_ref, s_buf, dp_buf, p_buf, dk_ref, dv_ref,
):
    fill_cap(lax.axis_index("z"), lax.axis_index("j"), rows_ref, flags_ref, cap_ref)
    block = q_ref.shape[0]
    root = 1.0 / math.sqrt(HD)
    to_exp2 = root * math.log2(math.e)
    bf16, f32 = jnp.bfloat16, jnp.float32
    pairs = QPK // 2
    chunks = [slice(at, at + CHUNK) for at in range(0, kv_ref.shape[0], CHUNK)]

    def of_pair(ref, pair):
        at = 2 * pair * HD
        return jnp.concatenate([ref[:, at : at + HD], ref[:, at + HD : at + 2 * HD]], axis=0)

    def fold(array, op):
        return op(array.reshape(-1, 8, 2 * block), axis=0)

    queries = [of_pair(q_ref, pair) for pair in range(pairs)]
    douts = [of_pair(do_ref, pair) for pair in range(pairs)]

    def products(pair, rows, top):
        s = lax.dot_general(kv_ref[rows, :HD], queries[pair], CONTRACT_LAST, preferred_element_type=f32)
        c = cap_ref[rows, :]
        s = jnp.minimum(s, jnp.concatenate([c, c], axis=1))
        s_buf[pair % 2, rows, :] = s
        dp_buf[pair % 2, rows, :] = lax.dot_general(
            kv_ref[rows, HD:], douts[pair], CONTRACT_LAST, preferred_element_type=f32
        )
        s = fold(s, jnp.max)
        return s if top is None else jnp.maximum(top, s)

    def sums(pair, rows):
        probs = p_buf[pair % 2, rows, :]
        grads = grads_ref[rows, 2 * pair * block : 2 * (pair + 1) * block]
        dv = jnp.dot(probs, douts[pair], preferred_element_type=f32)
        dk = jnp.dot(grads, queries[pair], preferred_element_type=f32)
        if pair > 0:
            dv, dk = dv + dv_ref[rows, :], dk + dk_ref[rows, :]
        if pair < pairs - 1:
            dv_ref[rows, :], dk_ref[rows, :] = dv, dk
        else:
            dkv_ref[rows, :HD] = (dk * root).astype(bf16)
            dkv_ref[rows, HD:] = dv.astype(bf16)

    top = None
    for rows in chunks:
        top = products(0, rows, top)
    for pair in range(pairs):
        top_now = jnp.max(top, axis=0, keepdims=True)
        total = jnp.zeros((8, 2 * block), f32)
        dot = jnp.zeros((8, 2 * block), f32)
        top = None
        for rows in chunks:
            if pair + 1 < pairs:
                top = products(pair + 1, rows, top)
            e = jnp.exp2((s_buf[pair % 2, rows, :] - top_now) * to_exp2)
            s_buf[pair % 2, rows, :] = e
            total += fold(e, jnp.sum)
            dot += fold(e * dp_buf[pair % 2, rows, :], jnp.sum)
        inverse = 1.0 / jnp.sum(total, axis=0, keepdims=True)
        row_dot = jnp.sum(dot, axis=0, keepdims=True) * inverse
        for rows in chunks:
            if pair > 0:
                sums(pair - 1, rows)
            p = s_buf[pair % 2, rows, :] * inverse
            p_buf[pair % 2, rows, :] = p.astype(bf16)
            grads = p * (dp_buf[pair % 2, rows, :] - row_dot)
            grads_ref[rows, 2 * pair * block : 2 * (pair + 1) * block] = grads.astype(bf16)
    for rows in chunks:
        sums(pairs - 1, rows)


def dquery_kernel(kv_ref, grads_ref, dq_ref):
    block = dq_ref.shape[0]
    keys_t = kv_ref[:, :HD].T
    dq_t = jnp.dot(keys_t, grads_ref[...], preferred_element_type=jnp.float32)
    dq_t = dq_t * (1.0 / math.sqrt(HD))
    for h in range(QPK):
        cols = slice(h * HD, (h + 1) * HD)
        dq_ref[:, cols] = dq_t[:, h * block : (h + 1) * block].T.astype(jnp.bfloat16)


def part_sum(parts_ref, g, keep):
    groups = parts_ref.shape[0] // ROW
    total = None
    for j in range(ROW):
        part = parts_ref[j * groups + g].astype(jnp.float32)
        part = jnp.where(keep(j), part, 0.0)
        total = part if total is None else total + part
    return total


def prev_sum_kernel(parts_ref, prev_ref):
    groups = prev_ref.shape[0]
    count = jnp.where(lax.axis_index("z") > 0, lax.axis_index("j"), 0)

    def add(j, sums):
        return tuple(
            total + parts_ref[j * groups + g].astype(jnp.float32) for g, total in enumerate(sums)
        )

    zero = jnp.zeros(prev_ref.shape[1:], jnp.float32)
    for g, total in enumerate(lax.fori_loop(0, count, add, (zero,) * groups)):
        prev_ref[g] = total.astype(jnp.bfloat16)


def own_sum_kernel(parts_ref, own_ref):
    jp = lax.axis_index("j")
    for g in range(own_ref.shape[0]):
        own_ref[g] = part_sum(parts_ref, g, lambda j: j >= jp)


def join_kernel(own_ref, next_ref, dkey_ref, dvalue_ref):
    for g in range(own_ref.shape[0]):
        cols = slice(g * HD, (g + 1) * HD)
        both = own_ref[g] + next_ref[g].astype(jnp.float32)
        dkey_ref[:, cols] = both[:, :HD].astype(jnp.bfloat16)
        dvalue_ref[:, cols] = both[:, HD:].astype(jnp.bfloat16)


def held(array):
    return pltpu.with_memory_space_constraint(array, pltpu.VMEM)


def off_chip(array):
    return pltpu.with_memory_space_constraint(array, pltpu.HBM)


def shards(query, key, value, dout, doc_ids, pair_flags):
    bf16, f32 = jnp.bfloat16, jnp.float32
    tokens, width = key.shape
    groups = width // HD
    block = query.shape[0]
    slots = ROW * groups
    rows = lax.axis_size("z")
    mine = pl.pallas_call(
        pack_kernel,
        out_shape=pltpu.VMEM((tokens, 2 * width), bf16),
        in_specs=[HBM, HBM],
        out_specs=VMEM,
        scratch_shapes=[pltpu.SemaphoreType.DMA((2,))],
        compiler_params=pltpu.CompilerParams(vmem_limit_bytes=4 << 20),
        name="pack",
    )(off_chip(key), off_chip(value))
    passed = [(z * ROW + j, (z + 1) * ROW + j) for z in range(rows - 1) for j in range(1, ROW)]
    prev = lax.ppermute(mine, ("z", "j"), passed)
    sent, doc_rows, flags = pl.pallas_call(
        spread_kernel,
        out_shape=(
            pltpu.VMEM((slots, tokens, 2 * HD), bf16),
            pltpu.VMEM((2, ROW, block), jnp.int32),
            pltpu.VMEM(pair_flags.shape, jnp.int32),
        ),
        in_specs=[VMEM, VMEM, HBM, HBM],
        out_specs=(VMEM, VMEM, VMEM),
        scratch_shapes=[pltpu.SemaphoreType.DMA((3,))],
        compiler_params=pltpu.CompilerParams(vmem_limit_bytes=4 << 20),
        name="spread",
    )(held(mine), held(prev), off_chip(doc_ids.reshape(-1, block)), off_chip(pair_flags))
    taken = lax.all_to_all(sent, ("j", "head"), 0, 0, tiled=True)
    taken = taken.reshape(ROW * block, 2 * HD)
    parts, grads = pl.pallas_call(
        attention_kernel,
        out_shape=(
            pltpu.VMEM((ROW * block, 2 * HD), bf16),
            pltpu.VMEM((ROW * block, QPK * block), bf16),
        ),
        in_specs=[VMEM, VMEM, VMEM, VMEM, VMEM],
        out_specs=(VMEM, VMEM),
        scratch_shapes=[
            pltpu.VMEM((ROW * block, block), f32),
            pltpu.VMEM((2, ROW * block, 2 * block), f32),
            pltpu.VMEM((2, ROW * block, 2 * block), f32),
            pltpu.VMEM((2, ROW * block, 2 * block), bf16),
            pltpu.VMEM((ROW * block, HD), f32),
            pltpu.VMEM((ROW * block, HD), f32),
        ],
        compiler_params=pltpu.CompilerParams(vmem_limit_bytes=32 << 20),
        name="attention",
    )(held(doc_rows), held(flags), held(query), held(dout), held(taken))
    back = lax.all_to_all(
        parts.reshape(slots, tokens, 2 * HD), ("j", "head"), 0, 0, tiled=True
    )
    dquery = pl.pallas_call(
        dquery_kernel,
        out_shape=jax.ShapeDtypeStruct(query.shape, bf16),
        in_specs=[VMEM, VMEM],
        out_specs=VMEM,
        compiler_params=pltpu.CompilerParams(vmem_limit_bytes=8 << 20),
        name="dquery",
    )(held(taken), held(grads))
    to_prev = pl.pallas_call(
        prev_sum_kernel,
        out_shape=pltpu.VMEM((groups, tokens, 2 * HD), bf16),
        in_specs=[VMEM],
        out_specs=VMEM,
        compiler_params=pltpu.CompilerParams(vmem_limit_bytes=4 << 20),
        name="prev_sum",
    )(held(back))
    from_next = lax.ppermute(to_prev, ("z", "j"), [(b, a) for a, b in passed])
    own = pl.pallas_call(
        own_sum_kernel,
        out_shape=pltpu.VMEM((groups, tokens, 2 * HD), f32),
        in_specs=[VMEM],
        out_specs=VMEM,
        compiler_params=pltpu.CompilerParams(vmem_limit_bytes=4 << 20),
        name="own_sum",
    )(held(back))
    dkey, dvalue = pl.pallas_call(
        join_kernel,
        out_shape=(
            jax.ShapeDtypeStruct(key.shape, bf16),
            jax.ShapeDtypeStruct(value.shape, bf16),
        ),
        in_specs=[VMEM, VMEM],
        out_specs=(VMEM, VMEM),
        compiler_params=pltpu.CompilerParams(vmem_limit_bytes=4 << 20),
        name="join",
    )(held(own), held(from_next))
    return (dquery, dkey, dvalue)


def solution(mesh):
    ctx, head = mesh.shape["ctx"], mesh.shape["head"]
    fine = Mesh(mesh.devices.reshape(ctx // ROW, ROW, head), ("z", "j", "head"))
    by_token = P(("z", "j", "head"), None)
    in_specs = (
        P(("z", "j"), "head"),
        by_token,
        by_token,
        P(("z", "j"), "head"),
        P(),
        P(("z", "j"), None),
    )
    out_specs = (P(("z", "j"), "head"), by_token, by_token)
    return jax.shard_map(shards, mesh=fine, in_specs=in_specs, out_specs=out_specs, check_vma=False)
```

time: 57.9 us -> 57.7 us (level)
  Pallas kernels: 9.77 us -> 7.13 us
  local copies, waits for them, and re-layouts: 0.01 us -> 1.9 us
    unnamed x4, local copies, waits for them, and re-layouts: 0.01 us -> 1.9 us
    pallas_call x1, Pallas kernels: 4.71 us -> 3.54 us  [shards(): pl.pallas_call(attention_kernel, out_shape=(pltpu.VMEM((ROW * block, 2 *...]
  transfers between devices with their start and end apart: 2 -> 2, of which waited for: 2 -> 2; matrix products, arithmetic and copies ran while one was open for 0% -> 0% of each run, Pallas kernels for 3% -> 2%
where the time goes in v4:
time: 57.7 us; the launch traced here: 57.4 us
  blocking collectives  38.3 us (66%)
  Pallas kernels  7.13 us (12%)
  starting transfers between devices  5.65 us (10%)
  waiting for transfers between devices  3.68 us (6%)
  local copies, waits for them, and re-layouts  1.9 us (3%)
  between operations  0.68 us (1%)
    all_to_all x1, blocking collectives, shards(): taken = lax.all_to_all(sent, ('j', 'head'), 0, 0, tiled=True)  23 us
    all_to_all x1, blocking collectives, shards(): lax.all_to_all(parts.reshape(slots, tokens, 2 * HD), ('j', 'head'), 0, 0,...  15.4 us
    ppermute x1, starting transfers between devices, shards(): prev = lax.ppermute(mine, ('z', 'j'), passed)  4.36 us
    pallas_call x1, Pallas kernels, shards(): pl.pallas_call(attention_kernel, out_shape=(pltpu.VMEM((ROW * block, 2 *...  3.54 us
    ppermute x1, waiting for transfers between devices, shards(): from_next = lax.ppermute(to_prev, ('z', 'j'), [(b, a) for a, b in passed])  2.35 us
    unnamed x4, local copies, waits for them, and re-layouts  1.9 us
    ppermute x1, waiting for transfers between devices, shards(): prev = lax.ppermute(mine, ('z', 'j'), passed)  1.33 us
    ppermute x1, starting transfers between devices, shards(): from_next = lax.ppermute(to_prev, ('z', 'j'), [(b, a) for a, b in passed])  1.29 us
  transfers between devices with their start and end apart: 2, of which 2 were waited for; matrix products, arithmetic and copies ran while one was open for 0% of the time, Pallas kernels for 2%

profile of v4, /device:TPU:1, one launch (start us, length us, event | category | flops | bytes accessed | tf_op | source)
XLA Modules:
  0.0 57.4 jit_solution(366484554667832053)
XLA Ops:
  0.6 0.8 %pack.1.mine_ref = bf16[32,1024]{1,0:T(8,128)(2,1)S(1)} custom-call(bf16[32,512]{1,0:T(8,128)(2,1)} %key_ref.1, bf16[32,512]{1,0:T(8,128)(2,1)} %value_ref.1), custom_call_target="tpu_custom_call" | custom-call | tf_op jit(solution)/shard_map/pack/pallas_call | solution.py:212
  1.4 4.4 %collective-permute-start = (bf16[32,1024]{1,0:T(8,128)(2,1)S(1)}, bf16[32,1024]{1,0:T(8,128)(2,1)S(1)}, u32[]{:S(2)}, u32[]{:S(2)}) collective-permute-start(bf16[32,1024]{1,0:T(8,128)(2,1)S(1)} %pack.1.mine_ref), channel_id=1, source_target_pairs={{4,36},{8,40},{12,44},{16,48},{20,52},{24,56},{28,60},{36,68},{40,... | collective-permute-start | bytes 196616 | tf_op jit(solution)/shard_map/ppermute | solution.py:222
  5.8 1.3 %collective-permute-done.prev_ref = bf16[32,1024]{1,0:T(8,128)(2,1)S(1)} collective-permute-done((bf16[32,1024]{1,0:T(8,128)(2,1)S(1)}, bf16[32,1024]{1,0:T(8,128)(2,1)S(1)}, u32[]{:S(2)}, u32[]{:S(2)}) %collective-permute-start) | collective-permute-done | bytes 65568 | tf_op jit(solution)/shard_map/ppermute | solution.py:222
  7.1 0.8 %spread.1 = (bf16[32,32,256]{2,1,0:T(8,128)(2,1)S(1)}, s32[2,8,128]{2,1,0:T(8,128)S(1)}, s32[1,8]{1,0:T(1,128)S(1)}) custom-call(bf16[32,1024]{1,0:T(8,128)(2,1)S(1)} %pack.1.mine_ref, bf16[32,1024]{1,0:T(8,128)(2,1)S(1)} %collective-permute-done.prev_ref, s32[256,128]{1,0:T(8,128)} %bitcast.6, s32[1,8]{1,0:T(1,128)} %flags_ref.1), custom_call_target="tpu_custom_call" | custom-call | tf_op jit(solution)/shard_map/spread/pallas_call | solution.py:223
  7.9 23.0 %all_to_all.10 = bf16[32,32,256]{2,1,0:T(8,128)(2,1)S(1)} all-to-all(bf16[32,32,256]{2,1,0:T(8,128)(2,1)S(1)} %get-tuple-element.10), channel_id=1, replica_groups=mesh['z'=32,'j'=8,'head'=4] {'j','head'}, dimensions={0} | all-to-all | bytes 1048576 | tf_op jit(solution)/shard_map/all_to_all | solution.py:236
  30.9 0.0 copy-start
  30.9 0.9 %copy-done = bf16[128,1024]{1,0:T(8,128)(2,1)S(1)} copy-done((bf16[128,1024]{1,0:T(8,128)(2,1)S(1)}, bf16[128,1024]{1,0:T(8,128)(2,1)}, u32[]{:S(2)}) %copy-start) | copy-done | bytes 262168
  31.8 0.0 copy-start.1
  31.8 0.9 %copy-done.1 = bf16[128,1024]{1,0:T(8,128)(2,1)S(1)} copy-done((bf16[128,1024]{1,0:T(8,128)(2,1)S(1)}, bf16[128,1024]{1,0:T(8,128)(2,1)}, u32[]{:S(2)}) %copy-start.1) | copy-done | bytes 262168
  32.8 3.5 %attention.1 = (bf16[1024,256]{1,0:T(8,128)(2,1)S(1)}, bf16[1024,1024]{1,0:T(8,128)(2,1)S(1)}) custom-call(s32[2,8,128]{2,1,0:T(8,128)S(1)} %get-tuple-element.11.rows_ref, s32[1,8]{1,0:T(1,128)S(1)} %get-tuple-element.12.flags_ref, bf16[128,1024]{1,0:T(8,128)(2,1)S(1)} %copy-done, bf16[128,1024]{1,0:T(8,128)(2,1)S(1)} %copy-done.1, ...), custom_call_target="tpu_custom_call" | custom-call | tf_op jit(solution)/shard_map/attention/pallas_call | solution.py:238
  36.3 15.4 %all_to_all.11.parts_ref = bf16[32,32,256]{2,1,0:T(8,128)(2,1)S(1)} all-to-all(bf16[32,32,256]{2,1,0:T(8,128)(2,1)S(1)} %bitcast.5), channel_id=1, replica_groups=mesh['z'=32,'j'=8,'head'=4] {'j','head'}, dimensions={0} | all-to-all | bytes 1048576 | tf_op jit(solution)/shard_map/all_to_all | solution.py:257
  51.7 1.3 %collective-permute-start.1 = (bf16[4,32,256]{2,1,0:T(8,128)(2,1)S(1)}, bf16[4,32,256]{2,1,0:T(8,128)(2,1)S(1)}, u32[]{:S(2)}, u32[]{:S(2)}) collective-permute-start(bf16[4,32,256]{2,1,0:T(8,128)(2,1)S(1)} %prev_sum.1), channel_id=1, source_target_pairs={{36,4},{40,8},{44,12},{48,16},{52,20},{56,24},{60,28},{68,36},{72,... | collective-permute-start | bytes 196616 | tf_op jit(solution)/shard_map/ppermute | solution.py:276
  53.0 1.2 %dquery.1 = bf16[128,1024]{1,0:T(8,128)(2,1)} custom-call(bf16[1024,256]{1,0:T(8,128)(2,1)S(1)} %bitcast.4, bf16[1024,1024]{1,0:T(8,128)(2,1)S(1)} %get-tuple-element.13.grads_ref), custom_call_target="tpu_custom_call" | custom-call | tf_op jit(solution)/shard_map/dquery/pallas_call | solution.py:260
  54.3 0.1 own_sum.1.own_ref
  54.4 2.4 %collective-permute-done.1.next_ref = bf16[4,32,256]{2,1,0:T(8,128)(2,1)S(1)} collective-permute-done((bf16[4,32,256]{2,1,0:T(8,128)(2,1)S(1)}, bf16[4,32,256]{2,1,0:T(8,128)(2,1)S(1)}, u32[]{:S(2)}, u32[]{:S(2)}) %collective-permute-start.1) | collective-permute-done | bytes 65568 | tf_op jit(solution)/shard_map/ppermute | solution.py:276
  56.7 0.6 %join.1 = (bf16[32,512]{1,0:T(8,128)(2,1)}, bf16[32,512]{1,0:T(8,128)(2,1)}) custom-call(f32[4,32,256]{2,1,0:T(8,128)S(1)} %own_sum.1.own_ref, bf16[4,32,256]{2,1,0:T(8,128)(2,1)S(1)} %collective-permute-done.1.next_ref), custom_call_target="tpu_custom_call" | custom-call | tf_op jit(solution)/shard_map/join/pallas_call | solution.py:285
  (1 shorter events, 0.0 us)
Async XLA Ops:
  1.4 5.7 %collective-permute-start = (bf16[32,1024]{1,0:T(8,128)(2,1)S(1)}, bf16[32,1024]{1,0:T(8,128)(2,1)S(1)}, u32[]{:S(2)}, u32[]{:S(2)}) collective-permute-start(bf16[32,1024]{1,0:T(8,128)(2,1)S(1)} %pack.1.mine_ref), channel_id=1, source_target_pairs={{4,36},{8,40},{12,44},{16,48},{20,52},{24,56},{28,60},{36,68},{40,... | collective-permute-start | bytes 196616 | tf_op jit(solution)/shard_map/ppermute | solution.py:222
  30.9 1.0 %copy-start = (bf16[128,1024]{1,0:T(8,128)(2,1)S(1)}, bf16[128,1024]{1,0:T(8,128)(2,1)}, u32[]{:S(2)}) copy-start(bf16[128,1024]{1,0:T(8,128)(2,1)} %q_ref.1) | copy-start | bytes 786436
  31.8 0.9 %copy-start.1 = (bf16[128,1024]{1,0:T(8,128)(2,1)S(1)}, bf16[128,1024]{1,0:T(8,128)(2,1)}, u32[]{:S(2)}) copy-start(bf16[128,1024]{1,0:T(8,128)(2,1)} %do_ref.1) | copy-start | bytes 786436
  51.7 5.0 %collective-permute-start.1 = (bf16[4,32,256]{2,1,0:T(8,128)(2,1)S(1)}, bf16[4,32,256]{2,1,0:T(8,128)(2,1)S(1)}, u32[]{:S(2)}, u32[]{:S(2)}) collective-permute-start(bf16[4,32,256]{2,1,0:T(8,128)(2,1)S(1)} %prev_sum.1), channel_id=1, source_target_pairs={{36,4},{40,8},{44,12},{48,16},{52,20},{56,24},{60,28},{68,36},{72,... | collective-permute-start | bytes 196616 | tf_op jit(solution)/shard_map/ppermute | solution.py:276

commit v5 on v4

--- a/solution.py
+++ b/solution.py
@@ -16,26 +16,30 @@
 CONTRACT_LAST = (((1,), (1,)), ((), ()))
 
 
-def pack_kernel(key_ref, value_ref, mine_ref, sems):
+def pack_kernel(
+    key_ref, value_ref, docs_ref, flags_ref, q_ref, do_ref,
+    mine_ref, rows_ref, flags_out_ref, q_out_ref, do_out_ref, sems,
+):
+    z = lax.axis_index("z")
     width = key_ref.shape[1]
-    copies = [
-        pltpu.make_async_copy(key_ref, mine_ref.at[:, :width], sems.at[0]),
-        pltpu.make_async_copy(value_ref, mine_ref.at[:, width:], sems.at[1]),
+    moves = [
+        (key_ref, mine_ref.at[:, :width]),
+        (value_ref, mine_ref.at[:, width:]),
+        (flags_ref, flags_out_ref),
+        (q_ref, q_out_ref),
+        (do_ref, do_out_ref),
     ]
+    for at, row in enumerate((z, jnp.maximum(z - 1, 0))):
+        moves.append((docs_ref.at[pl.ds(pl.multiple_of(row * ROW, ROW), ROW), :], rows_ref.at[at]))
+    copies = [pltpu.make_async_copy(a, b, sems.at[i]) for i, (a, b) in enumerate(moves)]
     for copy in copies:
         copy.start()
     for copy in copies:
         copy.wait()
 
 
-def spread_kernel(mine_ref, prev_ref, docs_ref, flags_ref, out_ref, rows_ref, flags_out_ref, sems):
-    z, j = lax.axis_index("z"), lax.axis_index("j")
-    copies = [pltpu.make_async_copy(flags_ref, flags_out_ref, sems.at[2])]
-    for at, row in enumerate((z, jnp.maximum(z - 1, 0))):
-        source = docs_ref.at[pl.ds(pl.multiple_of(row * ROW, ROW), ROW), :]
-        copies.append(pltpu.make_async_copy(source, rows_ref.at[at], sems.at[at]))
-    for copy in copies:
-        copy.start()
+def spread_kernel(mine_ref, prev_ref, out_ref):
+    j = lax.axis_index("j")
     groups = mine_ref.shape[1] // (2 * HD)
     for part in range(2):
         for g in range(groups):
@@ -45,8 +49,6 @@
                 out_ref[jp * groups + g, :, part * HD : (part + 1) * HD] = jnp.where(
                     j <= jp, mine, prev
                 )
-    for copy in copies:
-        copy.wait()
 
 
 def fill_cap(z, jp, rows_ref, flags_ref, cap):
@@ -209,30 +211,31 @@
     block = query.shape[0]
     slots = ROW * groups
     rows = lax.axis_size("z")
-    mine = pl.pallas_call(
+    mine, doc_rows, flags, query, dout = pl.pallas_call(
         pack_kernel,
-        out_shape=pltpu.VMEM((tokens, 2 * width), bf16),
-        in_specs=[HBM, HBM],
-        out_specs=VMEM,
-        scratch_shapes=[pltpu.SemaphoreType.DMA((2,))],
+        out_shape=(
+            pltpu.VMEM((tokens, 2 * width), bf16),
+            pltpu.VMEM((2, ROW, block), jnp.int32),
+            pltpu.VMEM(pair_flags.shape, jnp.int32),
+            pltpu.VMEM(query.shape, bf16),
+            pltpu.VMEM(dout.shape, bf16),
+        ),
+        in_specs=[HBM] * 6,
+        out_specs=(VMEM,) * 5,
+        scratch_shapes=[pltpu.SemaphoreType.DMA((7,))],
         compiler_params=pltpu.CompilerParams(vmem_limit_bytes=4 << 20),
         name="pack",
-    )(off_chip(key), off_chip(value))
+    )(*map(off_chip, (key, value, doc_ids.reshape(-1, block), pair_flags, query, dout)))
     passed = [(z * ROW + j, (z + 1) * ROW + j) for z in range(rows - 1) for j in range(1, ROW)]
     prev = lax.ppermute(mine, ("z", "j"), passed)
-    sent, doc_rows, flags = pl.pallas_call(
+    sent = pl.pallas_call(
         spread_kernel,
-        out_shape=(
-            pltpu.VMEM((slots, tokens, 2 * HD), bf16),
-            pltpu.VMEM((2, ROW, block), jnp.int32),
-            pltpu.VMEM(pair_flags.shape, jnp.int32),
-        ),
-        in_specs=[VMEM, VMEM, HBM, HBM],
-        out_specs=(VMEM, VMEM, VMEM),
-        scratch_shapes=[pltpu.SemaphoreType.DMA((3,))],
+        out_shape=pltpu.VMEM((slots, tokens, 2 * HD), bf16),
+        in_specs=[VMEM, VMEM],
+        out_specs=VMEM,
         compiler_params=pltpu.CompilerParams(vmem_limit_bytes=4 << 20),
         name="spread",
-    )(held(mine), held(prev), off_chip(doc_ids.reshape(-1, block)), off_chip(pair_flags))
+    )(held(mine), held(prev))
     taken = lax.all_to_all(sent, ("j", "head"), 0, 0, tiled=True)
     taken = taken.reshape(ROW * block, 2 * HD)
     parts, grads = pl.pallas_call(

time: 57.7 us -> 55.3 us (0.958)
  local copies, waits for them, and re-layouts: 1.9 us -> 0 us
    unnamed x4 -> x0, local copies, waits for them, and re-layouts: 1.9 us -> none
where the time goes in v5:
time: 55.3 us; the launch traced here: 55.1 us
  blocking collectives  38.3 us (69%)
  Pallas kernels  6.77 us (12%)
  starting transfers between devices  5.65 us (10%)
  waiting for transfers between devices  3.66 us (7%)
  between operations  0.67 us (1%)
    all_to_all x1, blocking collectives, shards(): taken = lax.all_to_all(sent, ('j', 'head'), 0, 0, tiled=True)  23 us
    all_to_all x1, blocking collectives, shards(): lax.all_to_all(parts.reshape(slots, tokens, 2 * HD), ('j', 'head'), 0, 0,...  15.4 us
    ppermute x1, starting transfers between devices, shards(): prev = lax.ppermute(mine, ('z', 'j'), passed)  4.36 us
    pallas_call x1, Pallas kernels, shards(): pl.pallas_call(attention_kernel, out_shape=(pltpu.VMEM((ROW * block, 2 *...  3.54 us
    ppermute x1, waiting for transfers between devices, shards(): from_next = lax.ppermute(to_prev, ('z', 'j'), [(b, a) for a, b in passed])  2.35 us
    ppermute x1, waiting for transfers between devices, shards(): prev = lax.ppermute(mine, ('z', 'j'), passed)  1.31 us
    ppermute x1, starting transfers between devices, shards(): from_next = lax.ppermute(to_prev, ('z', 'j'), [(b, a) for a, b in passed])  1.29 us
    pallas_call x1, Pallas kernels, shards(): pl.pallas_call(dquery_kernel, out_shape=jax.ShapeDtypeStruct(query.shape,...  1.25 us
  transfers between devices with their start and end apart: 2, of which 2 were waited for; matrix products, arithmetic and copies ran while one was open for 0% of the time, Pallas kernels for 2%

profile of v5, /device:TPU:1, one launch (start us, length us, event | category | flops | bytes accessed | tf_op | source)
XLA Modules:
  0.0 55.1 jit_solution(12936711613512756440)
XLA Ops:
  0.6 1.2 %pack.1 = (bf16[32,1024]{1,0:T(8,128)(2,1)S(1)}, s32[2,8,128]{2,1,0:T(8,128)S(1)}, s32[1,8]{1,0:T(1,128)S(1)}, bf16[128,1024]{1,0:T(8,128)(2,1)S(1)}, bf16[128,1024]{1,0:T(8,128)(2,1)S(1)}) custom-call(bf16[32,512]{1,0:T(8,128)(2,1)} %key_ref.1, bf16[32,512]{1,0:T(8,128)(2,1)} %value_ref.1, s32[256,128]{1,0:T(8,128)} %bitcast.6, s32[1,8]{1,0:T(1,128)} %flags_ref.1, ...), custom_call_target="tpu_custom_call" | custom-call | tf_op jit(solution)/shard_map/pack/pallas_call | solution.py:214
  1.8 4.4 %collective-permute-start = (bf16[32,1024]{1,0:T(8,128)(2,1)S(1)}, bf16[32,1024]{1,0:T(8,128)(2,1)S(1)}, u32[]{:S(2)}, u32[]{:S(2)}) collective-permute-start(bf16[32,1024]{1,0:T(8,128)(2,1)S(1)} %get-tuple-element.12.mine_ref), channel_id=1, source_target_pairs={{4,36},{8,40},{12,44},{16,48},{20,52},{24,56},{28,60},{36,68},{40,... | collective-permute-start | bytes 196616 | tf_op jit(solution)/shard_map/ppermute | solution.py:230
  6.2 1.3 %collective-permute-done.prev_ref = bf16[32,1024]{1,0:T(8,128)(2,1)S(1)} collective-permute-done((bf16[32,1024]{1,0:T(8,128)(2,1)S(1)}, bf16[32,1024]{1,0:T(8,128)(2,1)S(1)}, u32[]{:S(2)}, u32[]{:S(2)}) %collective-permute-start) | collective-permute-done | bytes 65568 | tf_op jit(solution)/shard_map/ppermute | solution.py:230
  7.5 0.1 spread.1
  7.6 23.0 %all_to_all.10 = bf16[32,32,256]{2,1,0:T(8,128)(2,1)S(1)} all-to-all(bf16[32,32,256]{2,1,0:T(8,128)(2,1)S(1)} %spread.1), channel_id=1, replica_groups=mesh['z'=32,'j'=8,'head'=4] {'j','head'}, dimensions={0} | all-to-all | bytes 1048576 | tf_op jit(solution)/shard_map/all_to_all | solution.py:239
  30.5 3.5 %attention.1 = (bf16[1024,256]{1,0:T(8,128)(2,1)S(1)}, bf16[1024,1024]{1,0:T(8,128)(2,1)S(1)}) custom-call(s32[2,8,128]{2,1,0:T(8,128)S(1)} %get-tuple-element.13.rows_ref, s32[1,8]{1,0:T(1,128)S(1)} %get-tuple-element.14.flags_ref, bf16[128,1024]{1,0:T(8,128)(2,1)S(1)} %get-tuple-element.15.q_ref, bf16[128,1024]{1,0:T(8,128)(2,1)S(1)} %get-tuple-element.16.do_ref, ...), custom_call_target="tpu_custom_call" | custom-call | tf_op jit(solution)/shard_map/attention/pallas_call | solution.py:241
  34.1 15.4 %all_to_all.11.parts_ref = bf16[32,32,256]{2,1,0:T(8,128)(2,1)S(1)} all-to-all(bf16[32,32,256]{2,1,0:T(8,128)(2,1)S(1)} %bitcast.5), channel_id=1, replica_groups=mesh['z'=32,'j'=8,'head'=4] {'j','head'}, dimensions={0} | all-to-all | bytes 1048576 | tf_op jit(solution)/shard_map/all_to_all | solution.py:260
  49.4 1.3 %collective-permute-start.1 = (bf16[4,32,256]{2,1,0:T(8,128)(2,1)S(1)}, bf16[4,32,256]{2,1,0:T(8,128)(2,1)S(1)}, u32[]{:S(2)}, u32[]{:S(2)}) collective-permute-start(bf16[4,32,256]{2,1,0:T(8,128)(2,1)S(1)} %prev_sum.1), channel_id=1, source_target_pairs={{36,4},{40,8},{44,12},{48,16},{52,20},{56,24},{60,28},{68,36},{72,... | collective-permute-start | bytes 196616 | tf_op jit(solution)/shard_map/ppermute | solution.py:279
  50.7 1.2 %dquery.1 = bf16[128,1024]{1,0:T(8,128)(2,1)} custom-call(bf16[1024,256]{1,0:T(8,128)(2,1)S(1)} %bitcast.4, bf16[1024,1024]{1,0:T(8,128)(2,1)S(1)} %get-tuple-element.17.grads_ref), custom_call_target="tpu_custom_call" | custom-call | tf_op jit(solution)/shard_map/dquery/pallas_call | solution.py:263
  52.0 0.1 own_sum.1.own_ref
  52.1 2.3 %collective-permute-done.1.next_ref = bf16[4,32,256]{2,1,0:T(8,128)(2,1)S(1)} collective-permute-done((bf16[4,32,256]{2,1,0:T(8,128)(2,1)S(1)}, bf16[4,32,256]{2,1,0:T(8,128)(2,1)S(1)}, u32[]{:S(2)}, u32[]{:S(2)}) %collective-permute-start.1) | collective-permute-done | bytes 65568 | tf_op jit(solution)/shard_map/ppermute | solution.py:279
  54.4 0.6 %join.1 = (bf16[32,512]{1,0:T(8,128)(2,1)}, bf16[32,512]{1,0:T(8,128)(2,1)}) custom-call(f32[4,32,256]{2,1,0:T(8,128)S(1)} %own_sum.1.own_ref, bf16[4,32,256]{2,1,0:T(8,128)(2,1)S(1)} %collective-permute-done.1.next_ref), custom_call_target="tpu_custom_call" | custom-call | tf_op jit(solution)/shard_map/join/pallas_call | solution.py:288
  (1 shorter events, 0.0 us)
Async XLA Ops:
  1.8 5.7 %collective-permute-start = (bf16[32,1024]{1,0:T(8,128)(2,1)S(1)}, bf16[32,1024]{1,0:T(8,128)(2,1)S(1)}, u32[]{:S(2)}, u32[]{:S(2)}) collective-permute-start(bf16[32,1024]{1,0:T(8,128)(2,1)S(1)} %get-tuple-element.12.mine_ref), channel_id=1, source_target_pairs={{4,36},{8,40},{12,44},{16,48},{20,52},{24,56},{28,60},{36,68},{40,... | collective-permute-start | bytes 196616 | tf_op jit(solution)/shard_map/ppermute | solution.py:230
  49.4 5.0 %collective-permute-start.1 = (bf16[4,32,256]{2,1,0:T(8,128)(2,1)S(1)}, bf16[4,32,256]{2,1,0:T(8,128)(2,1)S(1)}, u32[]{:S(2)}, u32[]{:S(2)}) collective-permute-start(bf16[4,32,256]{2,1,0:T(8,128)(2,1)S(1)} %prev_sum.1), channel_id=1, source_target_pairs={{36,4},{40,8},{44,12},{48,16},{52,20},{56,24},{60,28},{68,36},{72,... | collective-permute-start | bytes 196616 | tf_op jit(solution)/shard_map/ppermute | solution.py:279

commit v6 on v5

--- a/solution.py
+++ b/solution.py
@@ -17,8 +17,8 @@
 
 
 def pack_kernel(
-    key_ref, value_ref, docs_ref, flags_ref, q_ref, do_ref,
-    mine_ref, rows_ref, flags_out_ref, q_out_ref, do_out_ref, sems,
+    key_ref, value_ref, docs_ref, flags_ref, q_ref,
+    mine_ref, rows_ref, flags_out_ref, q_out_ref, sems,
 ):
     z = lax.axis_index("z")
     width = key_ref.shape[1]
@@ -27,7 +27,6 @@
         (value_ref, mine_ref.at[:, width:]),
         (flags_ref, flags_out_ref),
         (q_ref, q_out_ref),
-        (do_ref, do_out_ref),
     ]
     for at, row in enumerate((z, jnp.maximum(z - 1, 0))):
         moves.append((docs_ref.at[pl.ds(pl.multiple_of(row * ROW, ROW), ROW), :], rows_ref.at[at]))
@@ -75,10 +74,13 @@
 
 
 def attention_kernel(
-    rows_ref, flags_ref, q_ref, do_ref, kv_ref, dkv_ref, grads_ref,
-    cap_ref, s_buf, dp_buf, p_buf, dk_ref, dv_ref,
+    rows_ref, flags_ref, q_ref, do_hbm, kv_ref, dkv_ref, grads_ref,
+    cap_ref, s_buf, dp_buf, p_buf, dk_ref, dv_ref, do_ref, sem,
 ):
+    fetch = pltpu.make_async_copy(do_hbm, do_ref, sem)
+    fetch.start()
     fill_cap(lax.axis_index("z"), lax.axis_index("j"), rows_ref, flags_ref, cap_ref)
+    fetch.wait()
     block = q_ref.shape[0]
     root = 1.0 / math.sqrt(HD)
     to_exp2 = root * math.log2(math.e)
@@ -211,23 +213,24 @@
     block = query.shape[0]
     slots = ROW * groups
     rows = lax.axis_size("z")
-    mine, doc_rows, flags, query, dout = pl.pallas_call(
+    mine, doc_rows, flags, query = pl.pallas_call(
         pack_kernel,
         out_shape=(
             pltpu.VMEM((tokens, 2 * width), bf16),
             pltpu.VMEM((2, ROW, block), jnp.int32),
             pltpu.VMEM(pair_flags.shape, jnp.int32),
             pltpu.VMEM(query.shape, bf16),
-            pltpu.VMEM(dout.shape, bf16),
         ),
-        in_specs=[HBM] * 6,
-        out_specs=(VMEM,) * 5,
-        scratch_shapes=[pltpu.SemaphoreType.DMA((7,))],
+        in_specs=[HBM] * 5,
+        out_specs=(VMEM,) * 4,
+        scratch_shapes=[pltpu.SemaphoreType.DMA((6,))],
         compiler_params=pltpu.CompilerParams(vmem_limit_bytes=4 << 20),
         name="pack",
-    )(*map(off_chip, (key, value, doc_ids.reshape(-1, block), pair_flags, query, dout)))
+    )(*map(off_chip, (key, value, doc_ids.reshape(-1, block), pair_flags, query)))
     passed = [(z * ROW + j, (z + 1) * ROW + j) for z in range(rows - 1) for j in range(1, ROW)]
     prev = lax.ppermute(mine, ("z", "j"), passed)
+    first_row = (lax.axis_index("z") == 0).astype(jnp.int32)
+    prev, first_row = lax.optimization_barrier((prev, first_row))
     sent = pl.pallas_call(
         spread_kernel,
         out_shape=pltpu.VMEM((slots, tokens, 2 * HD), bf16),
@@ -237,6 +240,7 @@
         name="spread",
     )(held(mine), held(prev))
     taken = lax.all_to_all(sent, ("j", "head"), 0, 0, tiled=True)
+    taken, first_row = lax.optimization_barrier((taken, first_row))
     taken = taken.reshape(ROW * block, 2 * HD)
     parts, grads = pl.pallas_call(
         attention_kernel,
@@ -244,7 +248,7 @@
             pltpu.VMEM((ROW * block, 2 * HD), bf16),
             pltpu.VMEM((ROW * block, QPK * block), bf16),
         ),
-        in_specs=[VMEM, VMEM, VMEM, VMEM, VMEM],
+        in_specs=[VMEM, VMEM, VMEM, HBM, VMEM],
         out_specs=(VMEM, VMEM),
         scratch_shapes=[
             pltpu.VMEM((ROW * block, block), f32),
@@ -253,13 +257,15 @@
             pltpu.VMEM((2, ROW * block, 2 * block), bf16),
             pltpu.VMEM((ROW * block, HD), f32),
             pltpu.VMEM((ROW * block, HD), f32),
+            pltpu.VMEM(dout.shape, bf16),
+            pltpu.SemaphoreType.DMA(()),
         ],
         compiler_params=pltpu.CompilerParams(vmem_limit_bytes=32 << 20),
         name="attention",
-    )(held(doc_rows), held(flags), held(query), held(dout), held(taken))
-    back = lax.all_to_all(
-        parts.reshape(slots, tokens, 2 * HD), ("j", "head"), 0, 0, tiled=True
-    )
+    )(held(doc_rows), held(flags), held(query), off_chip(dout), held(taken))
+    exchange = lambda a: lax.all_to_all(a, ("j", "head"), 0, 0, tiled=True)
+    parts = parts.reshape(slots, tokens, 2 * HD)
+    back = lax.switch(first_row, (exchange, lambda a: a), parts)
     dquery = pl.pallas_call(
         dquery_kernel,
         out_shape=jax.ShapeDtypeStruct(query.shape, bf16),
@@ -276,7 +282,9 @@
         compiler_params=pltpu.CompilerParams(vmem_limit_bytes=4 << 20),
         name="prev_sum",
     )(held(back))
+    to_prev, back = lax.optimization_barrier((to_prev, back))
     from_next = lax.ppermute(to_prev, ("z", "j"), [(b, a) for a, b in passed])
+    back = lax.switch(first_row, (lambda b: b, exchange), back)
     own = pl.pallas_call(
         own_sum_kernel,
         out_shape=pltpu.VMEM((groups, tokens, 2 * HD), f32),

time: 55.3 us -> 55.2 us (level)
  the two profiles are of different devices: /device:TPU:1 before, /device:TPU:354 now
where the time goes in v6:
time: 55.2 us; the launch traced here: 54.9 us
  blocking collectives  33.2 us (60%)
  Pallas kernels  7.6 us (14%)
  starting transfers between devices  6.96 us (13%)
  waiting for transfers between devices  6.43 us (12%)
  between operations  0.68 us (1%)
    all_to_all x1, blocking collectives, shards(): taken = lax.all_to_all(sent, ('j', 'head'), 0, 0, tiled=True)  17.9 us
    all_to_all x1, blocking collectives, shards(): exchange = lambda a: lax.all_to_all(a, ('j', 'head'), 0, 0, tiled=True)  15.3 us
    ppermute x1, starting transfers between devices, shards(): prev = lax.ppermute(mine, ('z', 'j'), passed)  5.04 us
    ppermute x1, waiting for transfers between devices, shards(): from_next = lax.ppermute(to_prev, ('z', 'j'), [(b, a) for a, b in passed])  4.55 us
    pallas_call x1, Pallas kernels, shards(): pl.pallas_call(attention_kernel, out_shape=(pltpu.VMEM((ROW * block, 2 *...  4.42 us
    ppermute x1, starting transfers between devices, shards(): from_next = lax.ppermute(to_prev, ('z', 'j'), [(b, a) for a, b in passed])  1.92 us
    ppermute x1, waiting for transfers between devices, shards(): prev = lax.ppermute(mine, ('z', 'j'), passed)  1.88 us
    pallas_call x1, Pallas kernels, shards(): pl.pallas_call(dquery_kernel, out_shape=jax.ShapeDtypeStruct(query.shape,...  1.25 us
  transfers between devices with their start and end apart: 2, of which 2 were waited for; matrix products, arithmetic and copies ran while one was open for 0% of the time, Pallas kernels for 2%

profile of v6, /device:TPU:354, one launch (start us, length us, event | category | flops | bytes accessed | tf_op | source)
XLA Modules:
  0.0 54.9 jit_solution(16785648982326063314)
XLA Ops:
  0.6 1.1 %pack.1 = (bf16[32,1024]{1,0:T(8,128)(2,1)S(1)}, s32[2,8,128]{2,1,0:T(8,128)S(1)}, s32[1,8]{1,0:T(1,128)S(1)}, bf16[128,1024]{1,0:T(8,128)(2,1)S(1)}) custom-call(bf16[32,512]{1,0:T(8,128)(2,1)} %key_ref.1, bf16[32,512]{1,0:T(8,128)(2,1)} %value_ref.1, s32[256,128]{1,0:T(8,128)} %bitcast.7, s32[1,8]{1,0:T(1,128)} %flags_ref.1, bf16[128,1024]{1,0:T(8,128)(2,1)} %q_ref.1), custom_call_target="tpu_custom_call" | custom-call | tf_op jit(solution)/shard_map/pack/pallas_call | solution.py:216
  1.7 5.0 %collective-permute-start = (bf16[32,1024]{1,0:T(8,128)(2,1)S(1)}, bf16[32,1024]{1,0:T(8,128)(2,1)S(1)}, u32[]{:S(2)}, u32[]{:S(2)}) collective-permute-start(bf16[32,1024]{1,0:T(8,128)(2,1)S(1)} %get-tuple-element.27.mine_ref), channel_id=1, source_target_pairs={{4,36},{8,40},{12,44},{16,48},{20,52},{24,56},{28,60},{36,68},{40,... | collective-permute-start | bytes 196616 | tf_op jit(solution)/shard_map/ppermute | solution.py:231
  6.8 1.9 %collective-permute-done.prev_ref = bf16[32,1024]{1,0:T(8,128)(2,1)S(1)} collective-permute-done((bf16[32,1024]{1,0:T(8,128)(2,1)S(1)}, bf16[32,1024]{1,0:T(8,128)(2,1)S(1)}, u32[]{:S(2)}, u32[]{:S(2)}) %collective-permute-start) | collective-permute-done | bytes 65568 | tf_op jit(solution)/shard_map/ppermute | solution.py:231
  8.6 0.1 spread.1
  8.7 17.9 %all_to_all.15 = bf16[32,32,256]{2,1,0:T(8,128)(2,1)S(1)} all-to-all(bf16[32,32,256]{2,1,0:T(8,128)(2,1)S(1)} %spread.1), channel_id=1, replica_groups=mesh['z'=32,'j'=8,'head'=4] {'j','head'}, dimensions={0} | all-to-all | bytes 1048576 | tf_op jit(solution)/shard_map/all_to_all | solution.py:242
  26.6 4.4 %attention.1 = (bf16[1024,256]{1,0:T(8,128)(2,1)S(1)}, bf16[1024,1024]{1,0:T(8,128)(2,1)S(1)}) custom-call(s32[2,8,128]{2,1,0:T(8,128)S(1)} %get-tuple-element.31.rows_ref, s32[1,8]{1,0:T(1,128)S(1)} %get-tuple-element.32.flags_ref, bf16[128,1024]{1,0:T(8,128)(2,1)S(1)} %get-tuple-element.33.q_ref, bf16[128,1024]{1,0:T(8,128)(2,1)} %do_hbm.1, ...), custom_call_target="tpu_custom_call" | custom-call | tf_op jit(solution)/shard_map/attention/pallas_call | solution.py:245
  31.0 15.4 %conditional.2 = (bf16[32,32,256]{2,1,0:T(8,128)(2,1)S(1)}) conditional(s32[]{:T(128)} %clamp.4, bf16[32,32,256]{2,1,0:T(8,128)(2,1)S(1)} %bitcast.3, bf16[32,32,256]{2,1,0:T(8,128)(2,1)S(1)} %bitcast.4), branch_computations={%region_0.0_spmd, %region_1.0_spmd} | conditional | bytes 2097160 | solution.py:268
  31.0 15.3 %all_to_all.13 = bf16[32,32,256]{2,1,0:T(8,128)(2,1)S(1)} all-to-all(bf16[32,32,256]{2,1,0:T(8,128)(2,1)S(1)} %copy.13), channel_id=1, replica_groups=mesh['z'=32,'j'=8,'head'=4] {'j','head'}, dimensions={0} | all-to-all | bytes 1048576 | tf_op jit(solution)/shard_map/cond/branch_0_fun/all_to_all | solution.py:266
  46.4 1.9 %collective-permute-start.1 = (bf16[4,32,256]{2,1,0:T(8,128)(2,1)S(1)}, bf16[4,32,256]{2,1,0:T(8,128)(2,1)S(1)}, u32[]{:S(2)}, u32[]{:S(2)}) collective-permute-start(bf16[4,32,256]{2,1,0:T(8,128)(2,1)S(1)} %prev_sum.1), channel_id=1, source_target_pairs={{36,4},{40,8},{44,12},{48,16},{52,20},{56,24},{60,28},{68,36},{72,... | collective-permute-start | bytes 196616 | tf_op jit(solution)/shard_map/ppermute | solution.py:286
  48.4 1.2 %dquery.1 = bf16[128,1024]{1,0:T(8,128)(2,1)} custom-call(bf16[1024,256]{1,0:T(8,128)(2,1)S(1)} %bitcast.6, bf16[1024,1024]{1,0:T(8,128)(2,1)S(1)} %get-tuple-element.34.grads_ref), custom_call_target="tpu_custom_call" | custom-call | tf_op jit(solution)/shard_map/dquery/pallas_call | solution.py:269
  49.6 0.1 own_sum.1.own_ref
  49.7 4.6 %collective-permute-done.1.next_ref = bf16[4,32,256]{2,1,0:T(8,128)(2,1)S(1)} collective-permute-done((bf16[4,32,256]{2,1,0:T(8,128)(2,1)S(1)}, bf16[4,32,256]{2,1,0:T(8,128)(2,1)S(1)}, u32[]{:S(2)}, u32[]{:S(2)}) %collective-permute-start.1) | collective-permute-done | bytes 65568 | tf_op jit(solution)/shard_map/ppermute | solution.py:286
  54.3 0.6 %join.1 = (bf16[32,512]{1,0:T(8,128)(2,1)}, bf16[32,512]{1,0:T(8,128)(2,1)}) custom-call(f32[4,32,256]{2,1,0:T(8,128)S(1)} %own_sum.1.own_ref, bf16[4,32,256]{2,1,0:T(8,128)(2,1)S(1)} %collective-permute-done.1.next_ref), custom_call_target="tpu_custom_call" | custom-call | tf_op jit(solution)/shard_map/join/pallas_call | solution.py:296
  (3 shorter events, 0.1 us)
Async XLA Ops:
  1.7 6.9 %collective-permute-start = (bf16[32,1024]{1,0:T(8,128)(2,1)S(1)}, bf16[32,1024]{1,0:T(8,128)(2,1)S(1)}, u32[]{:S(2)}, u32[]{:S(2)}) collective-permute-start(bf16[32,1024]{1,0:T(8,128)(2,1)S(1)} %get-tuple-element.27.mine_ref), channel_id=1, source_target_pairs={{4,36},{8,40},{12,44},{16,48},{20,52},{24,56},{28,60},{36,68},{40,... | collective-permute-start | bytes 196616 | tf_op jit(solution)/shard_map/ppermute | solution.py:231
  46.4 7.8 %collective-permute-start.1 = (bf16[4,32,256]{2,1,0:T(8,128)(2,1)S(1)}, bf16[4,32,256]{2,1,0:T(8,128)(2,1)S(1)}, u32[]{:S(2)}, u32[]{:S(2)}) collective-permute-start(bf16[4,32,256]{2,1,0:T(8,128)(2,1)S(1)} %prev_sum.1), channel_id=1, source_target_pairs={{36,4},{40,8},{44,12},{48,16},{52,20},{56,24},{60,28},{68,36},{72,... | collective-permute-start | bytes 196616 | tf_op jit(solution)/shard_map/ppermute | solution.py:286

commit v7 on v6

--- a/solution.py
+++ b/solution.py
@@ -80,7 +80,6 @@
     fetch = pltpu.make_async_copy(do_hbm, do_ref, sem)
     fetch.start()
     fill_cap(lax.axis_index("z"), lax.axis_index("j"), rows_ref, flags_ref, cap_ref)
-    fetch.wait()
     block = q_ref.shape[0]
     root = 1.0 / math.sqrt(HD)
     to_exp2 = root * math.log2(math.e)
@@ -96,18 +95,20 @@
         return op(array.reshape(-1, 8, 2 * block), axis=0)
 
     queries = [of_pair(q_ref, pair) for pair in range(pairs)]
-    douts = [of_pair(do_ref, pair) for pair in range(pairs)]
-
-    def products(pair, rows, top):
+    douts = []
+
+    def scores(pair, rows, top):
         s = lax.dot_general(kv_ref[rows, :HD], queries[pair], CONTRACT_LAST, preferred_element_type=f32)
         c = cap_ref[rows, :]
         s = jnp.minimum(s, jnp.concatenate([c, c], axis=1))
         s_buf[pair % 2, rows, :] = s
+        s = fold(s, jnp.max)
+        return s if top is None else jnp.maximum(top, s)
+
+    def dout_products(pair, rows):
         dp_buf[pair % 2, rows, :] = lax.dot_general(
             kv_ref[rows, HD:], douts[pair], CONTRACT_LAST, preferred_element_type=f32
         )
-        s = fold(s, jnp.max)
-        return s if top is None else jnp.maximum(top, s)
 
     def sums(pair, rows):
         probs = p_buf[pair % 2, rows, :]
@@ -124,7 +125,11 @@
 
     top = None
     for rows in chunks:
-        top = products(0, rows, top)
+        top = scores(0, rows, top)
+    fetch.wait()
+    douts.extend(of_pair(do_ref, pair) for pair in range(pairs))
+    for rows in chunks:
+        dout_products(0, rows)
     for pair in range(pairs):
         top_now = jnp.max(top, axis=0, keepdims=True)
         total = jnp.zeros((8, 2 * block), f32)
@@ -132,7 +137,8 @@
         top = None
         for rows in chunks:
             if pair + 1 < pairs:
-                top = products(pair + 1, rows, top)
+                top = scores(pair + 1, rows, top)
+                dout_products(pair + 1, rows)
             e = jnp.exp2((s_buf[pair % 2, rows, :] - top_now) * to_exp2)
             s_buf[pair % 2, rows, :] = e
             total += fold(e, jnp.sum)

time: 55.2 us -> 55.1 us (level)
  the two profiles are of different devices: /device:TPU:354 before, /device:TPU:98 now
where the time goes in v7:
time: 55.1 us; the launch traced here: 54.9 us
  blocking collectives  33.2 us (60%)
  Pallas kernels  7.54 us (14%)
  starting transfers between devices  6.96 us (13%)
  waiting for transfers between devices  6.43 us (12%)
  between operations  0.68 us (1%)
    all_to_all x1, blocking collectives, shards(): taken = lax.all_to_all(sent, ('j', 'head'), 0, 0, tiled=True)  17.9 us
    all_to_all x1, blocking collectives, shards(): exchange = lambda a: lax.all_to_all(a, ('j', 'head'), 0, 0, tiled=True)  15.4 us
    ppermute x1, starting transfers between devices, shards(): prev = lax.ppermute(mine, ('z', 'j'), passed)  5.04 us
    ppermute x1, waiting for transfers between devices, shards(): from_next = lax.ppermute(to_prev, ('z', 'j'), [(b, a) for a, b in passed])  4.55 us
    pallas_call x1, Pallas kernels, shards(): pl.pallas_call(attention_kernel, out_shape=(pltpu.VMEM((ROW * block, 2 *...  4.35 us
    ppermute x1, starting transfers between devices, shards(): from_next = lax.ppermute(to_prev, ('z', 'j'), [(b, a) for a, b in passed])  1.92 us
    ppermute x1, waiting for transfers between devices, shards(): prev = lax.ppermute(mine, ('z', 'j'), passed)  1.88 us
    pallas_call x1, Pallas kernels, shards(): pl.pallas_call(dquery_kernel, out_shape=jax.ShapeDtypeStruct(query.shape,...  1.25 us
  transfers between devices with their start and end apart: 2, of which 2 were waited for; matrix products, arithmetic and copies ran while one was open for 0% of the time, Pallas kernels for 2%

profile of v7, /device:TPU:98, one launch (start us, length us, event | category | flops | bytes accessed | tf_op | source)
XLA Modules:
  0.0 54.9 jit_solution(8606005173308734297)
XLA Ops:
  0.6 1.1 %pack.1 = (bf16[32,1024]{1,0:T(8,128)(2,1)S(1)}, s32[2,8,128]{2,1,0:T(8,128)S(1)}, s32[1,8]{1,0:T(1,128)S(1)}, bf16[128,1024]{1,0:T(8,128)(2,1)S(1)}) custom-call(bf16[32,512]{1,0:T(8,128)(2,1)} %key_ref.1, bf16[32,512]{1,0:T(8,128)(2,1)} %value_ref.1, s32[256,128]{1,0:T(8,128)} %bitcast.7, s32[1,8]{1,0:T(1,128)} %flags_ref.1, bf16[128,1024]{1,0:T(8,128)(2,1)} %q_ref.1), custom_call_target="tpu_custom_call" | custom-call | tf_op jit(solution)/shard_map/pack/pallas_call | solution.py:222
  1.7 5.0 %collective-permute-start = (bf16[32,1024]{1,0:T(8,128)(2,1)S(1)}, bf16[32,1024]{1,0:T(8,128)(2,1)S(1)}, u32[]{:S(2)}, u32[]{:S(2)}) collective-permute-start(bf16[32,1024]{1,0:T(8,128)(2,1)S(1)} %get-tuple-element.27.mine_ref), channel_id=1, source_target_pairs={{4,36},{8,40},{12,44},{16,48},{20,52},{24,56},{28,60},{36,68},{40,... | collective-permute-start | bytes 196616 | tf_op jit(solution)/shard_map/ppermute | solution.py:237
  6.8 1.9 %collective-permute-done.prev_ref = bf16[32,1024]{1,0:T(8,128)(2,1)S(1)} collective-permute-done((bf16[32,1024]{1,0:T(8,128)(2,1)S(1)}, bf16[32,1024]{1,0:T(8,128)(2,1)S(1)}, u32[]{:S(2)}, u32[]{:S(2)}) %collective-permute-start) | collective-permute-done | bytes 65568 | tf_op jit(solution)/shard_map/ppermute | solution.py:237
  8.6 0.1 spread.1
  8.7 17.9 %all_to_all.15 = bf16[32,32,256]{2,1,0:T(8,128)(2,1)S(1)} all-to-all(bf16[32,32,256]{2,1,0:T(8,128)(2,1)S(1)} %spread.1), channel_id=1, replica_groups=mesh['z'=32,'j'=8,'head'=4] {'j','head'}, dimensions={0} | all-to-all | bytes 1048576 | tf_op jit(solution)/shard_map/all_to_all | solution.py:248
  26.6 4.4 %attention.1 = (bf16[1024,256]{1,0:T(8,128)(2,1)S(1)}, bf16[1024,1024]{1,0:T(8,128)(2,1)S(1)}) custom-call(s32[2,8,128]{2,1,0:T(8,128)S(1)} %get-tuple-element.31.rows_ref, s32[1,8]{1,0:T(1,128)S(1)} %get-tuple-element.32.flags_ref, bf16[128,1024]{1,0:T(8,128)(2,1)S(1)} %get-tuple-element.33.q_ref, bf16[128,1024]{1,0:T(8,128)(2,1)} %do_hbm.1, ...), custom_call_target="tpu_custom_call" | custom-call | tf_op jit(solution)/shard_map/attention/pallas_call | solution.py:251
  30.9 15.4 %conditional.2 = (bf16[32,32,256]{2,1,0:T(8,128)(2,1)S(1)}) conditional(s32[]{:T(128)} %clamp.4, bf16[32,32,256]{2,1,0:T(8,128)(2,1)S(1)} %bitcast.3, bf16[32,32,256]{2,1,0:T(8,128)(2,1)S(1)} %bitcast.4), branch_computations={%region_0.0_spmd, %region_1.0_spmd} | conditional | bytes 2097160 | solution.py:274
  31.0 15.4 %all_to_all.13 = bf16[32,32,256]{2,1,0:T(8,128)(2,1)S(1)} all-to-all(bf16[32,32,256]{2,1,0:T(8,128)(2,1)S(1)} %copy.13), channel_id=1, replica_groups=mesh['z'=32,'j'=8,'head'=4] {'j','head'}, dimensions={0} | all-to-all | bytes 1048576 | tf_op jit(solution)/shard_map/cond/branch_0_fun/all_to_all | solution.py:272
  46.4 1.9 %collective-permute-start.1 = (bf16[4,32,256]{2,1,0:T(8,128)(2,1)S(1)}, bf16[4,32,256]{2,1,0:T(8,128)(2,1)S(1)}, u32[]{:S(2)}, u32[]{:S(2)}) collective-permute-start(bf16[4,32,256]{2,1,0:T(8,128)(2,1)S(1)} %prev_sum.1), channel_id=1, source_target_pairs={{36,4},{40,8},{44,12},{48,16},{52,20},{56,24},{60,28},{68,36},{72,... | collective-permute-start | bytes 196616 | tf_op jit(solution)/shard_map/ppermute | solution.py:292
  48.3 1.2 %dquery.1 = bf16[128,1024]{1,0:T(8,128)(2,1)} custom-call(bf16[1024,256]{1,0:T(8,128)(2,1)S(1)} %bitcast.6, bf16[1024,1024]{1,0:T(8,128)(2,1)S(1)} %get-tuple-element.34.grads_ref), custom_call_target="tpu_custom_call" | custom-call | tf_op jit(solution)/shard_map/dquery/pallas_call | solution.py:275
  49.6 0.1 own_sum.1.own_ref
  49.7 4.6 %collective-permute-done.1.next_ref = bf16[4,32,256]{2,1,0:T(8,128)(2,1)S(1)} collective-permute-done((bf16[4,32,256]{2,1,0:T(8,128)(2,1)S(1)}, bf16[4,32,256]{2,1,0:T(8,128)(2,1)S(1)}, u32[]{:S(2)}, u32[]{:S(2)}) %collective-permute-start.1) | collective-permute-done | bytes 65568 | tf_op jit(solution)/shard_map/ppermute | solution.py:292
  54.2 0.6 %join.1 = (bf16[32,512]{1,0:T(8,128)(2,1)}, bf16[32,512]{1,0:T(8,128)(2,1)}) custom-call(f32[4,32,256]{2,1,0:T(8,128)S(1)} %own_sum.1.own_ref, bf16[4,32,256]{2,1,0:T(8,128)(2,1)S(1)} %collective-permute-done.1.next_ref), custom_call_target="tpu_custom_call" | custom-call | tf_op jit(solution)/shard_map/join/pallas_call | solution.py:302
  (3 shorter events, 0.1 us)
Async XLA Ops:
  1.7 6.9 %collective-permute-start = (bf16[32,1024]{1,0:T(8,128)(2,1)S(1)}, bf16[32,1024]{1,0:T(8,128)(2,1)S(1)}, u32[]{:S(2)}, u32[]{:S(2)}) collective-permute-start(bf16[32,1024]{1,0:T(8,128)(2,1)S(1)} %get-tuple-element.27.mine_ref), channel_id=1, source_target_pairs={{4,36},{8,40},{12,44},{16,48},{20,52},{24,56},{28,60},{36,68},{40,... | collective-permute-start | bytes 196616 | tf_op jit(solution)/shard_map/ppermute | solution.py:237
  46.4 7.8 %collective-permute-start.1 = (bf16[4,32,256]{2,1,0:T(8,128)(2,1)S(1)}, bf16[4,32,256]{2,1,0:T(8,128)(2,1)S(1)}, u32[]{:S(2)}, u32[]{:S(2)}) collective-permute-start(bf16[4,32,256]{2,1,0:T(8,128)(2,1)S(1)} %prev_sum.1), channel_id=1, source_target_pairs={{36,4},{40,8},{44,12},{48,16},{52,20},{56,24},{60,28},{68,36},{72,... | collective-permute-start | bytes 196616 | tf_op jit(solution)/shard_map/ppermute | solution.py:292

commit v8 on v5

--- a/solution.py
+++ b/solution.py
@@ -75,8 +75,8 @@
 
 
 def attention_kernel(
-    rows_ref, flags_ref, q_ref, do_ref, kv_ref, dkv_ref, grads_ref,
-    cap_ref, s_buf, dp_buf, p_buf, dk_ref, dv_ref,
+    rows_ref, flags_ref, q_ref, do_ref, kv_ref, dkv_ref, grads_ref, dq_last_ref,
+    cap_ref, s_buf, dp_buf, p_buf, dk_ref, dv_ref, last_ref,
 ):
     fill_cap(lax.axis_index("z"), lax.axis_index("j"), rows_ref, flags_ref, cap_ref)
     block = q_ref.shape[0]
@@ -107,9 +107,14 @@
         s = fold(s, jnp.max)
         return s if top is None else jnp.maximum(top, s)
 
+    def grads_of(pair, rows):
+        if pair == pairs - 1:
+            return last_ref.at[rows, :]
+        return grads_ref.at[rows, 2 * pair * block : 2 * (pair + 1) * block]
+
     def sums(pair, rows):
         probs = p_buf[pair % 2, rows, :]
-        grads = grads_ref[rows, 2 * pair * block : 2 * (pair + 1) * block]
+        grads = grads_of(pair, rows)[...]
         dv = jnp.dot(probs, douts[pair], preferred_element_type=f32)
         dk = jnp.dot(grads, queries[pair], preferred_element_type=f32)
         if pair > 0:
@@ -143,19 +148,24 @@
             p = s_buf[pair % 2, rows, :] * inverse
             p_buf[pair % 2, rows, :] = p.astype(bf16)
             grads = p * (dp_buf[pair % 2, rows, :] - row_dot)
-            grads_ref[rows, 2 * pair * block : 2 * (pair + 1) * block] = grads.astype(bf16)
+            grads_of(pair, rows)[...] = grads.astype(bf16)
     for rows in chunks:
         sums(pairs - 1, rows)
-
-
-def dquery_kernel(kv_ref, grads_ref, dq_ref):
+    dquery_of(kv_ref[:, :HD].T, last_ref[...], dq_last_ref)
+
+
+def dquery_of(keys_t, grads, dq_ref):
     block = dq_ref.shape[0]
-    keys_t = kv_ref[:, :HD].T
-    dq_t = jnp.dot(keys_t, grads_ref[...], preferred_element_type=jnp.float32)
-    dq_t = dq_t * (1.0 / math.sqrt(HD))
-    for h in range(QPK):
+    dq_t = jnp.dot(keys_t, grads, preferred_element_type=jnp.float32) * (1.0 / math.sqrt(HD))
+    for h in range(grads.shape[1] // block):
         cols = slice(h * HD, (h + 1) * HD)
         dq_ref[:, cols] = dq_t[:, h * block : (h + 1) * block].T.astype(jnp.bfloat16)
+
+
+def dquery_kernel(kv_ref, grads_ref, dq_last_ref, dq_ref):
+    split = dq_ref.shape[1] - dq_last_ref.shape[1]
+    dquery_of(kv_ref[:, :HD].T, grads_ref[...], dq_ref.at[:, :split])
+    dq_ref[:, split:] = dq_last_ref[...]
 
 
 def part_sum(parts_ref, g, keep):
@@ -228,6 +238,8 @@
     )(*map(off_chip, (key, value, doc_ids.reshape(-1, block), pair_flags, query, dout)))
     passed = [(z * ROW + j, (z + 1) * ROW + j) for z in range(rows - 1) for j in range(1, ROW)]
     prev = lax.ppermute(mine, ("z", "j"), passed)
+    first_row = (lax.axis_index("z") == 0).astype(jnp.int32)
+    prev, first_row = lax.optimization_barrier((prev, first_row))
     sent = pl.pallas_call(
         spread_kernel,
         out_shape=pltpu.VMEM((slots, tokens, 2 * HD), bf16),
@@ -237,15 +249,17 @@
         name="spread",
     )(held(mine), held(prev))
     taken = lax.all_to_all(sent, ("j", "head"), 0, 0, tiled=True)
+    taken, first_row = lax.optimization_barrier((taken, first_row))
     taken = taken.reshape(ROW * block, 2 * HD)
-    parts, grads = pl.pallas_call(
+    parts, grads, dq_last = pl.pallas_call(
         attention_kernel,
         out_shape=(
             pltpu.VMEM((ROW * block, 2 * HD), bf16),
-            pltpu.VMEM((ROW * block, QPK * block), bf16),
+            pltpu.VMEM((ROW * block, (QPK - 2) * block), bf16),
+            pltpu.VMEM((block, 2 * HD), bf16),
         ),
         in_specs=[VMEM, VMEM, VMEM, VMEM, VMEM],
-        out_specs=(VMEM, VMEM),
+        out_specs=(VMEM, VMEM, VMEM),
         scratch_shapes=[
             pltpu.VMEM((ROW * block, block), f32),
             pltpu.VMEM((2, ROW * block, 2 * block), f32),
@@ -253,21 +267,22 @@
             pltpu.VMEM((2, ROW * block, 2 * block), bf16),
             pltpu.VMEM((ROW * block, HD), f32),
             pltpu.VMEM((ROW * block, HD), f32),
+            pltpu.VMEM((ROW * block, 2 * block), bf16),
         ],
         compiler_params=pltpu.CompilerParams(vmem_limit_bytes=32 << 20),
         name="attention",
     )(held(doc_rows), held(flags), held(query), held(dout), held(taken))
-    back = lax.all_to_all(
-        parts.reshape(slots, tokens, 2 * HD), ("j", "head"), 0, 0, tiled=True
-    )
+    exchange = lambda a: lax.all_to_all(a, ("j", "head"), 0, 0, tiled=True)
+    parts = parts.reshape(slots, tokens, 2 * HD)
+    back = lax.switch(first_row, (exchange, lambda a: a), parts)
     dquery = pl.pallas_call(
         dquery_kernel,
         out_shape=jax.ShapeDtypeStruct(query.shape, bf16),
-        in_specs=[VMEM, VMEM],
+        in_specs=[VMEM, VMEM, VMEM],
         out_specs=VMEM,
         compiler_params=pltpu.CompilerParams(vmem_limit_bytes=8 << 20),
         name="dquery",
-    )(held(taken), held(grads))
+    )(held(taken), held(grads), held(dq_last))
     to_prev = pl.pallas_call(
         prev_sum_kernel,
         out_shape=pltpu.VMEM((groups, tokens, 2 * HD), bf16),
@@ -276,7 +291,9 @@
         compiler_params=pltpu.CompilerParams(vmem_limit_bytes=4 << 20),
         name="prev_sum",
     )(held(back))
+    to_prev, back = lax.optimization_barrier((to_prev, back))
     from_next = lax.ppermute(to_prev, ("z", "j"), [(b, a) for a, b in passed])
+    back = lax.switch(first_row, (lambda b: b, exchange), back)
     own = pl.pallas_call(
         own_sum_kernel,
         out_shape=pltpu.VMEM((groups, tokens, 2 * HD), f32),

time: 55.3 us -> 54.5 us (0.986)
  the two profiles are of different devices: /device:TPU:1 before, /device:TPU:482 now
where the time goes in v8:
time: 54.5 us; the launch traced here: 54.2 us
  blocking collectives  33.2 us (61%)
  starting transfers between devices  6.96 us (13%)
  Pallas kernels  6.86 us (13%)
  waiting for transfers between devices  6.46 us (12%)
  between operations  0.69 us (1%)
    all_to_all x1, blocking collectives, shards(): taken = lax.all_to_all(sent, ('j', 'head'), 0, 0, tiled=True)  17.9 us
    all_to_all x1, blocking collectives, shards(): exchange = lambda a: lax.all_to_all(a, ('j', 'head'), 0, 0, tiled=True)  15.3 us
    ppermute x1, starting transfers between devices, shards(): prev = lax.ppermute(mine, ('z', 'j'), passed)  5.04 us
    ppermute x1, waiting for transfers between devices, shards(): from_next = lax.ppermute(to_prev, ('z', 'j'), [(b, a) for a, b in passed])  4.58 us
    pallas_call x1, Pallas kernels, shards(): pl.pallas_call(attention_kernel, out_shape=(pltpu.VMEM((ROW * block, 2 *...  3.64 us
    ppermute x1, starting transfers between devices, shards(): from_next = lax.ppermute(to_prev, ('z', 'j'), [(b, a) for a, b in passed])  1.92 us
    ppermute x1, waiting for transfers between devices, shards(): prev = lax.ppermute(mine, ('z', 'j'), passed)  1.88 us
    pallas_call x1, Pallas kernels, shards(): pl.pallas_call(dquery_kernel, out_shape=jax.ShapeDtypeStruct(query.shape,...  1.19 us
  transfers between devices with their start and end apart: 2, of which 2 were waited for; matrix products, arithmetic and copies ran while one was open for 0% of the time, Pallas kernels for 2%

profile of v8, /device:TPU:482, one launch (start us, length us, event | category | flops | bytes accessed | tf_op | source)
XLA Modules:
  0.0 54.2 jit_solution(15076426969820915701)
XLA Ops:
  0.6 1.2 %pack.1 = (bf16[32,1024]{1,0:T(8,128)(2,1)S(1)}, s32[2,8,128]{2,1,0:T(8,128)S(1)}, s32[1,8]{1,0:T(1,128)S(1)}, bf16[128,1024]{1,0:T(8,128)(2,1)S(1)}, bf16[128,1024]{1,0:T(8,128)(2,1)S(1)}) custom-call(bf16[32,512]{1,0:T(8,128)(2,1)} %key_ref.1, bf16[32,512]{1,0:T(8,128)(2,1)} %value_ref.1, s32[256,128]{1,0:T(8,128)} %bitcast.7, s32[1,8]{1,0:T(1,128)} %flags_ref.1, ...), custom_call_target="tpu_custom_call" | custom-call | tf_op jit(solution)/shard_map/pack/pallas_call | solution.py:224
  1.8 5.0 %collective-permute-start = (bf16[32,1024]{1,0:T(8,128)(2,1)S(1)}, bf16[32,1024]{1,0:T(8,128)(2,1)S(1)}, u32[]{:S(2)}, u32[]{:S(2)}) collective-permute-start(bf16[32,1024]{1,0:T(8,128)(2,1)S(1)} %get-tuple-element.29.mine_ref), channel_id=1, source_target_pairs={{4,36},{8,40},{12,44},{16,48},{20,52},{24,56},{28,60},{36,68},{40,... | collective-permute-start | bytes 196616 | tf_op jit(solution)/shard_map/ppermute | solution.py:240
  6.8 1.9 %collective-permute-done.prev_ref = bf16[32,1024]{1,0:T(8,128)(2,1)S(1)} collective-permute-done((bf16[32,1024]{1,0:T(8,128)(2,1)S(1)}, bf16[32,1024]{1,0:T(8,128)(2,1)S(1)}, u32[]{:S(2)}, u32[]{:S(2)}) %collective-permute-start) | collective-permute-done | bytes 65568 | tf_op jit(solution)/shard_map/ppermute | solution.py:240
  8.7 0.1 spread.1
  8.8 17.9 %all_to_all.15 = bf16[32,32,256]{2,1,0:T(8,128)(2,1)S(1)} all-to-all(bf16[32,32,256]{2,1,0:T(8,128)(2,1)S(1)} %spread.1), channel_id=1, replica_groups=mesh['z'=32,'j'=8,'head'=4] {'j','head'}, dimensions={0} | all-to-all | bytes 1048576 | tf_op jit(solution)/shard_map/all_to_all | solution.py:251
  26.7 3.6 %attention.1 = (bf16[1024,256]{1,0:T(8,128)(2,1)S(1)}, bf16[1024,768]{1,0:T(8,128)(2,1)S(1)}, bf16[128,256]{1,0:T(8,128)(2,1)S(1)}) custom-call(s32[2,8,128]{2,1,0:T(8,128)S(1)} %get-tuple-element.33.rows_ref, s32[1,8]{1,0:T(1,128)S(1)} %get-tuple-element.34.flags_ref, bf16[128,1024]{1,0:T(8,128)(2,1)S(1)} %get-tuple-element.35.q_ref, ...), custom_call_target="tpu_custom_call" | custom-call | tf_op jit(solution)/shard_map/attention/pallas_call | solution.py:254
  30.3 15.4 %conditional.2 = (bf16[32,32,256]{2,1,0:T(8,128)(2,1)S(1)}) conditional(s32[]{:T(128)} %clamp.4, bf16[32,32,256]{2,1,0:T(8,128)(2,1)S(1)} %bitcast.3, bf16[32,32,256]{2,1,0:T(8,128)(2,1)S(1)} %bitcast.4), branch_computations={%region_0.0_spmd, %region_1.0_spmd} | conditional | bytes 2097160 | solution.py:277
  30.4 15.3 %all_to_all.13 = bf16[32,32,256]{2,1,0:T(8,128)(2,1)S(1)} all-to-all(bf16[32,32,256]{2,1,0:T(8,128)(2,1)S(1)} %copy.13), channel_id=1, replica_groups=mesh['z'=32,'j'=8,'head'=4] {'j','head'}, dimensions={0} | all-to-all | bytes 1048576 | tf_op jit(solution)/shard_map/cond/branch_0_fun/all_to_all | solution.py:275
  45.8 1.9 %collective-permute-start.1 = (bf16[4,32,256]{2,1,0:T(8,128)(2,1)S(1)}, bf16[4,32,256]{2,1,0:T(8,128)(2,1)S(1)}, u32[]{:S(2)}, u32[]{:S(2)}) collective-permute-start(bf16[4,32,256]{2,1,0:T(8,128)(2,1)S(1)} %prev_sum.1), channel_id=1, source_target_pairs={{36,4},{40,8},{44,12},{48,16},{52,20},{56,24},{60,28},{68,36},{72,... | collective-permute-start | bytes 196616 | tf_op jit(solution)/shard_map/ppermute | solution.py:295
  47.7 0.1 own_sum.1.own_ref
  47.8 1.2 %dquery.1 = bf16[128,1024]{1,0:T(8,128)(2,1)} custom-call(bf16[1024,256]{1,0:T(8,128)(2,1)S(1)} %bitcast.6, bf16[1024,768]{1,0:T(8,128)(2,1)S(1)} %get-tuple-element.37.grads_ref, bf16[128,256]{1,0:T(8,128)(2,1)S(1)} %get-tuple-element.38.dq_last_ref), custom_call_target="tpu_custom_call" | custom-call | tf_op jit(solution)/shard_map/dquery/pallas_call | solution.py:278
  49.0 4.6 %collective-permute-done.1.next_ref = bf16[4,32,256]{2,1,0:T(8,128)(2,1)S(1)} collective-permute-done((bf16[4,32,256]{2,1,0:T(8,128)(2,1)S(1)}, bf16[4,32,256]{2,1,0:T(8,128)(2,1)S(1)}, u32[]{:S(2)}, u32[]{:S(2)}) %collective-permute-start.1) | collective-permute-done | bytes 65568 | tf_op jit(solution)/shard_map/ppermute | solution.py:295
  53.6 0.6 %join.1 = (bf16[32,512]{1,0:T(8,128)(2,1)}, bf16[32,512]{1,0:T(8,128)(2,1)}) custom-call(f32[4,32,256]{2,1,0:T(8,128)S(1)} %own_sum.1.own_ref, bf16[4,32,256]{2,1,0:T(8,128)(2,1)S(1)} %collective-permute-done.1.next_ref), custom_call_target="tpu_custom_call" | custom-call | tf_op jit(solution)/shard_map/join/pallas_call | solution.py:305
  (3 shorter events, 0.1 us)
Async XLA Ops:
  1.8 6.9 %collective-permute-start = (bf16[32,1024]{1,0:T(8,128)(2,1)S(1)}, bf16[32,1024]{1,0:T(8,128)(2,1)S(1)}, u32[]{:S(2)}, u32[]{:S(2)}) collective-permute-start(bf16[32,1024]{1,0:T(8,128)(2,1)S(1)} %get-tuple-element.29.mine_ref), channel_id=1, source_target_pairs={{4,36},{8,40},{12,44},{16,48},{20,52},{24,56},{28,60},{36,68},{40,... | collective-permute-start | bytes 196616 | tf_op jit(solution)/shard_map/ppermute | solution.py:240
  45.8 7.8 %collective-permute-start.1 = (bf16[4,32,256]{2,1,0:T(8,128)(2,1)S(1)}, bf16[4,32,256]{2,1,0:T(8,128)(2,1)S(1)}, u32[]{:S(2)}, u32[]{:S(2)}) collective-permute-start(bf16[4,32,256]{2,1,0:T(8,128)(2,1)S(1)} %prev_sum.1), channel_id=1, source_target_pairs={{36,4},{40,8},{44,12},{48,16},{52,20},{56,24},{60,28},{68,36},{72,... | collective-permute-start | bytes 196616 | tf_op jit(solution)/shard_map/ppermute | solution.py:295
